TPU v7x, 32 devices: a whole 2x2x4 slice. The times are simulated.
32 devices in a mesh: grp: 1, ev: 32 (over z, y, x, core).
Axes of the slice: x: 2, y: 2, z: 4, core: 2. Of those that a mesh axis runs over, the one named last changes fastest.
Arguments:
- windows: bfloat16 [256, 3, 64, 1024], P(('grp', 'ev')), may hold values from -400 to 400, as said below
- rotation: bfloat16 [256, 3, 64], P(('grp', 'ev')), may hold values from -3 to 3
- source_inverse: bfloat16 [256, 1024], P(('grp', 'ev')), may hold values from -3.4 to 3.4
- send_rows: int32 [1024, 64], P(('grp', 'ev')), may hold values from 0 to 511, as said below
- tile_station: int32 [2048], P(('grp', 'ev')), may hold values from 0 to 63, as said below
- tile_count: int32 [2048], P(('grp', 'ev')), may hold values from 16 to 128
- pair_rows: int32 [2, 262144], P(None, ('grp', 'ev')), may hold values from 0 to 2047, as said below
Outputs:
- correlation: float32 [262144, 255], P(('grp', 'ev'))
Inputs may be any that keep to these rules, and one draw needn't show every extreme that they name: Each event's windows carry a scale of their own, and each station's another. `send_rows`: row j of the block of device o names the rows of device o sent to device j, each as local event times 64 plus station, with the station of the tile whose residue matches the receiving slot (o * 64 + k) mod 64. `tile_station`: tile t of a device is fed by received slots r with r mod 64 = t mod 64, all at the tile's station. `pair_rows`: entries count the rows a device receives by sending device then slot; both members of a slot lie at its tile's station.
All inputs are finite; a program needn't handle non-finite values.
Results may differ from a plain program's by a relative error of at most 0.007.
Values may be sent and summed in bfloat16 or wider, within the bound.
No kernel may reach another device: no remote copies, remote signals or barrier semaphores. Data moves between devices by JAX's collectives and lax.ppermute only.
A program may use at most 64 MiB of HBM per device.

v0:
```python
from functools import partial
import math

import jax
import jax.numpy as jnp
from jax import lax
from jax.sharding import PartitionSpec as P

LAGS = 255


epsilon = 1e-06


def spectral_table(length):
    half_len = length // 2
    samples = jnp.arange(length, dtype=jnp.int32)[:, None]
    frequency = jnp.arange(half_len, dtype=jnp.int32)[None, :]
    angles = (samples * frequency % length).astype(jnp.float32) * (2.0 * math.pi / length)
    factor = 1.0 / math.sqrt(length)
    return jnp.concatenate([jnp.cos(angles) * factor, -jnp.sin(angles) * factor], axis=1).astype(
        jnp.bfloat16
    )


def lag_table(length, lag_count):
    half_len = length // 2
    frequency = jnp.arange(half_len, dtype=jnp.int32)[:, None]
    shifts = jnp.arange(lag_count, dtype=jnp.int32)[None, :] - lag_count // 2
    angles = (frequency * shifts % length).astype(jnp.float32) * (2.0 * math.pi / length)
    factor = 1.0 / math.sqrt(half_len)
    return jnp.concatenate([jnp.cos(angles) * factor, -jnp.sin(angles) * factor], axis=0).astype(
        jnp.bfloat16
    )


def event_spectra(windows, rotation, source_inverse, dft_table):
    half_len = dft_table.shape[1] // 2
    transverse = jnp.sum(
        rotation.astype(jnp.float32)[..., None] * windows.astype(jnp.float32), axis=1
    ).astype(jnp.bfloat16)
    events, stations, length = transverse.shape
    spectrum = jnp.dot(
        transverse.reshape(events * stations, length), dft_table, preferred_element_type=jnp.float32
    )
    spectrum = spectrum.reshape(events, stations, length)
    filter_gain = source_inverse.astype(jnp.float32)[:, None, :]
    real_in, imag_in = (spectrum[..., :half_len], spectrum[..., half_len:])
    real_gain, imag_gain = (filter_gain[..., :half_len], filter_gain[..., half_len:])
    return jnp.concatenate(
        [real_in * real_gain - imag_in * imag_gain, real_in * imag_gain + imag_in * real_gain],
        axis=-1,
    )


def correlate_group(spectra, lag_tab, tile_pairs, pieces):
    first_rows, second_rows, weights, counts = pieces
    half_len = spectra.shape[1] // 2
    first_spec = spectra[first_rows].astype(jnp.float32)
    second_spec = spectra[second_rows].astype(jnp.float32)
    first_re, first_im = (first_spec[:, :half_len], first_spec[:, half_len:])
    second_re, second_im = (second_spec[:, :half_len], second_spec[:, half_len:])
    row_weight = jnp.repeat(weights, tile_pairs, axis=0)
    cross_spec = jnp.concatenate(
        [
            (first_re * second_re + first_im * second_im) * row_weight,
            (first_im * second_re - first_re * second_im) * row_weight,
        ],
        axis=1,
    ).astype(jnp.bfloat16)
    lagged = jnp.dot(cross_spec, lag_tab, preferred_element_type=jnp.float32)
    live_rows = jnp.arange(lagged.shape[0], dtype=jnp.int32) % tile_pairs < jnp.repeat(
        counts, tile_pairs
    )
    return jnp.where(live_rows[:, None], lagged, jnp.zeros_like(lagged))


def shards(windows, rotation, source_inverse, send_rows, tile_station, tile_count, pair_rows):
    ev_dev, components, stations, length = windows.shape
    half_len = length // 2
    owners = lax.axis_size("ev")
    dft_table = spectral_table(length)
    deconvolved = event_spectra(windows, rotation, source_inverse, dft_table)
    local_power = jnp.sum(
        deconvolved[..., :half_len] ** 2 + deconvolved[..., half_len:] ** 2, axis=0
    )
    power_sum = lax.psum(local_power, "ev")
    weight = 1.0 / (power_sum / (ev_dev * owners) + epsilon)
    capacity = send_rows.shape[1]
    slot_total = owners * capacity
    own_rows = deconvolved.astype(jnp.bfloat16).reshape(ev_dev * stations, length)
    received = lax.all_to_all(own_rows[send_rows], "ev", split_axis=0, concat_axis=0, tiled=True)
    received = received.reshape(slot_total, length)
    tiles_dev = tile_station.shape[0]
    tile_pairs = pair_rows.shape[1] // tiles_dev
    onehot = (tile_station[:, None] == jnp.arange(stations, dtype=jnp.int32)[None, :]).astype(
        jnp.float32
    )
    tile_weight = jnp.dot(onehot, weight, precision=lax.Precision.HIGHEST)
    groups = tiles_dev // 4
    group_rows = 4 * tile_pairs
    correlate = partial(correlate_group, received, lag_table(length, LAGS), tile_pairs)
    result = lax.map(
        correlate,
        (
            pair_rows[0].reshape(groups, group_rows),
            pair_rows[1].reshape(groups, group_rows),
            tile_weight.reshape(groups, 4, half_len),
            tile_count.reshape(groups, 4),
        ),
    )
    return result.reshape(groups * group_rows, LAGS)


def solution(mesh):
    in_specs = (
        P(("grp", "ev"), None, None, None),
        P(("grp", "ev"), None, None),
        P(("grp", "ev"), None),
        P(("grp", "ev"), None),
        P(("grp", "ev")),
        P(("grp", "ev")),
        P(None, ("grp", "ev")),
    )
    out_specs = P(("grp", "ev"), None)
    return jax.shard_map(shards, mesh=mesh, in_specs=in_specs, out_specs=out_specs, check_vma=False)
```

profile of v0, /device:TPU:0, one launch (start us, length us, event | category | flops | bytes accessed | tf_op | source)
XLA Modules:
  0.0 418.1 jit_solution(10348635386327450920)
XLA Ops:
  6.5 8.6 %multiply_convert_fusion = (bf16[1024,512]{1,0:T(8,128)(2,1)S(1)}, bf16[1024,512]{1,0:T(8,128)(2,1)S(1)}) fusion(), kind=kLoop, calls=%fused_computation.38 | loop fusion | flops 9961472 | bytes 2097152 | tf_op jit(solution)/shard_map/convert.10
  20.5 9.7 %gather_fusion.2 = bf16[2048,1024]{1,0:T(8,128)(2,1)} fusion(bf16[512,1024]{1,0:T(8,128)(2,1)S(1)} %pad_maximum_fusion, s32[2048]{0:T(1024)S(1)} %broadcast_clamp_fusion), kind=kCustom, calls=%fused_computation.2 | custom fusion | bytes 8396800 | tf_op jit(solution)/shard_map/gather | solution.py:92
  30.1 7.5 %all-to-all-start = ((bf16[32,64,1024]{2,1,0:T(8,128)(2,1)}), bf16[32,64,1024]{2,1,0:T(8,128)(2,1)}, u32[]{:S(2)}, u32[]{:S(2)}) async-start(bf16[32,64,1024]{2,1,0:T(8,128)(2,1)} %bitcast.58), calls=%async_computation | async-start | bytes 8388608 | tf_op jit(solution)/shard_map/all_to_all | solution.py:92
  41.8 148.0 %all-reduce.2.cloned.1.call-done = f32[64,512]{1,0:T(8,128)} async-done(((f32[64,512]{1,0:T(8,128)}), f32[64,512]{1,0:T(8,128)}) %all-reduce.2.cloned.1.call-update) | async-done | bytes 131088 | tf_op jit(solution)/shard_map/psum | solution.py:87
  191.1 220.2 %while.12 = (s32[]{:T(128)}, f32[16,512,255]{2,1,0:T(8,128)}, s32[16,4]{1,0:T(8,128)S(1)}, s32[16,512]{1,0:T(8,128)S(1)}, bf16[2048,1024]{1,0:T(8,128)(2,1)}, /*...) while((s32[]{:T(128)}, f32[16,512,255]{2,1,0:T(8,128)}, ...), condition=%wide.region_4.5_spmd, body=%wide.region_3.4_spmd.sunk | while | flops 273293312 | bytes 19963572 | solution.py:103
  191.1 5.5 %gather_fusion = bf16[512,1024]{1,0:T(8,128)(2,1)S(1)} fusion(bf16[2048,1024]{1,0:T(8,128)(2,1)} %get-tuple-element.218, s32[1024]{0:T(1024)S(1)} %pad_clamp_fusion.4), kind=kCustom, calls=%fused_computation.1.clone.1 | custom fusion | bytes 2099200 | tf_op jit(solution)/shard_map/while/body/eval_jaxpr/gather | solution.py:60
  196.8 5.5 %gather_fusion.1 = bf16[512,1024]{1,0:T(8,128)(2,1)S(1)} fusion(bf16[2048,1024]{1,0:T(8,128)(2,1)} %get-tuple-element.218, s32[1024]{0:T(1024)S(1)} %pad_clamp_fusion.5), kind=kCustom, calls=%fused_computation.clone.1 | custom fusion | bytes 2099200 | tf_op jit(solution)/shard_map/while/body/eval_jaxpr/gather | solution.py:59
  204.9 5.5 %gather_fusion = bf16[512,1024]{1,0:T(8,128)(2,1)S(1)} fusion(bf16[2048,1024]{1,0:T(8,128)(2,1)} %get-tuple-element.218, s32[1024]{0:T(1024)S(1)} %pad_clamp_fusion.4), kind=kCustom, calls=%fused_computation.1.clone.1 | custom fusion | bytes 2099200 | tf_op jit(solution)/shard_map/while/body/eval_jaxpr/gather | solution.py:60
  210.6 5.5 %gather_fusion.1 = bf16[512,1024]{1,0:T(8,128)(2,1)S(1)} fusion(bf16[2048,1024]{1,0:T(8,128)(2,1)} %get-tuple-element.218, s32[1024]{0:T(1024)S(1)} %pad_clamp_fusion.5), kind=kCustom, calls=%fused_computation.clone.1 | custom fusion | bytes 2099200 | tf_op jit(solution)/shard_map/while/body/eval_jaxpr/gather | solution.py:59
  218.6 5.5 %gather_fusion = bf16[512,1024]{1,0:T(8,128)(2,1)S(1)} fusion(bf16[2048,1024]{1,0:T(8,128)(2,1)} %get-tuple-element.218, s32[1024]{0:T(1024)S(1)} %pad_clamp_fusion.4), kind=kCustom, calls=%fused_computation.1.clone.1 | custom fusion | bytes 2099200 | tf_op jit(solution)/shard_map/while/body/eval_jaxpr/gather | solution.py:60
  224.4 5.5 %gather_fusion.1 = bf16[512,1024]{1,0:T(8,128)(2,1)S(1)} fusion(bf16[2048,1024]{1,0:T(8,128)(2,1)} %get-tuple-element.218, s32[1024]{0:T(1024)S(1)} %pad_clamp_fusion.5), kind=kCustom, calls=%fused_computation.clone.1 | custom fusion | bytes 2099200 | tf_op jit(solution)/shard_map/while/body/eval_jaxpr/gather | solution.py:59
  232.4 5.5 %gather_fusion = bf16[512,1024]{1,0:T(8,128)(2,1)S(1)} fusion(bf16[2048,1024]{1,0:T(8,128)(2,1)} %get-tuple-element.218, s32[1024]{0:T(1024)S(1)} %pad_clamp_fusion.4), kind=kCustom, calls=%fused_computation.1.clone.1 | custom fusion | bytes 2099200 | tf_op jit(solution)/shard_map/while/body/eval_jaxpr/gather | solution.py:60
  238.1 5.5 %gather_fusion.1 = bf16[512,1024]{1,0:T(8,128)(2,1)S(1)} fusion(bf16[2048,1024]{1,0:T(8,128)(2,1)} %get-tuple-element.218, s32[1024]{0:T(1024)S(1)} %pad_clamp_fusion.5), kind=kCustom, calls=%fused_computation.clone.1 | custom fusion | bytes 2099200 | tf_op jit(solution)/shard_map/while/body/eval_jaxpr/gather | solution.py:59
  259.9 5.5 %gather_fusion = bf16[512,1024]{1,0:T(8,128)(2,1)S(1)} fusion(bf16[2048,1024]{1,0:T(8,128)(2,1)} %get-tuple-element.218, s32[1024]{0:T(1024)S(1)} %pad_clamp_fusion.4), kind=kCustom, calls=%fused_computation.1.clone.1 | custom fusion | bytes 2099200 | tf_op jit(solution)/shard_map/while/body/eval_jaxpr/gather | solution.py:60
  265.6 5.5 %gather_fusion.1 = bf16[512,1024]{1,0:T(8,128)(2,1)S(1)} fusion(bf16[2048,1024]{1,0:T(8,128)(2,1)} %get-tuple-element.218, s32[1024]{0:T(1024)S(1)} %pad_clamp_fusion.5), kind=kCustom, calls=%fused_computation.clone.1 | custom fusion | bytes 2099200 | tf_op jit(solution)/shard_map/while/body/eval_jaxpr/gather | solution.py:59
  273.7 5.5 %gather_fusion = bf16[512,1024]{1,0:T(8,128)(2,1)S(1)} fusion(bf16[2048,1024]{1,0:T(8,128)(2,1)} %get-tuple-element.218, s32[1024]{0:T(1024)S(1)} %pad_clamp_fusion.4), kind=kCustom, calls=%fused_computation.1.clone.1 | custom fusion | bytes 2099200 | tf_op jit(solution)/shard_map/while/body/eval_jaxpr/gather | solution.py:60
  279.4 5.5 %gather_fusion.1 = bf16[512,1024]{1,0:T(8,128)(2,1)S(1)} fusion(bf16[2048,1024]{1,0:T(8,128)(2,1)} %get-tuple-element.218, s32[1024]{0:T(1024)S(1)} %pad_clamp_fusion.5), kind=kCustom, calls=%fused_computation.clone.1 | custom fusion | bytes 2099200 | tf_op jit(solution)/shard_map/while/body/eval_jaxpr/gather | solution.py:59
  287.4 5.5 %gather_fusion = bf16[512,1024]{1,0:T(8,128)(2,1)S(1)} fusion(bf16[2048,1024]{1,0:T(8,128)(2,1)} %get-tuple-element.218, s32[1024]{0:T(1024)S(1)} %pad_clamp_fusion.4), kind=kCustom, calls=%fused_computation.1.clone.1 | custom fusion | bytes 2099200 | tf_op jit(solution)/shard_map/while/body/eval_jaxpr/gather | solution.py:60
  293.2 5.5 %gather_fusion.1 = bf16[512,1024]{1,0:T(8,128)(2,1)S(1)} fusion(bf16[2048,1024]{1,0:T(8,128)(2,1)} %get-tuple-element.218, s32[1024]{0:T(1024)S(1)} %pad_clamp_fusion.5), kind=kCustom, calls=%fused_computation.clone.1 | custom fusion | bytes 2099200 | tf_op jit(solution)/shard_map/while/body/eval_jaxpr/gather | solution.py:59
  301.2 5.5 %gather_fusion = bf16[512,1024]{1,0:T(8,128)(2,1)S(1)} fusion(bf16[2048,1024]{1,0:T(8,128)(2,1)} %get-tuple-element.218, s32[1024]{0:T(1024)S(1)} %pad_clamp_fusion.4), kind=kCustom, calls=%fused_computation.1.clone.1 | custom fusion | bytes 2099200 | tf_op jit(solution)/shard_map/while/body/eval_jaxpr/gather | solution.py:60
  306.9 5.5 %gather_fusion.1 = bf16[512,1024]{1,0:T(8,128)(2,1)S(1)} fusion(bf16[2048,1024]{1,0:T(8,128)(2,1)} %get-tuple-element.218, s32[1024]{0:T(1024)S(1)} %pad_clamp_fusion.5), kind=kCustom, calls=%fused_computation.clone.1 | custom fusion | bytes 2099200 | tf_op jit(solution)/shard_map/while/body/eval_jaxpr/gather | solution.py:59
  315.0 5.5 %gather_fusion = bf16[512,1024]{1,0:T(8,128)(2,1)S(1)} fusion(bf16[2048,1024]{1,0:T(8,128)(2,1)} %get-tuple-element.218, s32[1024]{0:T(1024)S(1)} %pad_clamp_fusion.4), kind=kCustom, calls=%fused_computation.1.clone.1 | custom fusion | bytes 2099200 | tf_op jit(solution)/shard_map/while/body/eval_jaxpr/gather | solution.py:60
  320.7 5.5 %gather_fusion.1 = bf16[512,1024]{1,0:T(8,128)(2,1)S(1)} fusion(bf16[2048,1024]{1,0:T(8,128)(2,1)} %get-tuple-element.218, s32[1024]{0:T(1024)S(1)} %pad_clamp_fusion.5), kind=kCustom, calls=%fused_computation.clone.1 | custom fusion | bytes 2099200 | tf_op jit(solution)/shard_map/while/body/eval_jaxpr/gather | solution.py:59
  328.7 5.5 %gather_fusion = bf16[512,1024]{1,0:T(8,128)(2,1)S(1)} fusion(bf16[2048,1024]{1,0:T(8,128)(2,1)} %get-tuple-element.218, s32[1024]{0:T(1024)S(1)} %pad_clamp_fusion.4), kind=kCustom, calls=%fused_computation.1.clone.1 | custom fusion | bytes 2099200 | tf_op jit(solution)/shard_map/while/body/eval_jaxpr/gather | solution.py:60
  334.4 5.5 %gather_fusion.1 = bf16[512,1024]{1,0:T(8,128)(2,1)S(1)} fusion(bf16[2048,1024]{1,0:T(8,128)(2,1)} %get-tuple-element.218, s32[1024]{0:T(1024)S(1)} %pad_clamp_fusion.5), kind=kCustom, calls=%fused_computation.clone.1 | custom fusion | bytes 2099200 | tf_op jit(solution)/shard_map/while/body/eval_jaxpr/gather | solution.py:59
  342.5 5.5 %gather_fusion = bf16[512,1024]{1,0:T(8,128)(2,1)S(1)} fusion(bf16[2048,1024]{1,0:T(8,128)(2,1)} %get-tuple-element.218, s32[1024]{0:T(1024)S(1)} %pad_clamp_fusion.4), kind=kCustom, calls=%fused_computation.1.clone.1 | custom fusion | bytes 2099200 | tf_op jit(solution)/shard_map/while/body/eval_jaxpr/gather | solution.py:60
  348.2 5.5 %gather_fusion.1 = bf16[512,1024]{1,0:T(8,128)(2,1)S(1)} fusion(bf16[2048,1024]{1,0:T(8,128)(2,1)} %get-tuple-element.218, s32[1024]{0:T(1024)S(1)} %pad_clamp_fusion.5), kind=kCustom, calls=%fused_computation.clone.1 | custom fusion | bytes 2099200 | tf_op jit(solution)/shard_map/while/body/eval_jaxpr/gather | solution.py:59
  356.2 5.5 %gather_fusion = bf16[512,1024]{1,0:T(8,128)(2,1)S(1)} fusion(bf16[2048,1024]{1,0:T(8,128)(2,1)} %get-tuple-element.218, s32[1024]{0:T(1024)S(1)} %pad_clamp_fusion.4), kind=kCustom, calls=%fused_computation.1.clone.1 | custom fusion | bytes 2099200 | tf_op jit(solution)/shard_map/while/body/eval_jaxpr/gather | solution.py:60
  362.0 5.5 %gather_fusion.1 = bf16[512,1024]{1,0:T(8,128)(2,1)S(1)} fusion(bf16[2048,1024]{1,0:T(8,128)(2,1)} %get-tuple-element.218, s32[1024]{0:T(1024)S(1)} %pad_clamp_fusion.5), kind=kCustom, calls=%fused_computation.clone.1 | custom fusion | bytes 2099200 | tf_op jit(solution)/shard_map/while/body/eval_jaxpr/gather | solution.py:59
  383.8 5.5 %gather_fusion = bf16[512,1024]{1,0:T(8,128)(2,1)S(1)} fusion(bf16[2048,1024]{1,0:T(8,128)(2,1)} %get-tuple-element.218, s32[1024]{0:T(1024)S(1)} %pad_clamp_fusion.4), kind=kCustom, calls=%fused_computation.1.clone.1 | custom fusion | bytes 2099200 | tf_op jit(solution)/shard_map/while/body/eval_jaxpr/gather | solution.py:60
  389.5 5.5 %gather_fusion.1 = bf16[512,1024]{1,0:T(8,128)(2,1)S(1)} fusion(bf16[2048,1024]{1,0:T(8,128)(2,1)} %get-tuple-element.218, s32[1024]{0:T(1024)S(1)} %pad_clamp_fusion.5), kind=kCustom, calls=%fused_computation.clone.1 | custom fusion | bytes 2099200 | tf_op jit(solution)/shard_map/while/body/eval_jaxpr/gather | solution.py:59
  397.5 5.5 %gather_fusion = bf16[512,1024]{1,0:T(8,128)(2,1)S(1)} fusion(bf16[2048,1024]{1,0:T(8,128)(2,1)} %get-tuple-element.218, s32[1024]{0:T(1024)S(1)} %pad_clamp_fusion.4), kind=kCustom, calls=%fused_computation.1.clone.1 | custom fusion | bytes 2099200 | tf_op jit(solution)/shard_map/while/body/eval_jaxpr/gather | solution.py:60
  (232 shorter events, 82.2 us)
Async XLA Ops:
  6.5 8.6 %copy-start.4 = (bf16[8,3,64]{2,0,1:T(8,128)(2,1)S(1)}, bf16[8,3,64]{2,0,1:T(8,128)(2,1)}, u32[]{:S(2)}) copy-start(bf16[8,3,64]{2,0,1:T(8,128)(2,1)} %param.10) | copy-start | bytes 9220
  6.5 8.6 %copy-start.2 = (bf16[8,1024]{1,0:T(8,128)(2,1)S(1)}, bf16[8,1024]{1,0:T(8,128)(2,1)}, u32[]{:S(2)}) copy-start(bf16[8,1024]{1,0:T(8,128)(2,1)} %param.11) | copy-start | bytes 49156
  6.5 8.7 %copy-start.3 = (s32[32,64]{1,0:T(8,128)S(1)}, s32[32,64]{1,0:T(8,128)}, u32[]{:S(2)}) copy-start(s32[32,64]{1,0:T(8,128)} %param.12) | copy-start | bytes 24580
  30.1 8.2 %copy-start.1 = (s32[2,8192]{1,0:T(2,128)S(1)}, s32[2,8192]{1,0:T(2,128)}, u32[]{:S(2)}) copy-start(s32[2,8192]{1,0:T(2,128)} %param.15) | copy-start | bytes 196612
  30.1 8.4 %copy-start.5 = (s32[64]{0:T(128)S(1)}, s32[64]{0:T(128)}, u32[]{:S(2)}) copy-start(s32[64]{0:T(128)} %param.14) | copy-start | bytes 772
  30.1 159.7 %copy-start.6 = (s32[64]{0:T(128)S(1)}, s32[64]{0:T(128)}, u32[]{:S(2)}) copy-start(s32[64]{0:T(128)} %param.13) | copy-start | bytes 772
  30.1 160.9 %all-to-all-start = ((bf16[32,64,1024]{2,1,0:T(8,128)(2,1)}), bf16[32,64,1024]{2,1,0:T(8,128)(2,1)}, u32[]{:S(2)}, u32[]{:S(2)}) async-start(bf16[32,64,1024]{2,1,0:T(8,128)(2,1)} %bitcast.58), calls=%async_computation | async-start | bytes 8388608 | tf_op jit(solution)/shard_map/all_to_all | solution.py:92
  37.6 152.3 %all-reduce.2.cloned.1.call-start = ((), (), s32[]{:S(2)}) async-start(), calls=%async_computation.1 | async-start | bytes 262144 | tf_op jit(solution)/shard_map/psum | solution.py:87
  202.6 1.0 copy-start
  216.3 1.0 copy-start
  230.1 1.0 copy-start
  243.9 1.0 copy-start
  257.6 1.0 copy-start
  271.4 1.0 copy-start
  285.1 1.0 copy-start
  298.9 1.0 copy-start
  312.7 1.0 copy-start
  326.4 1.0 copy-start
  340.2 1.0 copy-start
  353.9 1.0 copy-start
  367.7 1.0 copy-start
  381.5 1.0 copy-start
  395.2 1.0 copy-start
  409.0 1.0 copy-start
Sparse Core Ops, SparseCore 0:
  43.9 145.8 all-reduce.1
where the time goes:
time: 420 us; the launch traced here: 418 us
  local copies, waits for them, and re-layouts  191 us (45%)
  waiting for transfers between devices  149 us (35%)
  other arithmetic  33.9 us (8%)
  matrix products  22.1 us (5%)
  between operations  13.6 us (3%)
  starting transfers between devices  7.5 us (2%)
    psum x1, waiting for transfers between devices, shards(): power_sum = lax.psum(local_power, 'ev')  148 us
    gather x16, local copies, waits for them, and re-layouts, correlate_group(): second_spec = spectra[second_rows].astype(jnp.float32)  87.3 us
    gather x16, local copies, waits for them, and re-layouts, correlate_group(): first_spec = spectra[first_rows].astype(jnp.float32)  87.3 us
    another operation x18, other arithmetic  19.9 us
    dot_general x16, matrix products, correlate_group(): lagged = jnp.dot(cross_spec, lag_tab, preferred_element_type=jnp.float32)  19.7 us
    gather x1, local copies, waits for them, and re-layouts, shards(): own_rows[send_rows]  9.66 us
  transfers between devices with their start and end apart: 2, of which 1 were waited for; matrix products, arithmetic and copies ran while one was open for 1% of the time, Pallas kernels for 0%

commit v1 on v0

v1 whole, which is shorter than its diff:
```python
from functools import partial
import math

import jax
import jax.numpy as jnp
import numpy as np
from jax import lax
from jax.experimental import pallas as pl
from jax.experimental.pallas import tpu as pltpu
from jax.sharding import PartitionSpec as P

LAGS = 255
SUB = 8
LANES = 128
CHUNKS = 4

epsilon = 1e-06
F32 = jnp.float32
BF16 = jnp.bfloat16


def spectral_table(length):
    half_len = length // 2
    samples = np.arange(length)[:, None]
    frequency = np.arange(half_len)[None, :]
    angles = (samples * frequency % length) * (2.0 * math.pi / length)
    factor = 1.0 / math.sqrt(length)
    table = np.concatenate([np.cos(angles) * factor, -np.sin(angles) * factor], axis=1)
    return jnp.asarray(table.astype(np.float32)).astype(BF16)


def lag_table(length, lag_count, width):
    half_len = length // 2
    frequency = np.arange(half_len)[:, None]
    shifts = np.arange(lag_count)[None, :] - lag_count // 2
    angles = (frequency * shifts % length) * (2.0 * math.pi / length)
    factor = 1.0 / math.sqrt(half_len)
    table = np.concatenate([np.cos(angles) * factor, -np.sin(angles) * factor], axis=0)
    table = np.pad(table, ((0, 0), (0, width - lag_count)))
    return jnp.asarray(table.astype(np.float32)).astype(BF16)


def column(values):
    return jnp.transpose(jnp.broadcast_to(values, (LANES, LANES)))


def one_hot(values, width):
    down = column(values)
    lane = lax.broadcasted_iota(jnp.int32, (LANES, LANES), 1)
    parts = [
        jnp.where(down == lane + LANES * j, 1.0, 0.0).astype(BF16) for j in range(width // LANES)
    ]
    return jnp.concatenate(parts, axis=1)


def front_kernel(steps, win_ref, rot_ref, inv_ref, table_ref, index_ref, *refs):
    *send_refs, power_ref, rows_ref = refs
    step = pl.program_id(0)
    events, comps, stations, length = win_ref.shape
    half_len = length // 2
    blocks = []
    for e in range(events):
        rot = jnp.transpose(rot_ref[e].astype(F32))
        total = rot[:, 0:1] * win_ref[e, 0].astype(F32)
        for c in range(1, comps):
            total += rot[:, c : c + 1] * win_ref[e, c].astype(F32)
        blocks.append(total.astype(BF16))
    transverse = jnp.concatenate(blocks, axis=0)
    spectrum = jnp.dot(transverse, table_ref[...], preferred_element_type=F32)
    power = jnp.zeros((stations, half_len), F32)
    for e in range(events):
        re_in = spectrum[e * stations : (e + 1) * stations, :half_len]
        im_in = spectrum[e * stations : (e + 1) * stations, half_len:]
        gain = inv_ref[0, e : e + 1, :].astype(F32)
        re_g, im_g = gain[:, :half_len], gain[:, half_len:]
        re = re_in * re_g - im_in * im_g
        im = re_in * im_g + im_in * re_g
        power += re * re + im * im
        base = pl.multiple_of((step * events + e) * stations, stations)
        rows_ref[pl.ds(base, stations), :half_len] = re.astype(BF16)
        rows_ref[pl.ds(base, stations), half_len:] = im.astype(BF16)

    @pl.when(step == 0)
    def _():
        power_ref[...] = power

    @pl.when(step > 0)
    def _():
        power_ref[...] += power

    @pl.when(step == steps - 1)
    def _():
        rows = rows_ref[...]
        line = 0
        for ref in send_refs:
            for j in range(ref.shape[0] // LANES):
                pick = one_hot(index_ref[line : line + 1, :], rows.shape[0])
                picked = jnp.dot(pick, rows, preferred_element_type=F32)
                ref[j * LANES : (j + 1) * LANES, :] = picked.astype(BF16)
                line += 1


def front(windows, rotation, source_inverse, index, table, chunks):
    ev_dev, comps, stations, length = windows.shape
    steps = 2 if ev_dev % 2 == 0 else 1
    events = ev_dev // steps
    lines = index.shape[0]
    rows_c = lines * LANES // chunks
    whole = lambda *shape: pl.BlockSpec(shape, lambda i: (0,) * len(shape))
    return pl.pallas_call(
        partial(front_kernel, steps),
        grid=(steps,),
        in_specs=[
            pl.BlockSpec((events, comps, stations, length), lambda i: (i, 0, 0, 0)),
            pl.BlockSpec((events, comps, stations), lambda i: (i, 0, 0)),
            pl.BlockSpec((1, events, length), lambda i: (i, 0, 0)),
            whole(length, length),
            whole(lines, LANES),
        ],
        out_specs=[whole(rows_c, length)] * chunks + [whole(stations, length // 2)],
        out_shape=[jax.ShapeDtypeStruct((rows_c, length), BF16)] * chunks
        + [jax.ShapeDtypeStruct((stations, length // 2), F32)],
        scratch_shapes=[pltpu.VMEM((ev_dev * stations, length), BF16)],
        compiler_params=pltpu.CompilerParams(vmem_limit_bytes=48 << 20),
        name="front",
    )(windows, rotation, source_inverse.reshape(steps, events, length), table, index)


def pair_kernel(geo, first, station_ref, count_ref, pair_ref, got_ref, weight_ref, lag_ref, *refs):
    out_ref = refs[-1]
    owners, cap, joint = geo
    group = pl.program_id(0) + first
    length = got_ref.shape[-1]
    half_len = length // 2
    rows = got_ref[...].reshape(owners * SUB, length)
    width = owners * SUB
    for j in range(joint):
        for i in range(SUB):
            tile = j * cap + group * SUB + i
            picks = []
            for m in range(2):
                r = pair_ref[m, j, i : i + 1, :]
                place = lax.div(r, cap) * SUB + lax.rem(r, SUB)
                picks.append(one_hot(place, width))
            members = jnp.dot(jnp.concatenate(picks, axis=0), rows, preferred_element_type=F32)
            a, b = members[:LANES], members[LANES:]
            re_a, im_a = a[:, :half_len], a[:, half_len:]
            re_b, im_b = b[:, :half_len], b[:, half_len:]
            scale = weight_ref[pl.ds(station_ref[tile], 1), :]
            cross = jnp.concatenate(
                [
                    ((re_a * re_b + im_a * im_b) * scale).astype(BF16),
                    ((im_a * re_b - re_a * im_b) * scale).astype(BF16),
                ],
                axis=1,
            )
            lagged = jnp.dot(cross, lag_ref[...], preferred_element_type=F32)
            slot = lax.broadcasted_iota(jnp.int32, lagged.shape, 0)
            lagged = jnp.where(slot < count_ref[tile], lagged, 0.0)
            out_ref[j, i * LANES : (i + 1) * LANES, :] = lagged[:, :LAGS]


def correlate(chunk, chunks, geo, stations_of, counts, pairs, received, weight, lag_tab, previous):
    owners, cap, joint = geo
    groups = cap // SUB
    steps = groups // chunks
    first = chunk * steps
    length = received.shape[-1]
    stations = weight.shape[0]
    in_specs = [
        pl.BlockSpec((2, joint, SUB, LANES), lambda i, *_: (0, 0, i + first, 0)),
        pl.BlockSpec((owners, SUB, length), lambda i, *_: (0, i, 0)),
        pl.BlockSpec((stations, length // 2), lambda i, *_: (0, 0)),
        pl.BlockSpec(lag_tab.shape, lambda i, *_: (0, 0)),
    ]
    args = [pairs, received, weight, lag_tab]
    aliases = {}
    if previous is not None:
        in_specs.append(pl.BlockSpec(memory_space=pl.ANY))
        args.append(previous)
        aliases = {6: 0}
    return pl.pallas_call(
        partial(pair_kernel, geo, first),
        grid_spec=pltpu.PrefetchScalarGridSpec(
            num_scalar_prefetch=2,
            grid=(steps,),
            in_specs=in_specs,
            out_specs=pl.BlockSpec((joint, SUB * LANES, LAGS), lambda i, *_: (0, i + first, 0)),
        ),
        out_shape=jax.ShapeDtypeStruct((joint, cap * LANES, LAGS), F32),
        input_output_aliases=aliases,
        compiler_params=pltpu.CompilerParams(vmem_limit_bytes=48 << 20),
        name="pairs",
    )(stations_of, counts, *args)


def power_total(power, owners):
    stations, half_len = power.shape
    share = stations // owners
    parts = power.reshape(owners, share, half_len)
    mine = lax.all_to_all(parts, "ev", split_axis=0, concat_axis=0, tiled=True)
    mine = jnp.sum(mine, axis=0)
    every = jnp.broadcast_to(mine[None], (owners, share, half_len))
    every = lax.all_to_all(every, "ev", split_axis=0, concat_axis=0, tiled=True)
    return every.reshape(stations, half_len)


def shards(windows, rotation, source_inverse, send_rows, tile_station, tile_count, pair_rows):
    ev_dev, comps, stations, length = windows.shape
    owners = lax.axis_size("ev")
    cap = send_rows.shape[1]
    tiles_dev = tile_station.shape[0]
    joint = tiles_dev // cap
    geo = (owners, cap, joint)
    chunks = CHUNKS
    index = send_rows.reshape(owners, chunks, cap // chunks).swapaxes(0, 1).reshape(-1, LANES)
    *sends, power = front(
        windows, rotation, source_inverse, index, spectral_table(length), chunks
    )
    power_sum = power_total(power, owners)
    weight = 1.0 / (power_sum / (ev_dev * owners) + epsilon)
    pairs = pair_rows.reshape(2, joint, cap, LANES)
    lag_tab = lag_table(length, LAGS, LAGS + 1)
    result = None
    for chunk, send in enumerate(sends):
        got = lax.all_to_all(
            send.reshape(owners, cap // chunks, length), "ev", split_axis=0, concat_axis=0, tiled=True
        )
        result = correlate(
            chunk, chunks, geo, tile_station, tile_count, pairs, got, weight, lag_tab, result
        )
    return result.reshape(tiles_dev * LANES, LAGS)


def solution(mesh):
    in_specs = (
        P(("grp", "ev"), None, None, None),
        P(("grp", "ev"), None, None),
        P(("grp", "ev"), None),
        P(("grp", "ev"), None),
        P(("grp", "ev")),
        P(("grp", "ev")),
        P(None, ("grp", "ev")),
    )
    out_specs = P(("grp", "ev"), None)
    return jax.shard_map(shards, mesh=mesh, in_specs=in_specs, out_specs=out_specs, check_vma=False)
```

time: 420 us -> 164 us (0.39)
  local copies, waits for them, and re-layouts: 191 us -> 6.89 us
  waiting for transfers between devices: 149 us -> 3.11 us
  blocking collectives: 0 us -> 114 us
  Pallas kernels: 0 us -> 35.2 us
  other arithmetic: 33.9 us -> 0.16 us
  matrix products: 22.1 us -> 0 us
  between operations: 13.6 us -> 0.12 us
    gather x33 -> x0, local copies, waits for them, and re-layouts: 184 us -> none  [the longest x16 87.3 us: correlate_group(): second_spec = spectra[second_rows].astype(jnp.float32)]
    psum x1 -> x0, waiting for transfers between devices: 148 us -> none  [shards(): power_sum = lax.psum(local_power, 'ev')]
    all_to_all x0 -> x5, blocking collectives: none -> 114 us  [the longest x3 88.4 us: shards(): lax.all_to_all(send.reshape(owners, cap // chunks, length), 'ev', split_a...]
    pallas_call x0 -> x5, Pallas kernels: none -> 35.2 us  [the longest x4 28.5 us: correlate(): pl.pallas_call(partial(pair_kernel, geo, first), grid_spec=pltpu.Prefetch...]
    dot_general x18 -> x0, matrix products: 22.1 us -> none  [the longest x16 19.7 us: correlate_group(): lagged = jnp.dot(cross_spec, lag_tab, preferred_element_type=jnp.float32)]
    another operation x18 -> x0, other arithmetic: 19.9 us -> none
    convert_element_type x32 -> x0, other arithmetic: 7.7 us -> none  [the longest x16 3.95 us: correlate_group(): first_spec = spectra[first_rows].astype(jnp.float32)]
    while x32 -> x0, local copies, waits for them, and re-layouts: 6.02 us -> none
  transfers between devices with their start and end apart: 2 -> 1, of which waited for: 1 -> 1; matrix products, arithmetic and copies ran while one was open for 1% -> 0% of each run, Pallas kernels for 0% -> 13%
where the time goes in v1:
time: 164 us; the launch traced here: 163 us
  blocking collectives  114 us (70%)
  Pallas kernels  35.2 us (21%)
  local copies, waits for them, and re-layouts  6.89 us (4%)
  starting transfers between devices  3.8 us (2%)
  waiting for transfers between devices  3.11 us (2%)
    all_to_all x3, blocking collectives, shards(): lax.all_to_all(send.reshape(owners, cap // chunks, length), 'ev', split_a...  88.4 us
    pallas_call x4, Pallas kernels, correlate(): pl.pallas_call(partial(pair_kernel, geo, first), grid_spec=pltpu.Prefetch...  28.5 us
    all_to_all x1, blocking collectives, power_total(): mine = lax.all_to_all(parts, 'ev', split_axis=0, concat_axis=0, tiled=True)  15.4 us
    all_to_all x1, blocking collectives, power_total(): every = lax.all_to_all(every, 'ev', split_axis=0, concat_axis=0, tiled=True)  9.97 us
    pallas_call x1, Pallas kernels, front(): pl.pallas_call(partial(front_kernel, steps), grid=(steps,), in_specs=[pl....  6.77 us
    unnamed x21, local copies, waits for them, and re-layouts  5.79 us
    all_to_all x1, starting transfers between devices, shards(): lax.all_to_all(send.reshape(owners, cap // chunks, length), 'ev', split_a...  3.8 us
  transfers between devices with their start and end apart: 1, of which 1 were waited for; matrix products, arithmetic and copies ran while one was open for 0% of the time, Pallas kernels for 13%

profile of v1, /device:TPU:0, one launch (start us, length us, event | category | flops | bytes accessed | tf_op | source)
XLA Modules:
  0.0 163.0 jit_solution(17957674887920397766)
XLA Ops:
  0.0 0.8 copy.17.rot_ref
  0.8 0.7 reshape.39.inv_ref
  1.5 0.8 copy.15
  2.3 0.1 copy.16
  2.4 0.1 reshape.41.index_ref
  2.5 6.8 %front.1 = (bf16[512,1024]{1,0:T(8,128)(2,1)S(1)}, bf16[512,1024]{1,0:T(8,128)(2,1)S(1)}, bf16[512,1024]{1,0:T(8,128)(2,1)S(1)}, bf16[512,1024]{1,0:T(8,128)(2,1)S(1)}, f32[64,512]{1,0:T(8,128)S(1)}) custom-call(bf16[8,3,64,1024]{3,2,1,0:T(8,128)(2,1)} %win_ref.1, bf16[8,3,64]{2,1,0:T(4,128)(2,1)S(1)} %copy.17.rot_ref, ...), custom_call_target="tpu_custom_call" | custom-call | tf_op jit(solution)/shard_map/front/pallas_call | solution.py:110
  9.2 0.0 copy-start.3
  9.3 1.0 copy-done.3
  10.2 1.0 copy-done.4
  11.2 1.0 copy-done.5
  12.2 0.1 reshape.43
  12.2 15.4 %all_to_all.30 = f32[32,2,512]{2,1,0:T(2,128)S(1)} all-to-all(f32[32,2,512]{2,1,0:T(2,128)S(1)} %reshape.43), channel_id=1, replica_groups=mesh['grp'=1,'ev'=32] {'ev'}, dimensions={0} | all-to-all | bytes 262144 | tf_op jit(solution)/shard_map/all_to_all | solution.py:201
  27.6 0.1 reduce_sum.9
  27.7 10.0 %all_to_all.31 = f32[32,2,512]{2,1,0:T(2,128)S(1)} all-to-all(f32[32,2,512]{2,1,0:T(2,128)S(1)} %broadcast_in_dim.2), channel_id=1, replica_groups=mesh['grp'=1,'ev'=32] {'ev'}, dimensions={0} | all-to-all | bytes 262144 | tf_op jit(solution)/shard_map/all_to_all | solution.py:204
  37.7 28.8 %all_to_all.32.got_ref = bf16[32,16,1024]{2,1,0:T(8,128)(2,1)S(1)} all-to-all(bf16[32,16,1024]{2,1,0:T(8,128)(2,1)} %bitcast.20), channel_id=1, replica_groups=mesh['grp'=1,'ev'=32] {'ev'}, dimensions={0} | all-to-all | bytes 2097152 | tf_op jit(solution)/shard_map/all_to_all | solution.py:226
  66.5 29.9 %all_to_all.33.got_ref = bf16[32,16,1024]{2,1,0:T(8,128)(2,1)} all-to-all(bf16[32,16,1024]{2,1,0:T(8,128)(2,1)} %bitcast.19), channel_id=1, replica_groups=mesh['grp'=1,'ev'=32] {'ev'}, dimensions={0} | all-to-all | bytes 2097152 | tf_op jit(solution)/shard_map/all_to_all | solution.py:226
  96.3 29.7 %all_to_all.34.got_ref = bf16[32,16,1024]{2,1,0:T(8,128)(2,1)} all-to-all(bf16[32,16,1024]{2,1,0:T(8,128)(2,1)S(1)} %bitcast.18), channel_id=1, replica_groups=mesh['grp'=1,'ev'=32] {'ev'}, dimensions={0} | all-to-all | bytes 2097152 | tf_op jit(solution)/shard_map/all_to_all | solution.py:226
  126.1 3.8 %all-to-all-start = ((bf16[32,16,1024]{2,1,0:T(8,128)(2,1)}), bf16[32,16,1024]{2,1,0:T(8,128)(2,1)S(1)}, u32[]{:S(2)}, u32[]{:S(2)}) async-start(bf16[32,16,1024]{2,1,0:T(8,128)(2,1)} %bitcast.17), calls=%async_computation | async-start | bytes 2097152 | tf_op jit(solution)/shard_map/all_to_all | solution.py:226
  129.9 0.0 copy-done.8
  129.9 0.1 add_divide_fusion
  130.0 0.1 div.18.weight_ref
  130.1 0.0 copy-start.1
  130.1 0.0 copy-done
  130.1 0.0 copy-done.7
  130.1 0.0 copy-done.6
  130.2 0.0 copy-start.2
  130.2 1.3 copy-done.2
  131.5 7.1 %pairs.4.refs_0_ = f32[1,8192,255]{2,1,0:T(8,128)} custom-call(s32[64]{0:T(128)S(1)} %copy-done.6, s32[64]{0:T(128)S(1)} %copy-done.7, s32[2,1,64,128]{3,2,1,0:T(8,128)S(1)} %bitcast.13, bf16[32,16,1024]{2,1,0:T(8,128)(2,1)S(1)} %copy-done.2, f32[64,512]{1,0:T(8,128)S(1)} %div.18.weight_ref, bf16[1024,256]{1,0:T(8,128)(2,1)S(1)} %copy-done), custom_call_target="tpu_custom_call" | custom-call | tf_op jit(solution)/shard_map/pairs/pallas_call | solution.py:182
  138.6 7.1 %pairs.5.refs_0_ = f32[1,8192,255]{2,1,0:T(8,128)} custom-call(s32[64]{0:T(128)S(1)} %copy-done.6, s32[64]{0:T(128)S(1)} %copy-done.7, s32[2,1,64,128]{3,2,1,0:T(8,128)S(1)} %bitcast.14, bf16[32,16,1024]{2,1,0:T(8,128)(2,1)S(1)} %copy-done.1, f32[64,512]{1,0:T(8,128)S(1)} %div.18.weight_ref, ...), custom_call_target="tpu_custom_call", output_to_operand_aliasing={{}: (6, {})} | custom-call | tf_op jit(solution)/shard_map/pairs/pallas_call | solution.py:182
  145.7 7.1 %pairs.6.refs_0_ = f32[1,8192,255]{2,1,0:T(8,128)} custom-call(s32[64]{0:T(128)S(1)} %copy-done.6, s32[64]{0:T(128)S(1)} %copy-done.7, s32[2,1,64,128]{3,2,1,0:T(8,128)S(1)} %bitcast.15, bf16[32,16,1024]{2,1,0:T(8,128)(2,1)S(1)} %all_to_all.32.got_ref, f32[64,512]{1,0:T(8,128)S(1)} %div.18.weight_ref, ...), custom_call_target="tpu_custom_call", output_to_operand_aliasing={{}: (6, {})} | custom-call | tf_op jit(solution)/shard_map/pairs/pallas_call | solution.py:182
  152.8 3.1 %all-to-all-done.got_ref = bf16[32,16,1024]{2,1,0:T(8,128)(2,1)S(1)} async-done(((bf16[32,16,1024]{2,1,0:T(8,128)(2,1)}), bf16[32,16,1024]{2,1,0:T(8,128)(2,1)S(1)}, u32[]{:S(2)}, u32[]{:S(2)}) %all-to-all-start) | async-done | bytes 1048608 | tf_op jit(solution)/shard_map/all_to_all | solution.py:226
  155.9 7.1 %pairs.7 = f32[1,8192,255]{2,1,0:T(8,128)} custom-call(s32[64]{0:T(128)S(1)} %copy-done.6, s32[64]{0:T(128)S(1)} %copy-done.7, s32[2,1,64,128]{3,2,1,0:T(8,128)S(1)} %bitcast.16, bf16[32,16,1024]{2,1,0:T(8,128)(2,1)S(1)} %all-to-all-done.got_ref, f32[64,512]{1,0:T(8,128)S(1)} %div.18.weight_ref, ...), custom_call_target="tpu_custom_call", output_to_operand_aliasing={{}: (6, {})} | custom-call | tf_op jit(solution)/shard_map/pairs/pallas_call | solution.py:182
  (9 shorter events, 0.1 us)
Async XLA Ops:
  0.0 130.1 %copy-start = (bf16[1024,256]{1,0:T(8,128)(2,1)S(1)}, bf16[1024,256]{1,0:T(8,128)(2,1)}, u32[]{:S(2)}) copy-start(bf16[1024,256]{1,0:T(8,128)(2,1)} %constant.19.lag_ref) | copy-start | bytes 1572868
  0.0 129.9 %copy-start.8 = (s32[2,8192]{1,0:T(2,128)S(1)}, s32[2,8192]{1,0:T(2,128)}, u32[]{:S(2)}) copy-start(s32[2,8192]{1,0:T(2,128)} %param.15) | copy-start | bytes 196612
  0.0 130.1 %copy-start.7 = (s32[64]{0:T(128)S(1)}, s32[64]{0:T(128)}, u32[]{:S(2)}) copy-start(s32[64]{0:T(128)} %count_ref.7) | copy-start | bytes 772
  0.0 130.1 %copy-start.6 = (s32[64]{0:T(128)S(1)}, s32[64]{0:T(128)}, u32[]{:S(2)}) copy-start(s32[64]{0:T(128)} %station_ref.7) | copy-start | bytes 772
  9.2 1.0 copy-start.3
  10.2 1.0 copy-start.4
  11.2 1.0 copy-start.5
  126.1 29.8 %all-to-all-start = ((bf16[32,16,1024]{2,1,0:T(8,128)(2,1)}), bf16[32,16,1024]{2,1,0:T(8,128)(2,1)S(1)}, u32[]{:S(2)}, u32[]{:S(2)}) async-start(bf16[32,16,1024]{2,1,0:T(8,128)(2,1)} %bitcast.17), calls=%async_computation | async-start | bytes 2097152 | tf_op jit(solution)/shard_map/all_to_all | solution.py:226
  130.1 8.5 %copy-start.1 = (bf16[32,16,1024]{2,1,0:T(8,128)(2,1)S(1)}, bf16[32,16,1024]{2,1,0:T(8,128)(2,1)}, u32[]{:S(2)}) copy-start(bf16[32,16,1024]{2,1,0:T(8,128)(2,1)} %all_to_all.33.got_ref) | copy-start | bytes 3145732
  130.2 1.3 copy-start.2

commit v2 on v1

v2 whole, which is shorter than its diff:
```python
from functools import partial
import math

import jax
import jax.numpy as jnp
import numpy as np
from jax import lax
from jax.experimental import pallas as pl
from jax.experimental.pallas import tpu as pltpu
from jax.sharding import PartitionSpec as P

LAGS = 255
SUB = 8
LANES = 128
CHUNKS = 2

epsilon = 1e-06
F32 = jnp.float32
BF16 = jnp.bfloat16


def spectral_table(length):
    half_len = length // 2
    samples = np.arange(length)[:, None]
    frequency = np.arange(half_len)[None, :]
    angles = (samples * frequency % length) * (2.0 * math.pi / length)
    factor = 1.0 / math.sqrt(length)
    table = np.concatenate([np.cos(angles) * factor, -np.sin(angles) * factor], axis=1)
    return jnp.asarray(table.astype(np.float32)).astype(BF16)


def lag_table(length, lag_count, width):
    half_len = length // 2
    frequency = np.arange(half_len)[:, None]
    shifts = np.arange(lag_count)[None, :] - lag_count // 2
    angles = (frequency * shifts % length) * (2.0 * math.pi / length)
    factor = 1.0 / math.sqrt(half_len)
    table = np.concatenate([np.cos(angles) * factor, -np.sin(angles) * factor], axis=0)
    table = np.pad(table, ((0, 0), (0, width - lag_count)))
    return jnp.asarray(table.astype(np.float32)).astype(BF16)


def column(values):
    return jnp.transpose(jnp.broadcast_to(values, (LANES, LANES)))


def one_hot(values, width):
    down = column(values)
    lane = lax.broadcasted_iota(jnp.int32, (LANES, LANES), 1)
    parts = [
        jnp.where(down == lane + LANES * j, 1.0, 0.0).astype(BF16) for j in range(width // LANES)
    ]
    return jnp.concatenate(parts, axis=1)


def split_high(values):
    high = values.astype(BF16)
    rest = (values - high.astype(F32)).astype(BF16)
    return jnp.concatenate([high, rest], axis=-1)


def join_high(values):
    width = values.shape[-1] // 2
    return values[..., :width].astype(F32) + values[..., width:].astype(F32)


def spectra_kernel(steps, half_ref, win_ref, rot_ref, inv_ref, table_ref, index_ref, rows_ref, power_ref):
    step = pl.program_id(0)
    events, comps, stations, length = win_ref.shape
    half_len = length // 2
    blocks = []
    turns = rot_ref[...].astype(F32)
    for e in range(events):
        turn = turns[:, e, :]
        for s in range(1, steps):
            turn = jnp.where(step == s, turns[:, s * events + e, :], turn)
        rot = jnp.transpose(turn)
        total = rot[:, 0:1] * win_ref[e, 0].astype(F32)
        for c in range(1, comps):
            total += rot[:, c : c + 1] * win_ref[e, c].astype(F32)
        blocks.append(total.astype(BF16))
    transverse = jnp.concatenate(blocks, axis=0)
    spectrum = jnp.dot(transverse, table_ref[...], preferred_element_type=F32)
    gains = inv_ref[...].astype(F32)
    power = jnp.zeros((stations, half_len), F32)
    for e in range(events):
        re_in = spectrum[e * stations : (e + 1) * stations, :half_len]
        im_in = spectrum[e * stations : (e + 1) * stations, half_len:]
        gain = gains[e : e + 1, :]
        for s in range(1, steps):
            gain = jnp.where(step == s, gains[s * events + e : s * events + e + 1, :], gain)
        re_g, im_g = gain[:, :half_len], gain[:, half_len:]
        re = re_in * re_g - im_in * im_g
        im = re_in * im_g + im_in * re_g
        power += re * re + im * im
        base = pl.multiple_of((step * events + e) * stations, stations)
        rows_ref[pl.ds(base, stations), :half_len] = re.astype(BF16)
        rows_ref[pl.ds(base, stations), half_len:] = im.astype(BF16)

    @pl.when(step == 0)
    def _():
        power_ref[...] = power
        owners, cap = index_ref.shape
        peers = owners // 2
        other = pl.multiple_of((1 - half_ref[0]) * peers, peers)
        wanted = index_ref[pl.ds(other, peers), :]
        tail = rows_ref.shape[0] - peers
        rows_ref[tail:, :] = jnp.zeros((peers, length), BF16)
        rows_ref[tail:, :cap] = (wanted // LANES).astype(F32).astype(BF16)
        rows_ref[tail:, LANES : LANES + cap] = (wanted % LANES).astype(F32).astype(BF16)

    @pl.when(step > 0)
    def _():
        power_ref[...] += power


def event_rows(half, windows, rotation, source_inverse, send_rows, table):
    ev_dev, comps, stations, length = windows.shape
    owners, cap = send_rows.shape
    steps = 2 if ev_dev % 2 == 0 else 1
    events = ev_dev // steps
    total = ev_dev * stations + owners // 2
    whole = lambda *shape: pl.BlockSpec(shape, lambda i, *_: (0,) * len(shape))
    return pl.pallas_call(
        partial(spectra_kernel, steps),
        grid_spec=pltpu.PrefetchScalarGridSpec(
            num_scalar_prefetch=1,
            grid=(steps,),
            in_specs=[
                pl.BlockSpec((events, comps, stations, length), lambda i, *_: (i, 0, 0, 0)),
                whole(comps, ev_dev, stations),
                whole(ev_dev, length),
                whole(length, length),
                whole(owners, cap),
            ],
            out_specs=[whole(total, length), whole(stations, length // 2)],
        ),
        out_shape=[
            jax.ShapeDtypeStruct((total, length), BF16),
            jax.ShapeDtypeStruct((stations, length // 2), F32),
        ],
        compiler_params=pltpu.CompilerParams(vmem_limit_bytes=48 << 20),
        name="spectra",
    )(half, windows, rotation.swapaxes(0, 1), source_inverse, table, send_rows)


def pick_rows(index, rows, store):
    peers, cap = index.shape
    lines = LANES // cap
    for first in range(0, peers, lines):
        line = jnp.concatenate([index[first + j : first + j + 1, :] for j in range(lines)], axis=1)
        picked = jnp.dot(one_hot(line, rows.shape[0]), rows, preferred_element_type=F32)
        picked = picked.astype(BF16)
        for j in range(lines):
            store(first + j, picked[j * cap : (j + 1) * cap])


def own_kernel(half_ref, rows_ref, power_ref, index_ref, send_ref, pad_ref):
    peers, total, length = send_ref.shape
    cap = index_ref.shape[1]
    stations = power_ref.shape[0]
    share = stations // peers
    mine = pl.multiple_of(half_ref[0] * peers, peers)

    def store(peer, picked):
        send_ref[peer, :cap, :] = picked

    pick_rows(index_ref[pl.ds(mine, peers), :], rows_ref[...], store)
    pad_ref[:stations, :] = power_ref[...]
    pad_ref[stations:, :] = jnp.zeros((SUB, length // 2), F32)
    for peer in range(peers):
        send_ref[peer, cap:, :] = split_high(pad_ref[peer * share : peer * share + SUB, :])


def own_sends(half, rows, power, send_rows):
    owners, cap = send_rows.shape
    peers = owners // 2
    length = rows.shape[1]
    stations = power.shape[0]
    whole = lambda *shape: pl.BlockSpec(shape, lambda i, *_: (0,) * len(shape))
    return pl.pallas_call(
        own_kernel,
        grid_spec=pltpu.PrefetchScalarGridSpec(
            num_scalar_prefetch=1,
            grid=(1,),
            in_specs=[
                whole(rows.shape[0] - peers, length),
                whole(*power.shape),
                whole(owners, cap),
            ],
            out_specs=whole(peers, cap + SUB, length),
            scratch_shapes=[pltpu.VMEM((stations + SUB, length // 2), F32)],
        ),
        out_shape=jax.ShapeDtypeStruct((peers, cap + SUB, length), BF16),
        compiler_params=pltpu.CompilerParams(vmem_limit_bytes=48 << 20),
        name="own",
    )(half, rows, power, send_rows)


def relay_kernel(cap, rows_ref, weight_ref, *send_refs):
    peers, length = send_refs[0].shape[0], send_refs[0].shape[2]
    tail = rows_ref.shape[0] - peers
    rows_c = cap // len(send_refs)
    digits = rows_ref[tail:, :].astype(F32).astype(jnp.int32)
    index = digits[:, :cap] * LANES + digits[:, LANES : LANES + cap]

    def store(peer, picked):
        for c, ref in enumerate(send_refs):
            ref[peer, :rows_c, :] = picked[c * rows_c : (c + 1) * rows_c]

    pick_rows(index, rows_ref[:tail, :], store)
    for peer in range(peers):
        send_refs[0][peer, rows_c:, :] = weight_ref[...]


def relay_sends(rows, weight, peers, cap, chunks):
    length = rows.shape[1]
    rows_c = cap // chunks
    sizes = [rows_c + SUB] + [rows_c] * (chunks - 1)
    return pl.pallas_call(
        partial(relay_kernel, cap),
        out_shape=[jax.ShapeDtypeStruct((peers, size, length), BF16) for size in sizes],
        compiler_params=pltpu.CompilerParams(vmem_limit_bytes=48 << 20),
        name="relay",
    )(rows, weight)


def pair_kernel(geo, first, station_ref, count_ref, place_ref, own_ref, far_ref, weight_ref, lag_ref, *refs):
    out_ref = refs[-1]
    peers, cap, joint = geo
    group = pl.program_id(0) + first
    length = own_ref.shape[-1]
    half_len = length // 2
    rows = jnp.concatenate(
        [ref[...].reshape(peers * SUB, length) for ref in (own_ref, far_ref)], axis=0
    )
    width = rows.shape[0]
    for j in range(joint):
        for i in range(SUB):
            tile = j * cap + group * SUB + i
            picks = [one_hot(place_ref[m, j, i : i + 1, :], width) for m in range(2)]
            members = jnp.dot(jnp.concatenate(picks, axis=0), rows, preferred_element_type=F32)
            a, b = members[:LANES], members[LANES:]
            re_a, im_a = a[:, :half_len], a[:, half_len:]
            re_b, im_b = b[:, :half_len], b[:, half_len:]
            scale = weight_ref[pl.ds(station_ref[tile], 1), :]
            cross = jnp.concatenate(
                [
                    ((re_a * re_b + im_a * im_b) * scale).astype(BF16),
                    ((im_a * re_b - re_a * im_b) * scale).astype(BF16),
                ],
                axis=1,
            )
            lagged = jnp.dot(cross, lag_ref[...], preferred_element_type=F32)
            slot = lax.broadcasted_iota(jnp.int32, lagged.shape, 0)
            lagged = jnp.where(slot < count_ref[tile], lagged, 0.0)
            out_ref[j, i * LANES : (i + 1) * LANES, :] = lagged[:, :LAGS]


def correlate(chunk, chunks, geo, stations_of, counts, places, own, far, weight, lag_tab, previous):
    peers, cap, joint = geo
    steps = cap // SUB // chunks
    first = chunk * steps
    length = own.shape[-1]
    stations = weight.shape[0]
    in_specs = [
        pl.BlockSpec((2, joint, SUB, LANES), lambda i, *_: (0, 0, i + first, 0)),
        pl.BlockSpec((peers, SUB, length), lambda i, *_: (0, i + first, 0)),
        pl.BlockSpec((peers, SUB, length), lambda i, *_: (0, i, 0)),
        pl.BlockSpec((stations, length // 2), lambda i, *_: (0, 0)),
        pl.BlockSpec(lag_tab.shape, lambda i, *_: (0, 0)),
    ]
    args = [places, own, far, weight, lag_tab]
    aliases = {}
    if previous is not None:
        in_specs.append(pl.BlockSpec(memory_space=pl.ANY))
        args.append(previous)
        aliases = {7: 0}
    tiles = joint * steps * SUB
    macs = tiles * LANES * length * (2 * 2 * peers * SUB + lag_tab.shape[1])
    return pl.pallas_call(
        partial(pair_kernel, geo, first),
        grid_spec=pltpu.PrefetchScalarGridSpec(
            num_scalar_prefetch=2,
            grid=(steps,),
            in_specs=in_specs,
            out_specs=pl.BlockSpec((joint, SUB * LANES, LAGS), lambda i, *_: (0, i + first, 0)),
        ),
        out_shape=jax.ShapeDtypeStruct((joint, cap * LANES, LAGS), F32),
        input_output_aliases=aliases,
        compiler_params=pltpu.CompilerParams(vmem_limit_bytes=48 << 20),
        cost_estimate=pl.CostEstimate(
            flops=2 * macs, bytes_accessed=tiles * LANES * LAGS * 4, transcendentals=0
        ),
        name="pairs",
    )(stations_of, counts, *args)


def shards(windows, rotation, source_inverse, send_rows, tile_station, tile_count, pair_rows):
    ev_dev, comps, stations, length = windows.shape
    owners = lax.axis_size("ev")
    cap = send_rows.shape[1]
    tiles_dev = tile_station.shape[0]
    joint = tiles_dev // cap
    chunks = CHUNKS
    peers = owners // 2
    share = stations // peers
    half = lax.axis_index("ev") // peers
    halves = [list(range(peers)), list(range(peers, owners))]
    across = [(i, (i + peers) % owners) for i in range(owners)]
    to_peers = partial(
        lax.all_to_all,
        axis_name="ev",
        split_axis=0,
        concat_axis=0,
        axis_index_groups=halves,
        tiled=True,
    )
    half_arg = half.astype(jnp.int32).reshape(1)

    rows, power = event_rows(
        half_arg, windows, rotation, source_inverse, send_rows, spectral_table(length)
    )
    swapped = lax.ppermute(rows, "ev", across)
    own = to_peers(own_sends(half_arg, rows, power, send_rows))
    part = jnp.sum(join_high(own[:, cap : cap + share, :]), axis=0)
    power_sum = part + lax.ppermute(part, "ev", across)
    weight = 1.0 / (power_sum / (ev_dev * owners) + epsilon)
    weight = jnp.pad(split_high(weight), ((0, SUB - share), (0, 0)))
    sends = relay_sends(swapped, weight, peers, cap, chunks)

    source = pair_rows // cap
    side = source // peers != half
    places = jnp.where(side, peers * SUB, 0) + source % peers * SUB + pair_rows % SUB
    places = places.reshape(2, joint, cap, LANES)
    lag_tab = lag_table(length, LAGS, LAGS + 1)
    geo = (peers, cap, joint)
    result = None
    for chunk, send in enumerate(sends):
        far = to_peers(send)
        if chunk == 0:
            table = join_high(far[:, cap // chunks :][:, :share]).reshape(stations, length // 2)
        result = correlate(
            chunk, chunks, geo, tile_station, tile_count, places, own, far, table, lag_tab, result
        )
    return result.reshape(tiles_dev * LANES, LAGS)


def solution(mesh):
    in_specs = (
        P(("grp", "ev"), None, None, None),
        P(("grp", "ev"), None, None),
        P(("grp", "ev"), None),
        P(("grp", "ev"), None),
        P(("grp", "ev")),
        P(("grp", "ev")),
        P(None, ("grp", "ev")),
    )
    out_specs = P(("grp", "ev"), None)
    return jax.shard_map(shards, mesh=mesh, in_specs=in_specs, out_specs=out_specs, check_vma=False)
```

time: 164 us -> 141 us (0.86)
  blocking collectives: 114 us -> 25.6 us
  waiting for transfers between devices: 3.11 us -> 52.6 us
  starting transfers between devices: 3.8 us -> 15.5 us
  local copies, waits for them, and re-layouts: 6.89 us -> 11.4 us
  Pallas kernels: 35.2 us -> 33.1 us
  other arithmetic: 0.16 us -> 2.21 us
    all_to_all x5 -> x1, blocking collectives: 114 us -> 25.6 us  [shards(): far = to_peers(send)]
    all_to_all x1 -> x2, waiting for transfers between devices: 3.11 us -> 50.8 us  [the longest x1 50.8 us: shards(): own = to_peers(own_sends(half_arg, rows, power, send_rows))]
    all_to_all x1 -> x2, starting transfers between devices: 3.8 us -> 9.97 us  [the longest x1 6.32 us: shards(): own = to_peers(own_sends(half_arg, rows, power, send_rows))]
    ppermute x0 -> x2, starting transfers between devices: none -> 5.53 us  [the longest x1 2.89 us: shards(): power_sum = part + lax.ppermute(part, 'ev', across)]
    unnamed x21 -> x31, local copies, waits for them, and re-layouts: 5.79 us -> 10.4 us
    pallas_call x4 -> x2, Pallas kernels: 28.5 us -> 25.3 us  [correlate(): pl.pallas_call(partial(pair_kernel, geo, first), grid_spec=pltpu.Prefetch...]
    ppermute x0 -> x2, waiting for transfers between devices: none -> 1.72 us  [the longest x1 1.72 us: shards(): power_sum = part + lax.ppermute(part, 'ev', across)]
    add x0 -> x1, other arithmetic: none -> 1.65 us  [join_high(): return values[..., :width].astype(F32) + values[..., width:].astype(F32)]
  transfers between devices with their start and end apart: 1 -> 4, of which waited for: 1 -> 2; matrix products, arithmetic and copies ran while one was open for 0% -> 3% of each run, Pallas kernels for 13% -> 9%
where the time goes in v2:
time: 141 us
  waiting for transfers between devices  52.6 us (37%)
  Pallas kernels  33.1 us (23%)
  blocking collectives  25.6 us (18%)
  starting transfers between devices  15.5 us (11%)
  local copies, waits for them, and re-layouts  11.4 us (8%)
  other arithmetic  2.21 us (2%)
    all_to_all x1, waiting for transfers between devices, shards(): own = to_peers(own_sends(half_arg, rows, power, send_rows))  50.8 us
    all_to_all x1, blocking collectives, shards(): far = to_peers(send)  25.6 us
    pallas_call x2, Pallas kernels, correlate(): pl.pallas_call(partial(pair_kernel, geo, first), grid_spec=pltpu.Prefetch...  25.3 us
    unnamed x31, local copies, waits for them, and re-layouts  10.4 us
    all_to_all x1, starting transfers between devices, shards(): own = to_peers(own_sends(half_arg, rows, power, send_rows))  6.32 us
    all_to_all x1, starting transfers between devices, shards(): far = to_peers(send)  3.65 us
    pallas_call x1, Pallas kernels, event_rows(): pl.pallas_call(partial(spectra_kernel, steps), grid_spec=pltpu.PrefetchSc...  3.65 us
    ppermute x1, starting transfers between devices, shards(): power_sum = part + lax.ppermute(part, 'ev', across)  2.89 us
  transfers between devices with their start and end apart: 4, of which 2 were waited for; matrix products, arithmetic and copies ran while one was open for 3% of the time, Pallas kernels for 9%

profile of v2, /device:TPU:0, one launch (start us, length us, event | category | flops | bytes accessed | tf_op | source)
XLA Modules:
  0.0 140.5 jit_solution(15205502016224286335)
XLA Ops:
  0.0 1.6 %copy-done = bf16[1024,1024]{1,0:T(8,128)(2,1)S(1)} copy-done((bf16[1024,1024]{1,0:T(8,128)(2,1)S(1)}, bf16[1024,1024]{1,0:T(8,128)(2,1)}, u32[]{:S(2)}) %copy-start) | copy-done | bytes 2097176
  1.6 0.7 copy-done.4
  2.3 0.7 copy-done.8
  3.0 0.7 copy-done.9
  3.7 3.6 %spectra.1 = (bf16[528,1024]{1,0:T(8,128)(2,1)S(1)}, f32[64,512]{1,0:T(8,128)S(1)}) custom-call(s32[1]{0:T(128)} %bitcast.half_ref, bf16[8,3,64,1024]{3,2,1,0:T(8,128)(2,1)} %win_ref.1, bf16[3,8,64]{2,1,0:T(8,128)(2,1)S(1)} %bitcast.11, bf16[8,1024]{1,0:T(8,128)(2,1)S(1)} %copy-done.8, bf16[1024,1024]{1,0:T(8,128)(2,1)S(1)} %copy-done, s32[32,64]{1,0:T(8,128)S(1)} %copy-done.4), custom_call_target="tpu_custom_call" | custom-call | tf_op jit(solution)/shard_map/spectra/pallas_call | solution.py:124
  7.4 2.8 %own.1 = bf16[16,72,1024]{2,1,0:T(8,128)(2,1)} custom-call(s32[1]{0:T(128)} %bitcast.half_ref, bf16[528,1024]{1,0:T(8,128)(2,1)S(1)} %get-tuple-element.9.rows_ref, f32[64,512]{1,0:T(8,128)S(1)} %get-tuple-element.10.power_ref, s32[32,64]{1,0:T(8,128)S(1)} %copy-done.5), custom_call_target="tpu_custom_call" | custom-call | tf_op jit(solution)/shard_map/own/pallas_call | solution.py:181
  10.2 1.0 copy-done.2
  11.2 6.3 %all-to-all-start = ((bf16[16,72,1024]{2,1,0:T(8,128)(2,1)}), bf16[16,72,1024]{2,1,0:T(8,128)(2,1)S(1)}, u32[]{:S(2)}, u32[]{:S(2)}) async-start(bf16[16,72,1024]{2,1,0:T(8,128)(2,1)} %own.1), calls=%async_computation | async-start | bytes 4718592 | tf_op jit(solution)/shard_map/all_to_all | solution.py:325
  17.5 2.6 %collective-permute-start = (bf16[528,1024]{1,0:T(8,128)(2,1)}, bf16[528,1024]{1,0:T(8,128)(2,1)S(1)}, u32[]{:S(2)}, u32[]{:S(2)}) collective-permute-start(bf16[528,1024]{1,0:T(8,128)(2,1)} %copy-done.2), channel_id=1, source_target_pairs={{0,16},{1,17},{2,18},{3,19},{4,20},{5,21},{6,22},{7,23},{8,24},{9,... | collective-permute-start | bytes 3244040 | tf_op jit(solution)/shard_map/ppermute | solution.py:324
  20.2 50.8 %all-to-all-done.own_ref = bf16[16,72,1024]{2,1,0:T(8,128)(2,1)S(1)} async-done(((bf16[16,72,1024]{2,1,0:T(8,128)(2,1)}), bf16[16,72,1024]{2,1,0:T(8,128)(2,1)S(1)}, u32[]{:S(2)}, u32[]{:S(2)}) %all-to-all-start) | async-done | bytes 2359328 | tf_op jit(solution)/shard_map/all_to_all | solution.py:325
  71.0 0.1 add_reduce_fusion
  71.1 2.9 %collective-permute-start.1 = (f32[4,512]{1,0:T(4,128)S(1)}, f32[4,512]{1,0:T(4,128)S(1)}, u32[]{:S(2)}, u32[]{:S(2)}) collective-permute-start(f32[4,512]{1,0:T(4,128)S(1)} %add_reduce_fusion), channel_id=1, source_target_pairs={{0,16},{1,17},{2,18},{3,19},{4,20},{5,21},{6,22},{7,23},{8,24},{9,... | collective-permute-start | bytes 24584 | tf_op jit(solution)/shard_map/ppermute | solution.py:327
  73.9 1.7 %collective-permute-done.1 = f32[4,512]{1,0:T(4,128)S(1)} collective-permute-done((f32[4,512]{1,0:T(4,128)S(1)}, f32[4,512]{1,0:T(4,128)S(1)}, u32[]{:S(2)}, u32[]{:S(2)}) %collective-permute-start.1) | collective-permute-done | bytes 8224 | tf_op jit(solution)/shard_map/ppermute | solution.py:327
  75.7 0.0 collective-permute-done.rows_ref
  75.7 1.4 relay.1
  77.1 0.0 copy-start.14
  77.1 0.0 copy-start.10
  77.1 0.0 copy-start.11
  77.1 25.6 %all_to_all.15.far_ref = bf16[16,40,1024]{2,1,0:T(8,128)(2,1)} all-to-all(bf16[16,40,1024]{2,1,0:T(8,128)(2,1)S(1)} %get-tuple-element.12), channel_id=1, replica_groups={{0,1,2,3,4,5,6,7,8,9,10,11,12,13,14,15},{16,17,18,19,20,21,22,23,24,25,..., dimensions={0} | all-to-all | bytes 2621440 | tf_op jit(solution)/shard_map/all_to_all | solution.py:340
  102.8 3.7 %all-to-all-start.1 = ((bf16[16,32,1024]{2,1,0:T(8,128)(2,1)}), bf16[16,32,1024]{2,1,0:T(8,128)(2,1)S(1)}, u32[]{:S(2)}, u32[]{:S(2)}) async-start(bf16[16,32,1024]{2,1,0:T(8,128)(2,1)} %copy-done.3), calls=%async_computation.1 | async-start | bytes 2097152 | tf_op jit(solution)/shard_map/all_to_all | solution.py:340
  106.5 0.5 fusion.3
  106.9 0.6 copy.13
  107.6 1.7 %convert_add_fusion = f32[16,4,512]{2,1,0:T(4,128)} fusion(bf16[16,40,1024]{2,1,0:T(8,128)(2,1)} %all_to_all.15.far_ref), kind=kLoop, calls=%fused_computation | loop fusion | flops 98304 | bytes 262144 | tf_op jit(solution)/shard_map/add | solution.py:64
  109.2 0.9 reshape.14.weight_ref
  110.2 1.3 copy-done.1
  111.5 0.8 copy-done.6
  112.3 1.0 copy-done.12
  113.4 12.6 %pairs.2.refs_0_ = f32[1,8192,255]{2,1,0:T(8,128)} custom-call(s32[64]{0:T(128)S(1)} %copy-done.10, s32[64]{0:T(128)S(1)} %copy-done.11, s32[2,1,64,128]{3,2,1,0:T(8,128)S(1)} %bitcast.9, bf16[16,72,1024]{2,1,0:T(8,128)(2,1)S(1)} %all-to-all-done.own_ref, bf16[16,40,1024]{2,1,0:T(8,128)(2,1)S(1)} %copy-done.1, f32[64,512]{1,0:T(8,128)S(1)} %reshape.14.weight_ref, ...), custom_call_target="tpu_custom_call" | custom-call | flops 6442450944 | bytes 4177920 | tf_op jit(solution)/shard_map/pairs/pallas_call | solution.py:281
  126.0 0.0 all-to-all-done.1.far_ref
  126.0 0.8 copy-done.7
  126.9 1.0 copy-done.13
  127.9 12.6 %pairs.3 = f32[1,8192,255]{2,1,0:T(8,128)} custom-call(s32[64]{0:T(128)S(1)} %copy-done.10, s32[64]{0:T(128)S(1)} %copy-done.11, s32[2,1,64,128]{3,2,1,0:T(8,128)S(1)} %bitcast.10, bf16[16,72,1024]{2,1,0:T(8,128)(2,1)S(1)} %all-to-all-done.own_ref, bf16[16,32,1024]{2,1,0:T(8,128)(2,1)S(1)} %all-to-all-done.1.far_ref, ...), custom_call_target="tpu_custom_call", output_to_operand_aliasing={{}: (7, {})} | custom-call | flops 6442450944 | bytes 4177920 | tf_op jit(solution)/shard_map/pairs/pallas_call | solution.py:281
  (19 shorter events, 0.1 us)
Async XLA Ops:
  0.0 1.6 %copy-start = (bf16[1024,1024]{1,0:T(8,128)(2,1)S(1)}, bf16[1024,1024]{1,0:T(8,128)(2,1)}, u32[]{:S(2)}) copy-start(bf16[1024,1024]{1,0:T(8,128)(2,1)} %constant.89.table_ref) | copy-start | bytes 6291460
  1.6 0.7 copy-start.4
  2.3 0.7 copy-start.8
  3.0 0.7 copy-start.9
  3.7 3.7 %copy-start.5 = (s32[32,64]{1,0:T(8,128)S(1)}, s32[32,64]{1,0:T(8,128)}, u32[]{:S(2)}) copy-start(s32[32,64]{1,0:T(8,128)} %index_ref.3) | copy-start | bytes 24580
  10.2 1.0 copy-start.2
  11.2 59.8 %all-to-all-start = ((bf16[16,72,1024]{2,1,0:T(8,128)(2,1)}), bf16[16,72,1024]{2,1,0:T(8,128)(2,1)S(1)}, u32[]{:S(2)}, u32[]{:S(2)}) async-start(bf16[16,72,1024]{2,1,0:T(8,128)(2,1)} %own.1), calls=%async_computation | async-start | bytes 4718592 | tf_op jit(solution)/shard_map/all_to_all | solution.py:325
  17.5 58.2 %collective-permute-start = (bf16[528,1024]{1,0:T(8,128)(2,1)}, bf16[528,1024]{1,0:T(8,128)(2,1)S(1)}, u32[]{:S(2)}, u32[]{:S(2)}) collective-permute-start(bf16[528,1024]{1,0:T(8,128)(2,1)} %copy-done.2), channel_id=1, source_target_pairs={{0,16},{1,17},{2,18},{3,19},{4,20},{5,21},{6,22},{7,23},{8,24},{9,... | collective-permute-start | bytes 3244040 | tf_op jit(solution)/shard_map/ppermute | solution.py:324
  71.1 4.6 %collective-permute-start.1 = (f32[4,512]{1,0:T(4,128)S(1)}, f32[4,512]{1,0:T(4,128)S(1)}, u32[]{:S(2)}, u32[]{:S(2)}) collective-permute-start(f32[4,512]{1,0:T(4,128)S(1)} %add_reduce_fusion), channel_id=1, source_target_pairs={{0,16},{1,17},{2,18},{3,19},{4,20},{5,21},{6,22},{7,23},{8,24},{9,... | collective-permute-start | bytes 24584 | tf_op jit(solution)/shard_map/ppermute | solution.py:327
  77.1 25.7 %copy-start.3 = (bf16[16,32,1024]{2,1,0:T(8,128)(2,1)}, bf16[16,32,1024]{2,1,0:T(8,128)(2,1)S(1)}, u32[]{:S(2)}) copy-start(bf16[16,32,1024]{2,1,0:T(8,128)(2,1)S(1)} %get-tuple-element.11) | copy-start | bytes 3145732
  77.1 29.3 %copy-start.14 = (s32[2,8192]{1,0:T(2,128)S(1)}, s32[2,8192]{1,0:T(2,128)}, u32[]{:S(2)}) copy-start(s32[2,8192]{1,0:T(2,128)} %param.15) | copy-start | bytes 196612
  77.1 33.0 %copy-start.10 = (s32[64]{0:T(128)S(1)}, s32[64]{0:T(128)}, u32[]{:S(2)}) copy-start(s32[64]{0:T(128)} %station_ref.3) | copy-start | bytes 772
  77.1 33.0 %copy-start.11 = (s32[64]{0:T(128)S(1)}, s32[64]{0:T(128)}, u32[]{:S(2)}) copy-start(s32[64]{0:T(128)} %count_ref.3) | copy-start | bytes 772
  102.8 23.2 %all-to-all-start.1 = ((bf16[16,32,1024]{2,1,0:T(8,128)(2,1)}), bf16[16,32,1024]{2,1,0:T(8,128)(2,1)S(1)}, u32[]{:S(2)}, u32[]{:S(2)}) async-start(bf16[16,32,1024]{2,1,0:T(8,128)(2,1)} %copy-done.3), calls=%async_computation.1 | async-start | bytes 2097152 | tf_op jit(solution)/shard_map/all_to_all | solution.py:340
  110.2 1.3 copy-start.1
  111.5 0.8 copy-start.6
  112.3 1.0 copy-start.12
  126.0 0.8 copy-start.7
  126.9 1.0 copy-start.13

commit v3 on v2

--- a/solution.py
+++ b/solution.py
@@ -9,10 +9,13 @@
 from jax.experimental.pallas import tpu as pltpu
 from jax.sharding import PartitionSpec as P
 
+
 LAGS = 255
 SUB = 8
 LANES = 128
-CHUNKS = 2
+CHUNKS = 1
+TOGETHER = 2
+VMEM = 60 << 20
 
 epsilon = 1e-06
 F32 = jnp.float32
@@ -139,7 +142,7 @@
             jax.ShapeDtypeStruct((total, length), BF16),
             jax.ShapeDtypeStruct((stations, length // 2), F32),
         ],
-        compiler_params=pltpu.CompilerParams(vmem_limit_bytes=48 << 20),
+        compiler_params=pltpu.CompilerParams(vmem_limit_bytes=VMEM),
         name="spectra",
     )(half, windows, rotation.swapaxes(0, 1), source_inverse, table, send_rows)
 
@@ -156,7 +159,7 @@
 
 
 def own_kernel(half_ref, rows_ref, power_ref, index_ref, send_ref, pad_ref):
-    peers, total, length = send_ref.shape
+    peers, _, length = send_ref.shape
     cap = index_ref.shape[1]
     stations = power_ref.shape[0]
     share = stations // peers
@@ -192,13 +195,15 @@
             scratch_shapes=[pltpu.VMEM((stations + SUB, length // 2), F32)],
         ),
         out_shape=jax.ShapeDtypeStruct((peers, cap + SUB, length), BF16),
-        compiler_params=pltpu.CompilerParams(vmem_limit_bytes=48 << 20),
+        compiler_params=pltpu.CompilerParams(vmem_limit_bytes=VMEM),
         name="own",
     )(half, rows, power, send_rows)
 
 
-def relay_kernel(cap, rows_ref, weight_ref, *send_refs):
-    peers, length = send_refs[0].shape[0], send_refs[0].shape[2]
+def relay_kernel(cap, events, rows_ref, mine_ref, other_ref, *refs):
+    *send_refs, pad_ref = refs
+    peers = send_refs[0].shape[0]
+    share = mine_ref.shape[0]
     tail = rows_ref.shape[0] - peers
     rows_c = cap // len(send_refs)
     digits = rows_ref[tail:, :].astype(F32).astype(jnp.int32)
@@ -209,68 +214,92 @@
             ref[peer, :rows_c, :] = picked[c * rows_c : (c + 1) * rows_c]
 
     pick_rows(index, rows_ref[:tail, :], store)
+    pad_ref[...] = jnp.ones_like(pad_ref)
+    pad_ref[:share, :] = 1.0 / ((mine_ref[...] + other_ref[...]) / events + epsilon)
+    weight = split_high(pad_ref[...])
     for peer in range(peers):
-        send_refs[0][peer, rows_c:, :] = weight_ref[...]
-
-
-def relay_sends(rows, weight, peers, cap, chunks):
+        send_refs[0][peer, rows_c:, :] = weight
+
+
+def relay_sends(rows, mine, other, peers, cap, chunks, events):
     length = rows.shape[1]
     rows_c = cap // chunks
     sizes = [rows_c + SUB] + [rows_c] * (chunks - 1)
     return pl.pallas_call(
-        partial(relay_kernel, cap),
+        partial(relay_kernel, cap, events),
         out_shape=[jax.ShapeDtypeStruct((peers, size, length), BF16) for size in sizes],
-        compiler_params=pltpu.CompilerParams(vmem_limit_bytes=48 << 20),
+        scratch_shapes=[pltpu.VMEM((SUB, length // 2), F32)],
+        compiler_params=pltpu.CompilerParams(vmem_limit_bytes=VMEM),
         name="relay",
-    )(rows, weight)
-
-
-def pair_kernel(geo, first, station_ref, count_ref, place_ref, own_ref, far_ref, weight_ref, lag_ref, *refs):
-    out_ref = refs[-1]
+    )(rows, mine, other)
+
+
+def pair_kernel(geo, first, station_ref, count_ref, place_ref, own_ref, far_ref, got_ref, lag_ref, *refs):
+    *_, out_ref, weight_ref = refs
     peers, cap, joint = geo
     group = pl.program_id(0) + first
     length = own_ref.shape[-1]
     half_len = length // 2
+    share = weight_ref.shape[0] // peers
+
+    @pl.when(pl.program_id(0) == 0)
+    def _():
+        for peer in range(peers):
+            weight_ref[peer * share : (peer + 1) * share, :] = join_high(got_ref[peer])[:share]
+
     rows = jnp.concatenate(
         [ref[...].reshape(peers * SUB, length) for ref in (own_ref, far_ref)], axis=0
     )
     width = rows.shape[0]
+    many = TOGETHER * LANES
     for j in range(joint):
-        for i in range(SUB):
-            tile = j * cap + group * SUB + i
-            picks = [one_hot(place_ref[m, j, i : i + 1, :], width) for m in range(2)]
+        for i in range(0, SUB, TOGETHER):
+            picks = [
+                one_hot(place_ref[m, j, i + n : i + n + 1, :], width)
+                for m in range(2)
+                for n in range(TOGETHER)
+            ]
             members = jnp.dot(jnp.concatenate(picks, axis=0), rows, preferred_element_type=F32)
-            a, b = members[:LANES], members[LANES:]
-            re_a, im_a = a[:, :half_len], a[:, half_len:]
-            re_b, im_b = b[:, :half_len], b[:, half_len:]
-            scale = weight_ref[pl.ds(station_ref[tile], 1), :]
-            cross = jnp.concatenate(
-                [
-                    ((re_a * re_b + im_a * im_b) * scale).astype(BF16),
-                    ((im_a * re_b - re_a * im_b) * scale).astype(BF16),
-                ],
-                axis=1,
-            )
+            halves = []
+            for n in range(TOGETHER):
+                a = members[n * LANES : (n + 1) * LANES]
+                b = members[many + n * LANES : many + (n + 1) * LANES]
+                re_a, im_a = a[:, :half_len], a[:, half_len:]
+                re_b, im_b = b[:, :half_len], b[:, half_len:]
+                tile = j * cap + group * SUB + i + n
+                scale = weight_ref[pl.ds(station_ref[tile], 1), :]
+                halves.append(
+                    jnp.concatenate(
+                        [
+                            ((re_a * re_b + im_a * im_b) * scale).astype(BF16),
+                            ((im_a * re_b - re_a * im_b) * scale).astype(BF16),
+                        ],
+                        axis=1,
+                    )
+                )
+            cross = jnp.concatenate(halves, axis=0)
             lagged = jnp.dot(cross, lag_ref[...], preferred_element_type=F32)
-            slot = lax.broadcasted_iota(jnp.int32, lagged.shape, 0)
-            lagged = jnp.where(slot < count_ref[tile], lagged, 0.0)
-            out_ref[j, i * LANES : (i + 1) * LANES, :] = lagged[:, :LAGS]
-
-
-def correlate(chunk, chunks, geo, stations_of, counts, places, own, far, weight, lag_tab, previous):
+            for n in range(TOGETHER):
+                tile = j * cap + group * SUB + i + n
+                piece = lagged[n * LANES : (n + 1) * LANES]
+                slot = lax.broadcasted_iota(jnp.int32, piece.shape, 0)
+                piece = jnp.where(slot < count_ref[tile], piece, 0.0)
+                out_ref[j, (i + n) * LANES : (i + n + 1) * LANES, :] = piece[:, :LAGS]
+
+
+def correlate(chunk, chunks, geo, stations, stations_of, counts, places, own, far, got, lag_tab, previous):
     peers, cap, joint = geo
     steps = cap // SUB // chunks
     first = chunk * steps
     length = own.shape[-1]
-    stations = weight.shape[0]
     in_specs = [
         pl.BlockSpec((2, joint, SUB, LANES), lambda i, *_: (0, 0, i + first, 0)),
         pl.BlockSpec((peers, SUB, length), lambda i, *_: (0, i + first, 0)),
         pl.BlockSpec((peers, SUB, length), lambda i, *_: (0, i, 0)),
-        pl.BlockSpec((stations, length // 2), lambda i, *_: (0, 0)),
+        pl.BlockSpec((peers, SUB, length), lambda i, *_: (0, steps, 0)),
         pl.BlockSpec(lag_tab.shape, lambda i, *_: (0, 0)),
     ]
-    args = [places, own, far, weight, lag_tab]
+    args = [places, own, far, got, lag_tab]
     aliases = {}
     if previous is not None:
         in_specs.append(pl.BlockSpec(memory_space=pl.ANY))
@@ -285,10 +314,11 @@
             grid=(steps,),
             in_specs=in_specs,
             out_specs=pl.BlockSpec((joint, SUB * LANES, LAGS), lambda i, *_: (0, i + first, 0)),
+            scratch_shapes=[pltpu.VMEM((stations, length // 2), F32)],
         ),
         out_shape=jax.ShapeDtypeStruct((joint, cap * LANES, LAGS), F32),
         input_output_aliases=aliases,
-        compiler_params=pltpu.CompilerParams(vmem_limit_bytes=48 << 20),
+        compiler_params=pltpu.CompilerParams(vmem_limit_bytes=VMEM),
         cost_estimate=pl.CostEstimate(
             flops=2 * macs, bytes_accessed=tiles * LANES * LAGS * 4, transcendentals=0
         ),
@@ -297,7 +327,7 @@
 
 
 def shards(windows, rotation, source_inverse, send_rows, tile_station, tile_count, pair_rows):
-    ev_dev, comps, stations, length = windows.shape
+    ev_dev, _, stations, length = windows.shape
     owners = lax.axis_size("ev")
     cap = send_rows.shape[1]
     tiles_dev = tile_station.shape[0]
@@ -322,12 +352,11 @@
         half_arg, windows, rotation, source_inverse, send_rows, spectral_table(length)
     )
     swapped = lax.ppermute(rows, "ev", across)
-    own = to_peers(own_sends(half_arg, rows, power, send_rows))
-    part = jnp.sum(join_high(own[:, cap : cap + share, :]), axis=0)
-    power_sum = part + lax.ppermute(part, "ev", across)
-    weight = 1.0 / (power_sum / (ev_dev * owners) + epsilon)
-    weight = jnp.pad(split_high(weight), ((0, SUB - share), (0, 0)))
-    sends = relay_sends(swapped, weight, peers, cap, chunks)
+    sends = own_sends(half_arg, rows, power, send_rows)
+    own = to_peers(sends)
+    mine = jnp.sum(join_high(own[:, cap : cap + share, :]), axis=0)
+    other = lax.ppermute(mine, "ev", across)
+    sends = relay_sends(swapped, mine, other, peers, cap, chunks, ev_dev * owners)
 
     source = pair_rows // cap
     side = source // peers != half
@@ -339,9 +368,9 @@
     for chunk, send in enumerate(sends):
         far = to_peers(send)
         if chunk == 0:
-            table = join_high(far[:, cap // chunks :][:, :share]).reshape(stations, length // 2)
+            got = far
         result = correlate(
-            chunk, chunks, geo, tile_station, tile_count, places, own, far, table, lag_tab, result
+            chunk, chunks, geo, stations, tile_station, tile_count, places, own, far, got, lag_tab, result
         )
     return result.reshape(tiles_dev * LANES, LAGS)
 

time: 141 us -> 142 us (level)
  waiting for transfers between devices: 52.6 us -> 83.7 us
  blocking collectives: 25.6 us -> 0 us
  local copies, waits for them, and re-layouts: 11.4 us -> 1.23 us
  starting transfers between devices: 15.5 us -> 19 us
  Pallas kernels: 33.1 us -> 36.1 us
  other arithmetic: 2.21 us -> 0.54 us
    all_to_all x1, waiting for transfers between devices: 0.01 us -> 31.3 us  [shards(): far = to_peers(send)]
    all_to_all x1 -> x0, blocking collectives: 25.6 us -> none  [shards(): far = to_peers(send)]
    unnamed x31 -> x11, local copies, waits for them, and re-layouts: 10.4 us -> 1.23 us
    all_to_all x1, starting transfers between devices: 3.65 us -> 6.91 us  [shards(): far = to_peers(send)]
    pallas_call x1, Pallas kernels: 1.38 us -> 4.05 us  [relay_sends(): pl.pallas_call(partial(relay_kernel, cap, events), out_shape=[jax.ShapeDt...]
    pallas_call x2 -> x1, Pallas kernels: 25.3 us -> 22.6 us  [correlate(): pl.pallas_call(partial(pair_kernel, geo, first), grid_spec=pltpu.Prefetch...]
    pallas_call x1, Pallas kernels: 3.65 us -> 5.33 us  [event_rows(): pl.pallas_call(partial(spectra_kernel, steps), grid_spec=pltpu.PrefetchSc...]
    add x1 -> x0, other arithmetic: 1.65 us -> none  [join_high(): return values[..., :width].astype(F32) + values[..., width:].astype(F32)]
  transfers between devices with their start and end apart: 4 -> 4, of which waited for: 2 -> 3; matrix products, arithmetic and copies ran while one was open for 3% -> 1% of each run, Pallas kernels for 9% -> 0%
where the time goes in v3:
time: 142 us; the launch traced here: 141 us
  waiting for transfers between devices  83.7 us (59%)
  Pallas kernels  36.1 us (25%)
  starting transfers between devices  19 us (13%)
    all_to_all x1, waiting for transfers between devices, shards(): own = to_peers(sends)  50.8 us
    all_to_all x1, waiting for transfers between devices, shards(): far = to_peers(send)  31.3 us
    pallas_call x1, Pallas kernels, correlate(): pl.pallas_call(partial(pair_kernel, geo, first), grid_spec=pltpu.Prefetch...  22.6 us
    all_to_all x1, starting transfers between devices, shards(): far = to_peers(send)  6.91 us
    all_to_all x1, starting transfers between devices, shards(): own = to_peers(sends)  6.44 us
    pallas_call x1, Pallas kernels, event_rows(): pl.pallas_call(partial(spectra_kernel, steps), grid_spec=pltpu.PrefetchSc...  5.33 us
    pallas_call x1, Pallas kernels, own_sends(): pl.pallas_call(own_kernel, grid_spec=pltpu.PrefetchScalarGridSpec(num_sca...  4.09 us
    pallas_call x1, Pallas kernels, relay_sends(): pl.pallas_call(partial(relay_kernel, cap, events), out_shape=[jax.ShapeDt...  4.05 us
  transfers between devices with their start and end apart: 4, of which 3 were waited for; matrix products, arithmetic and copies ran while one was open for 1% of the time, Pallas kernels for 0%

profile of v3, /device:TPU:0, one launch (start us, length us, event | category | flops | bytes accessed | tf_op | source)
XLA Modules:
  0.0 140.6 jit_solution(4317064924679793423)
XLA Ops:
  0.0 5.3 %spectra.1 = (bf16[528,1024]{1,0:T(8,128)(2,1)}, f32[64,512]{1,0:T(8,128)}) custom-call(s32[1]{0:T(128)} %bitcast.half_ref, bf16[8,3,64,1024]{3,2,1,0:T(8,128)(2,1)} %win_ref.1, bf16[3,8,64]{2,1,0:T(8,128)(2,1)} %bitcast.10, bf16[8,1024]{1,0:T(8,128)(2,1)} %inv_ref.1, bf16[1024,1024]{1,0:T(8,128)(2,1)} %constant.78.table_ref, s32[32,64]{1,0:T(8,128)} %index_ref.3), custom_call_target="tpu_custom_call" | custom-call | tf_op jit(solution)/shard_map/spectra/pallas_call | solution.py:127
  5.3 4.1 %own.1 = bf16[16,72,1024]{2,1,0:T(8,128)(2,1)} custom-call(s32[1]{0:T(128)} %bitcast.half_ref, bf16[528,1024]{1,0:T(8,128)(2,1)} %get-tuple-element.7.rows_ref, f32[64,512]{1,0:T(8,128)} %get-tuple-element.8.power_ref, s32[32,64]{1,0:T(8,128)} %index_ref.3), custom_call_target="tpu_custom_call" | custom-call | tf_op jit(solution)/shard_map/own/pallas_call | solution.py:184
  9.4 0.0 copy-start.1
  9.4 6.4 %all-to-all-start = ((bf16[16,72,1024]{2,1,0:T(8,128)(2,1)}), bf16[16,72,1024]{2,1,0:T(8,128)(2,1)S(1)}, u32[]{:S(2)}, u32[]{:S(2)}) async-start(bf16[16,72,1024]{2,1,0:T(8,128)(2,1)} %own.1), calls=%async_computation | async-start | bytes 4718592 | tf_op jit(solution)/shard_map/all_to_all | solution.py:356
  15.9 0.0 copy-done.1
  15.9 2.7 %collective-permute-start = (bf16[528,1024]{1,0:T(8,128)(2,1)S(1)}, bf16[528,1024]{1,0:T(8,128)(2,1)}, u32[]{:S(2)}, u32[]{:S(2)}) collective-permute-start(bf16[528,1024]{1,0:T(8,128)(2,1)S(1)} %copy-done.1), channel_id=1, source_target_pairs={{0,16},{1,17},{2,18},{3,19},{4,20},{5,21},{6,22},{7,23},{8,24},{9,... | collective-permute-start | bytes 3244040 | tf_op jit(solution)/shard_map/ppermute | solution.py:354
  18.5 50.8 %all-to-all-done.own_ref = bf16[16,72,1024]{2,1,0:T(8,128)(2,1)S(1)} async-done(((bf16[16,72,1024]{2,1,0:T(8,128)(2,1)}), bf16[16,72,1024]{2,1,0:T(8,128)(2,1)S(1)}, u32[]{:S(2)}, u32[]{:S(2)}) %all-to-all-start) | async-done | bytes 2359328 | tf_op jit(solution)/shard_map/all_to_all | solution.py:356
  69.3 0.0 copy-start
  69.3 0.1 add_reduce_fusion.mine_ref
  69.4 0.0 copy-start.3
  69.4 3.0 %collective-permute-start.1 = (f32[4,512]{1,0:T(4,128)S(1)}, f32[4,512]{1,0:T(4,128)S(1)}, u32[]{:S(2)}, u32[]{:S(2)}) collective-permute-start(f32[4,512]{1,0:T(4,128)S(1)} %add_reduce_fusion.mine_ref), channel_id=1, source_target_pairs={{0,16},{1,17},{2,18},{3,19},{4,20},{5,21},{6,22},{7,23},{8,24},{9,... | collective-permute-start | bytes 24584 | tf_op jit(solution)/shard_map/ppermute | solution.py:358
  72.3 0.0 collective-permute-done.rows_ref
  72.3 1.6 %collective-permute-done.1.other_ref = f32[4,512]{1,0:T(4,128)S(1)} collective-permute-done((f32[4,512]{1,0:T(4,128)S(1)}, f32[4,512]{1,0:T(4,128)S(1)}, u32[]{:S(2)}, u32[]{:S(2)}) %collective-permute-start.1) | collective-permute-done | bytes 8224 | tf_op jit(solution)/shard_map/ppermute | solution.py:358
  74.0 0.0 copy-done.3
  74.0 0.0 copy-start.4
  74.0 0.6 copy-done.4
  74.6 4.0 %relay.1 = bf16[16,72,1024]{2,1,0:T(8,128)(2,1)} custom-call(bf16[528,1024]{1,0:T(8,128)(2,1)} %collective-permute-done.rows_ref, f32[4,512]{1,0:T(4,128)} %copy-done.3, f32[4,512]{1,0:T(4,128)} %copy-done.4), custom_call_target="tpu_custom_call" | custom-call | tf_op jit(solution)/shard_map/relay/pallas_call | solution.py:228
  78.6 0.0 copy-start.2
  78.6 0.0 copy-done
  78.6 6.9 %all-to-all-start.1 = ((bf16[16,72,1024]{2,1,0:T(8,128)(2,1)}), bf16[16,72,1024]{2,1,0:T(8,128)(2,1)}, u32[]{:S(2)}, u32[]{:S(2)}) async-start(bf16[16,72,1024]{2,1,0:T(8,128)(2,1)} %relay.1), calls=%async_computation.1 | async-start | bytes 4718592 | tf_op jit(solution)/shard_map/all_to_all | solution.py:369
  85.5 0.0 copy-done.2
  85.6 0.5 fusion.3
  86.0 0.6 copy.12
  86.7 31.3 %all-to-all-done.1.far_ref.got_ref = bf16[16,72,1024]{2,1,0:T(8,128)(2,1)} async-done(((bf16[16,72,1024]{2,1,0:T(8,128)(2,1)}), bf16[16,72,1024]{2,1,0:T(8,128)(2,1)}, u32[]{:S(2)}, u32[]{:S(2)}) %all-to-all-start.1) | async-done | bytes 2359328 | tf_op jit(solution)/shard_map/all_to_all | solution.py:369
  118.0 22.6 %pairs.1 = f32[1,8192,255]{2,1,0:T(8,128)} custom-call(s32[64]{0:T(128)} %station_ref.1, s32[64]{0:T(128)} %count_ref.1, s32[2,1,64,128]{3,2,1,0:T(8,128)} %bitcast.9, bf16[16,72,1024]{2,1,0:T(8,128)(2,1)} %copy-done, bf16[16,72,1024]{2,1,0:T(8,128)(2,1)} %all-to-all-done.1.far_ref.got_ref, bf16[16,72,1024]{2,1,0:T(8,128)(2,1)} %all-to-all-done.1.far_ref.got_ref, ...), custom_call_target="tpu_custom_call" | custom-call | flops 12884901888 | bytes 8355840 | tf_op jit(solution)/shard_map/pairs/pallas_call | solution.py:310
Async XLA Ops:
  9.4 6.5 %copy-start.1 = (bf16[528,1024]{1,0:T(8,128)(2,1)S(1)}, bf16[528,1024]{1,0:T(8,128)(2,1)}, u32[]{:S(2)}) copy-start(bf16[528,1024]{1,0:T(8,128)(2,1)} %get-tuple-element.7.rows_ref) | copy-start | bytes 3244036
  9.4 59.9 %all-to-all-start = ((bf16[16,72,1024]{2,1,0:T(8,128)(2,1)}), bf16[16,72,1024]{2,1,0:T(8,128)(2,1)S(1)}, u32[]{:S(2)}, u32[]{:S(2)}) async-start(bf16[16,72,1024]{2,1,0:T(8,128)(2,1)} %own.1), calls=%async_computation | async-start | bytes 4718592 | tf_op jit(solution)/shard_map/all_to_all | solution.py:356
  15.9 56.4 %collective-permute-start = (bf16[528,1024]{1,0:T(8,128)(2,1)S(1)}, bf16[528,1024]{1,0:T(8,128)(2,1)}, u32[]{:S(2)}, u32[]{:S(2)}) collective-permute-start(bf16[528,1024]{1,0:T(8,128)(2,1)S(1)} %copy-done.1), channel_id=1, source_target_pairs={{0,16},{1,17},{2,18},{3,19},{4,20},{5,21},{6,22},{7,23},{8,24},{9,... | collective-permute-start | bytes 3244040 | tf_op jit(solution)/shard_map/ppermute | solution.py:354
  69.3 9.3 %copy-start = (bf16[16,72,1024]{2,1,0:T(8,128)(2,1)}, bf16[16,72,1024]{2,1,0:T(8,128)(2,1)S(1)}, u32[]{:S(2)}) copy-start(bf16[16,72,1024]{2,1,0:T(8,128)(2,1)S(1)} %all-to-all-done.own_ref) | copy-start | bytes 7077892
  69.4 4.6 %copy-start.3 = (f32[4,512]{1,0:T(4,128)}, f32[4,512]{1,0:T(4,128)S(1)}, u32[]{:S(2)}) copy-start(f32[4,512]{1,0:T(4,128)S(1)} %add_reduce_fusion.mine_ref) | copy-start | bytes 24580
  69.4 4.6 %collective-permute-start.1 = (f32[4,512]{1,0:T(4,128)S(1)}, f32[4,512]{1,0:T(4,128)S(1)}, u32[]{:S(2)}, u32[]{:S(2)}) collective-permute-start(f32[4,512]{1,0:T(4,128)S(1)} %add_reduce_fusion.mine_ref), channel_id=1, source_target_pairs={{0,16},{1,17},{2,18},{3,19},{4,20},{5,21},{6,22},{7,23},{8,24},{9,... | collective-permute-start | bytes 24584 | tf_op jit(solution)/shard_map/ppermute | solution.py:358
  74.0 0.6 copy-start.4
  78.6 6.9 %copy-start.2 = (s32[2,8192]{1,0:T(2,128)S(1)}, s32[2,8192]{1,0:T(2,128)}, u32[]{:S(2)}) copy-start(s32[2,8192]{1,0:T(2,128)} %param.15) | copy-start | bytes 196612
  78.6 39.4 %all-to-all-start.1 = ((bf16[16,72,1024]{2,1,0:T(8,128)(2,1)}), bf16[16,72,1024]{2,1,0:T(8,128)(2,1)}, u32[]{:S(2)}, u32[]{:S(2)}) async-start(bf16[16,72,1024]{2,1,0:T(8,128)(2,1)} %relay.1), calls=%async_computation.1 | async-start | bytes 4718592 | tf_op jit(solution)/shard_map/all_to_all | solution.py:369

commit v4 on v3

--- a/solution.py
+++ b/solution.py
@@ -13,9 +13,10 @@
 LAGS = 255
 SUB = 8
 LANES = 128
-CHUNKS = 1
+SPLIT = (6, 2)
 TOGETHER = 2
 VMEM = 60 << 20
+SMALL = 20 << 20
 
 epsilon = 1e-06
 F32 = jnp.float32
@@ -54,17 +55,6 @@
         jnp.where(down == lane + LANES * j, 1.0, 0.0).astype(BF16) for j in range(width // LANES)
     ]
     return jnp.concatenate(parts, axis=1)
-
-
-def split_high(values):
-    high = values.astype(BF16)
-    rest = (values - high.astype(F32)).astype(BF16)
-    return jnp.concatenate([high, rest], axis=-1)
-
-
-def join_high(values):
-    width = values.shape[-1] // 2
-    return values[..., :width].astype(F32) + values[..., width:].astype(F32)
 
 
 def spectra_kernel(steps, half_ref, win_ref, rot_ref, inv_ref, table_ref, index_ref, rows_ref, power_ref):
@@ -158,94 +148,67 @@
             store(first + j, picked[j * cap : (j + 1) * cap])
 
 
-def own_kernel(half_ref, rows_ref, power_ref, index_ref, send_ref, pad_ref):
-    peers, _, length = send_ref.shape
-    cap = index_ref.shape[1]
-    stations = power_ref.shape[0]
-    share = stations // peers
+def own_kernel(half_ref, rows_ref, index_ref, send_ref):
+    peers = send_ref.shape[0]
     mine = pl.multiple_of(half_ref[0] * peers, peers)
 
     def store(peer, picked):
-        send_ref[peer, :cap, :] = picked
+        send_ref[peer] = picked
 
     pick_rows(index_ref[pl.ds(mine, peers), :], rows_ref[...], store)
-    pad_ref[:stations, :] = power_ref[...]
-    pad_ref[stations:, :] = jnp.zeros((SUB, length // 2), F32)
-    for peer in range(peers):
-        send_ref[peer, cap:, :] = split_high(pad_ref[peer * share : peer * share + SUB, :])
-
-
-def own_sends(half, rows, power, send_rows):
+
+
+def own_sends(half, rows, send_rows):
     owners, cap = send_rows.shape
     peers = owners // 2
     length = rows.shape[1]
-    stations = power.shape[0]
     whole = lambda *shape: pl.BlockSpec(shape, lambda i, *_: (0,) * len(shape))
     return pl.pallas_call(
         own_kernel,
         grid_spec=pltpu.PrefetchScalarGridSpec(
             num_scalar_prefetch=1,
             grid=(1,),
-            in_specs=[
-                whole(rows.shape[0] - peers, length),
-                whole(*power.shape),
-                whole(owners, cap),
-            ],
-            out_specs=whole(peers, cap + SUB, length),
-            scratch_shapes=[pltpu.VMEM((stations + SUB, length // 2), F32)],
+            in_specs=[whole(rows.shape[0] - peers, length), whole(owners, cap)],
+            out_specs=whole(peers, cap, length),
         ),
-        out_shape=jax.ShapeDtypeStruct((peers, cap + SUB, length), BF16),
-        compiler_params=pltpu.CompilerParams(vmem_limit_bytes=VMEM),
+        out_shape=jax.ShapeDtypeStruct((peers, cap, length), BF16),
+        compiler_params=pltpu.CompilerParams(vmem_limit_bytes=SMALL),
         name="own",
-    )(half, rows, power, send_rows)
-
-
-def relay_kernel(cap, events, rows_ref, mine_ref, other_ref, *refs):
-    *send_refs, pad_ref = refs
+    )(half, rows, send_rows)
+
+
+def relay_kernel(rows_ref, *send_refs):
     peers = send_refs[0].shape[0]
-    share = mine_ref.shape[0]
+    cap = sum(ref.shape[1] for ref in send_refs)
     tail = rows_ref.shape[0] - peers
-    rows_c = cap // len(send_refs)
     digits = rows_ref[tail:, :].astype(F32).astype(jnp.int32)
     index = digits[:, :cap] * LANES + digits[:, LANES : LANES + cap]
 
     def store(peer, picked):
-        for c, ref in enumerate(send_refs):
-            ref[peer, :rows_c, :] = picked[c * rows_c : (c + 1) * rows_c]
+        start = 0
+        for ref in send_refs:
+            ref[peer] = picked[start : start + ref.shape[1]]
+            start += ref.shape[1]
 
     pick_rows(index, rows_ref[:tail, :], store)
-    pad_ref[...] = jnp.ones_like(pad_ref)
-    pad_ref[:share, :] = 1.0 / ((mine_ref[...] + other_ref[...]) / events + epsilon)
-    weight = split_high(pad_ref[...])
-    for peer in range(peers):
-        send_refs[0][peer, rows_c:, :] = weight
-
-
-def relay_sends(rows, mine, other, peers, cap, chunks, events):
+
+
+def relay_sends(rows, peers, sizes):
     length = rows.shape[1]
-    rows_c = cap // chunks
-    sizes = [rows_c + SUB] + [rows_c] * (chunks - 1)
     return pl.pallas_call(
-        partial(relay_kernel, cap, events),
-        out_shape=[jax.ShapeDtypeStruct((peers, size, length), BF16) for size in sizes],
-        scratch_shapes=[pltpu.VMEM((SUB, length // 2), F32)],
-        compiler_params=pltpu.CompilerParams(vmem_limit_bytes=VMEM),
+        relay_kernel,
+        out_shape=[jax.ShapeDtypeStruct((peers, size * SUB, length), BF16) for size in sizes],
+        compiler_params=pltpu.CompilerParams(vmem_limit_bytes=SMALL),
         name="relay",
-    )(rows, mine, other)
-
-
-def pair_kernel(geo, first, station_ref, count_ref, place_ref, own_ref, far_ref, got_ref, lag_ref, *refs):
-    *_, out_ref, weight_ref = refs
+    )(rows)
+
+
+def pair_kernel(geo, first, station_ref, count_ref, place_ref, own_ref, far_ref, weight_ref, lag_ref, *refs):
+    out_ref = refs[-1]
     peers, cap, joint = geo
     group = pl.program_id(0) + first
     length = own_ref.shape[-1]
     half_len = length // 2
-    share = weight_ref.shape[0] // peers
-
-    @pl.when(pl.program_id(0) == 0)
-    def _():
-        for peer in range(peers):
-            weight_ref[peer * share : (peer + 1) * share, :] = join_high(got_ref[peer])[:share]
 
     rows = jnp.concatenate(
         [ref[...].reshape(peers * SUB, length) for ref in (own_ref, far_ref)], axis=0
@@ -287,19 +250,17 @@
                 out_ref[j, (i + n) * LANES : (i + n + 1) * LANES, :] = piece[:, :LAGS]
 
 
-def correlate(chunk, chunks, geo, stations, stations_of, counts, places, own, far, got, lag_tab, previous):
+def correlate(first, steps, geo, stations_of, counts, places, own, far, weight, lag_tab, previous):
     peers, cap, joint = geo
-    steps = cap // SUB // chunks
-    first = chunk * steps
     length = own.shape[-1]
     in_specs = [
         pl.BlockSpec((2, joint, SUB, LANES), lambda i, *_: (0, 0, i + first, 0)),
         pl.BlockSpec((peers, SUB, length), lambda i, *_: (0, i + first, 0)),
         pl.BlockSpec((peers, SUB, length), lambda i, *_: (0, i, 0)),
-        pl.BlockSpec((peers, SUB, length), lambda i, *_: (0, steps, 0)),
+        pl.BlockSpec(weight.shape, lambda i, *_: (0, 0)),
         pl.BlockSpec(lag_tab.shape, lambda i, *_: (0, 0)),
     ]
-    args = [places, own, far, got, lag_tab]
+    args = [places, own, far, weight, lag_tab]
     aliases = {}
     if previous is not None:
         in_specs.append(pl.BlockSpec(memory_space=pl.ANY))
@@ -314,7 +275,6 @@
             grid=(steps,),
             in_specs=in_specs,
             out_specs=pl.BlockSpec((joint, SUB * LANES, LAGS), lambda i, *_: (0, i + first, 0)),
-            scratch_shapes=[pltpu.VMEM((stations, length // 2), F32)],
         ),
         out_shape=jax.ShapeDtypeStruct((joint, cap * LANES, LAGS), F32),
         input_output_aliases=aliases,
@@ -326,15 +286,23 @@
     )(stations_of, counts, *args)
 
 
+def power_total(power, owners):
+    if owners & (owners - 1):
+        return lax.psum(power, "ev")
+    step = 1
+    while step < owners:
+        power += lax.ppermute(power, "ev", [(i, i ^ step) for i in range(owners)])
+        step *= 2
+    return power
+
+
 def shards(windows, rotation, source_inverse, send_rows, tile_station, tile_count, pair_rows):
-    ev_dev, _, stations, length = windows.shape
+    ev_dev, _, _, length = windows.shape
     owners = lax.axis_size("ev")
     cap = send_rows.shape[1]
     tiles_dev = tile_station.shape[0]
     joint = tiles_dev // cap
-    chunks = CHUNKS
     peers = owners // 2
-    share = stations // peers
     half = lax.axis_index("ev") // peers
     halves = [list(range(peers)), list(range(peers, owners))]
     across = [(i, (i + peers) % owners) for i in range(owners)]
@@ -352,11 +320,13 @@
         half_arg, windows, rotation, source_inverse, send_rows, spectral_table(length)
     )
     swapped = lax.ppermute(rows, "ev", across)
-    sends = own_sends(half_arg, rows, power, send_rows)
+    sends = own_sends(half_arg, rows, send_rows)
     own = to_peers(sends)
-    mine = jnp.sum(join_high(own[:, cap : cap + share, :]), axis=0)
-    other = lax.ppermute(mine, "ev", across)
-    sends = relay_sends(swapped, mine, other, peers, cap, chunks, ev_dev * owners)
+    weight = 1.0 / (power_total(power, owners) / (ev_dev * owners) + epsilon)
+    groups = cap // SUB
+    parts = [groups * part // sum(SPLIT) for part in SPLIT[:-1]]
+    sizes = parts + [groups - sum(parts)]
+    sends = relay_sends(swapped, peers, sizes)
 
     source = pair_rows // cap
     side = source // peers != half
@@ -365,13 +335,13 @@
     lag_tab = lag_table(length, LAGS, LAGS + 1)
     geo = (peers, cap, joint)
     result = None
-    for chunk, send in enumerate(sends):
+    first = 0
+    for steps, send in zip(sizes, sends):
         far = to_peers(send)
-        if chunk == 0:
-            got = far
         result = correlate(
-            chunk, chunks, geo, stations, tile_station, tile_count, places, own, far, got, lag_tab, result
+            first, steps, geo, tile_station, tile_count, places, own, far, weight, lag_tab, result
         )
+        first += steps
     return result.reshape(tiles_dev * LANES, LAGS)
 
 

time: 142 us -> 147 us (1.035)
  starting transfers between devices: 19 us -> 25.9 us
  waiting for transfers between devices: 83.7 us -> 79.8 us
    all_to_all x1, waiting for transfers between devices: 50.8 us -> 0.01 us  [shards(): own = to_peers(sends)]
    ppermute x1, waiting for transfers between devices: 0.01 us -> 47.6 us  [shards(): swapped = lax.ppermute(rows, 'ev', across)]
    all_to_all x1 -> x2, waiting for transfers between devices: 31.3 us -> 0.01 us  [shards(): far = to_peers(send)]
    ppermute x1 -> x5, waiting for transfers between devices: 1.64 us -> 32.2 us  [power_total(): power += lax.ppermute(power, 'ev', [(i, i ^ step) for i in range(owners)])]
    all_to_all x1 -> x2, starting transfers between devices: 6.91 us -> 13.1 us  [shards(): far = to_peers(send)]
    pallas_call x1 -> x2, Pallas kernels: 22.6 us -> 25.6 us  [correlate(): pl.pallas_call(partial(pair_kernel, geo, first), grid_spec=pltpu.Prefetch...]
    ppermute x1 -> x5, starting transfers between devices: 2.97 us -> 3.74 us  [power_total(): power += lax.ppermute(power, 'ev', [(i, i ^ step) for i in range(owners)])]
  transfers between devices with their start and end apart: 4 -> 9, of which waited for: 3 -> 6; matrix products, arithmetic and copies ran while one was open for 1% -> 1% of each run, Pallas kernels for 0% -> 14%
where the time goes in v4:
time: 147 us; the launch traced here: 146 us
  waiting for transfers between devices  79.8 us (54%)
  Pallas kernels  36.5 us (25%)
  starting transfers between devices  25.9 us (18%)
  local copies, waits for them, and re-layouts  2.69 us (2%)
    ppermute x1, waiting for transfers between devices, shards(): swapped = lax.ppermute(rows, 'ev', across)  47.6 us
    ppermute x5, waiting for transfers between devices, power_total(): power += lax.ppermute(power, 'ev', [(i, i ^ step) for i in range(owners)])  32.2 us
    pallas_call x2, Pallas kernels, correlate(): pl.pallas_call(partial(pair_kernel, geo, first), grid_spec=pltpu.Prefetch...  25.6 us
    all_to_all x2, starting transfers between devices, shards(): far = to_peers(send)  13.1 us
    all_to_all x1, starting transfers between devices, shards(): own = to_peers(sends)  6.45 us
    pallas_call x1, Pallas kernels, event_rows(): pl.pallas_call(partial(spectra_kernel, steps), grid_spec=pltpu.PrefetchSc...  5.47 us
    ppermute x5, starting transfers between devices, power_total(): power += lax.ppermute(power, 'ev', [(i, i ^ step) for i in range(owners)])  3.74 us
  transfers between devices with their start and end apart: 9, of which 6 were waited for; matrix products, arithmetic and copies ran while one was open for 1% of the time, Pallas kernels for 14%

profile of v4, /device:TPU:0, one launch (start us, length us, event | category | flops | bytes accessed | tf_op | source)
XLA Modules:
  0.0 146.3 jit_solution(17981007404772336230)
XLA Ops:
  0.0 5.5 %spectra.1 = (bf16[528,1024]{1,0:T(8,128)(2,1)}, f32[64,512]{1,0:T(8,128)}) custom-call(s32[1]{0:T(128)} %bitcast.half_ref, bf16[8,3,64,1024]{3,2,1,0:T(8,128)(2,1)} %win_ref.1, bf16[3,8,64]{2,1,0:T(8,128)(2,1)} %bitcast.11, bf16[8,1024]{1,0:T(8,128)(2,1)} %inv_ref.1, bf16[1024,1024]{1,0:T(8,128)(2,1)} %constant.83.table_ref, s32[32,64]{1,0:T(8,128)} %index_ref.3), custom_call_target="tpu_custom_call" | custom-call | tf_op jit(solution)/shard_map/spectra/pallas_call | solution.py:117
  5.5 0.0 copy-done.2
  5.5 1.2 copy-done
  6.7 2.7 %own.1 = bf16[16,64,1024]{2,1,0:T(8,128)(2,1)} custom-call(s32[1]{0:T(128)} %bitcast.half_ref, bf16[528,1024]{1,0:T(8,128)(2,1)S(1)} %copy-done, s32[32,64]{1,0:T(8,128)S(1)} %copy-done.2), custom_call_target="tpu_custom_call" | custom-call | tf_op jit(solution)/shard_map/own/pallas_call | solution.py:166
  9.4 6.4 %all-to-all-start = ((bf16[16,64,1024]{2,1,0:T(8,128)(2,1)}), bf16[16,64,1024]{2,1,0:T(8,128)(2,1)S(1)}, u32[]{:S(2)}, u32[]{:S(2)}) async-start(bf16[16,64,1024]{2,1,0:T(8,128)(2,1)} %own.1), calls=%async_computation | async-start | bytes 4194304 | tf_op jit(solution)/shard_map/all_to_all | solution.py:324
  15.9 0.0 copy-done.1
  15.9 0.0 copy-start.5
  15.9 2.7 %collective-permute-start = (bf16[528,1024]{1,0:T(8,128)(2,1)S(1)}, bf16[528,1024]{1,0:T(8,128)(2,1)S(1)}, u32[]{:S(2)}, u32[]{:S(2)}) collective-permute-start(bf16[528,1024]{1,0:T(8,128)(2,1)S(1)} %copy-done.1), channel_id=1, source_target_pairs={{0,16},{1,17},{2,18},{3,19},{4,20},{5,21},{6,22},{7,23},{8,24},{9,... | collective-permute-start | bytes 3244040 | tf_op jit(solution)/shard_map/ppermute | solution.py:322
  18.6 47.6 %collective-permute-done.rows_ref = bf16[528,1024]{1,0:T(8,128)(2,1)S(1)} collective-permute-done((bf16[528,1024]{1,0:T(8,128)(2,1)S(1)}, bf16[528,1024]{1,0:T(8,128)(2,1)S(1)}, u32[]{:S(2)}, u32[]{:S(2)}) %collective-permute-start) | collective-permute-done | bytes 1081376 | tf_op jit(solution)/shard_map/ppermute | solution.py:322
  66.1 2.7 %relay.1 = (bf16[16,48,1024]{2,1,0:T(8,128)(2,1)}, bf16[16,16,1024]{2,1,0:T(8,128)(2,1)}) custom-call(bf16[528,1024]{1,0:T(8,128)(2,1)S(1)} %collective-permute-done.rows_ref), custom_call_target="tpu_custom_call" | custom-call | tf_op jit(solution)/shard_map/relay/pallas_call | solution.py:198
  68.9 0.0 all-to-all-done.own_ref
  68.9 7.8 %all-to-all-start.2 = ((bf16[16,48,1024]{2,1,0:T(8,128)(2,1)}), bf16[16,48,1024]{2,1,0:T(8,128)(2,1)}, u32[]{:S(2)}, u32[]{:S(2)}) async-start(bf16[16,48,1024]{2,1,0:T(8,128)(2,1)} %get-tuple-element.12), calls=%async_computation.2 | async-start | bytes 3145728 | tf_op jit(solution)/shard_map/all_to_all | solution.py:340
  76.6 0.4 collective-permute-start.1
  77.1 1.1 collective-permute-done.1
  78.2 1.8 %collective-permute-start.2 = (f32[64,512]{1,0:T(8,128)S(1)}, f32[64,512]{1,0:T(8,128)S(1)}, u32[]{:S(2)}, u32[]{:S(2)}) collective-permute-start(f32[64,512]{1,0:T(8,128)S(1)} %add.44), channel_id=1, source_target_pairs={{0,2},{1,3},{2,0},{3,1},{4,6},{5,7},{6,4},{7,5},{8,10},{9,11},{10,... | collective-permute-start | bytes 393224 | tf_op jit(solution)/shard_map/ppermute | solution.py:294
  80.0 21.7 %collective-permute-done.2 = f32[64,512]{1,0:T(8,128)S(1)} collective-permute-done((f32[64,512]{1,0:T(8,128)S(1)}, f32[64,512]{1,0:T(8,128)S(1)}, u32[]{:S(2)}, u32[]{:S(2)}) %collective-permute-start.2) | collective-permute-done | bytes 131104 | tf_op jit(solution)/shard_map/ppermute | solution.py:294
  101.7 0.3 collective-permute-start.3
  102.0 4.7 %collective-permute-done.3 = f32[64,512]{1,0:T(8,128)S(1)} collective-permute-done((f32[64,512]{1,0:T(8,128)S(1)}, f32[64,512]{1,0:T(8,128)S(1)}, u32[]{:S(2)}, u32[]{:S(2)}) %collective-permute-start.3) | collective-permute-done | bytes 131104 | tf_op jit(solution)/shard_map/ppermute | solution.py:294
  106.8 0.0 copy-done.3
  106.8 1.1 collective-permute-start.4
  107.9 4.0 %collective-permute-done.4 = f32[64,512]{1,0:T(8,128)S(1)} collective-permute-done((f32[64,512]{1,0:T(8,128)S(1)}, f32[64,512]{1,0:T(8,128)S(1)}, u32[]{:S(2)}, u32[]{:S(2)}) %collective-permute-start.4) | collective-permute-done | bytes 131104 | tf_op jit(solution)/shard_map/ppermute | solution.py:294
  111.9 0.1 collective-permute-start.5
  112.0 0.5 fusion.3
  112.5 0.6 copy.13
  113.1 0.0 all-to-all-done.2.far_ref
  113.1 5.3 %all-to-all-start.1 = ((bf16[16,16,1024]{2,1,0:T(8,128)(2,1)}), bf16[16,16,1024]{2,1,0:T(8,128)(2,1)S(1)}, u32[]{:S(2)}, u32[]{:S(2)}) async-start(bf16[16,16,1024]{2,1,0:T(8,128)(2,1)} %get-tuple-element.10), calls=%async_computation.1 | async-start | bytes 1048576 | tf_op jit(solution)/shard_map/all_to_all | solution.py:340
  118.5 0.7 collective-permute-done.5
  119.2 0.7 add_divide_fusion.weight_ref
  119.9 17.7 %pairs.2.refs_0_ = f32[1,8192,255]{2,1,0:T(8,128)} custom-call(s32[64]{0:T(128)} %station_ref.3, s32[64]{0:T(128)} %count_ref.3, s32[2,1,64,128]{3,2,1,0:T(8,128)} %bitcast.9, bf16[16,64,1024]{2,1,0:T(8,128)(2,1)} %copy-done.3, bf16[16,48,1024]{2,1,0:T(8,128)(2,1)} %all-to-all-done.2.far_ref, f32[64,512]{1,0:T(8,128)} %add_divide_fusion.weight_ref, ...), custom_call_target="tpu_custom_call" | custom-call | flops 9663676416 | bytes 6266880 | tf_op jit(solution)/shard_map/pairs/pallas_call | solution.py:271
  137.6 0.0 all-to-all-done.1.far_ref
  137.6 0.8 copy-done.4
  138.4 7.9 %pairs.3 = f32[1,8192,255]{2,1,0:T(8,128)} custom-call(s32[64]{0:T(128)} %station_ref.3, s32[64]{0:T(128)} %count_ref.3, s32[2,1,64,128]{3,2,1,0:T(8,128)} %bitcast.10, bf16[16,64,1024]{2,1,0:T(8,128)(2,1)} %copy-done.3, bf16[16,16,1024]{2,1,0:T(8,128)(2,1)} %copy-done.4, f32[64,512]{1,0:T(8,128)} %add_divide_fusion.weight_ref, ...), custom_call_target="tpu_custom_call", output_to_operand_aliasing={{}: (7, {})} | custom-call | flops 3221225472 | bytes 2088960 | tf_op jit(solution)/shard_map/pairs/pallas_call | solution.py:271
  (12 shorter events, 0.1 us)
Async XLA Ops:
  0.0 5.5 %copy-start.2 = (s32[32,64]{1,0:T(8,128)S(1)}, s32[32,64]{1,0:T(8,128)}, u32[]{:S(2)}) copy-start(s32[32,64]{1,0:T(8,128)} %index_ref.3) | copy-start | bytes 24580
  5.5 1.2 copy-start
  9.4 6.5 %copy-start.1 = (bf16[528,1024]{1,0:T(8,128)(2,1)S(1)}, bf16[528,1024]{1,0:T(8,128)(2,1)}, u32[]{:S(2)}) copy-start(bf16[528,1024]{1,0:T(8,128)(2,1)} %get-tuple-element.9.rows_ref) | copy-start | bytes 3244036
  9.4 59.4 %all-to-all-start = ((bf16[16,64,1024]{2,1,0:T(8,128)(2,1)}), bf16[16,64,1024]{2,1,0:T(8,128)(2,1)S(1)}, u32[]{:S(2)}, u32[]{:S(2)}) async-start(bf16[16,64,1024]{2,1,0:T(8,128)(2,1)} %own.1), calls=%async_computation | async-start | bytes 4194304 | tf_op jit(solution)/shard_map/all_to_all | solution.py:324
  15.9 60.7 %copy-start.5 = (f32[64,512]{1,0:T(8,128)S(1)}, f32[64,512]{1,0:T(8,128)}, u32[]{:S(2)}) copy-start(f32[64,512]{1,0:T(8,128)} %get-tuple-element.11) | copy-start | bytes 393220
  15.9 50.2 %collective-permute-start = (bf16[528,1024]{1,0:T(8,128)(2,1)S(1)}, bf16[528,1024]{1,0:T(8,128)(2,1)S(1)}, u32[]{:S(2)}, u32[]{:S(2)}) collective-permute-start(bf16[528,1024]{1,0:T(8,128)(2,1)S(1)} %copy-done.1), channel_id=1, source_target_pairs={{0,16},{1,17},{2,18},{3,19},{4,20},{5,21},{6,22},{7,23},{8,24},{9,... | collective-permute-start | bytes 3244040 | tf_op jit(solution)/shard_map/ppermute | solution.py:322
  68.9 37.9 %copy-start.3 = (bf16[16,64,1024]{2,1,0:T(8,128)(2,1)}, bf16[16,64,1024]{2,1,0:T(8,128)(2,1)S(1)}, u32[]{:S(2)}) copy-start(bf16[16,64,1024]{2,1,0:T(8,128)(2,1)S(1)} %all-to-all-done.own_ref) | copy-start | bytes 6291460
  68.9 43.1 %copy-start.6 = (s32[2,8192]{1,0:T(2,128)S(1)}, s32[2,8192]{1,0:T(2,128)}, u32[]{:S(2)}) copy-start(s32[2,8192]{1,0:T(2,128)} %param.15) | copy-start | bytes 196612
  68.9 44.3 %all-to-all-start.2 = ((bf16[16,48,1024]{2,1,0:T(8,128)(2,1)}), bf16[16,48,1024]{2,1,0:T(8,128)(2,1)}, u32[]{:S(2)}, u32[]{:S(2)}) async-start(bf16[16,48,1024]{2,1,0:T(8,128)(2,1)} %get-tuple-element.12), calls=%async_computation.2 | async-start | bytes 3145728 | tf_op jit(solution)/shard_map/all_to_all | solution.py:340
  76.6 1.5 %collective-permute-start.1 = (f32[64,512]{1,0:T(8,128)S(1)}, f32[64,512]{1,0:T(8,128)S(1)}, u32[]{:S(2)}, u32[]{:S(2)}) collective-permute-start(f32[64,512]{1,0:T(8,128)S(1)} %copy-done.5), channel_id=1, source_target_pairs={{0,1},{1,0},{2,3},{3,2},{4,5},{5,4},{6,7},{7,6},{8,9},{9,8},{10,11... | collective-permute-start | bytes 393224 | tf_op jit(solution)/shard_map/ppermute | solution.py:294
  78.2 23.5 %collective-permute-start.2 = (f32[64,512]{1,0:T(8,128)S(1)}, f32[64,512]{1,0:T(8,128)S(1)}, u32[]{:S(2)}, u32[]{:S(2)}) collective-permute-start(f32[64,512]{1,0:T(8,128)S(1)} %add.44), channel_id=1, source_target_pairs={{0,2},{1,3},{2,0},{3,1},{4,6},{5,7},{6,4},{7,5},{8,10},{9,11},{10,... | collective-permute-start | bytes 393224 | tf_op jit(solution)/shard_map/ppermute | solution.py:294
  101.7 5.0 %collective-permute-start.3 = (f32[64,512]{1,0:T(8,128)S(1)}, f32[64,512]{1,0:T(8,128)S(1)}, u32[]{:S(2)}, u32[]{:S(2)}) collective-permute-start(f32[64,512]{1,0:T(8,128)S(1)} %add.45), channel_id=1, source_target_pairs={{0,4},{1,5},{2,6},{3,7},{4,0},{5,1},{6,2},{7,3},{8,12},{9,13},{10,... | collective-permute-start | bytes 393224 | tf_op jit(solution)/shard_map/ppermute | solution.py:294
  106.8 5.0 %collective-permute-start.4 = (f32[64,512]{1,0:T(8,128)S(1)}, f32[64,512]{1,0:T(8,128)S(1)}, u32[]{:S(2)}, u32[]{:S(2)}) collective-permute-start(f32[64,512]{1,0:T(8,128)S(1)} %add.46), channel_id=1, source_target_pairs={{0,8},{1,9},{2,10},{3,11},{4,12},{5,13},{6,14},{7,15},{8,0},{9,1},... | collective-permute-start | bytes 393224 | tf_op jit(solution)/shard_map/ppermute | solution.py:294
  111.9 7.3 %collective-permute-start.5 = (f32[64,512]{1,0:T(8,128)S(1)}, f32[64,512]{1,0:T(8,128)S(1)}, u32[]{:S(2)}, u32[]{:S(2)}) collective-permute-start(f32[64,512]{1,0:T(8,128)S(1)} %add.47), channel_id=1, source_target_pairs={{0,16},{1,17},{2,18},{3,19},{4,20},{5,21},{6,22},{7,23},{8,24},{9,... | collective-permute-start | bytes 393224 | tf_op jit(solution)/shard_map/ppermute | solution.py:294
  113.1 24.4 %all-to-all-start.1 = ((bf16[16,16,1024]{2,1,0:T(8,128)(2,1)}), bf16[16,16,1024]{2,1,0:T(8,128)(2,1)S(1)}, u32[]{:S(2)}, u32[]{:S(2)}) async-start(bf16[16,16,1024]{2,1,0:T(8,128)(2,1)} %get-tuple-element.10), calls=%async_computation.1 | async-start | bytes 1048576 | tf_op jit(solution)/shard_map/all_to_all | solution.py:340
  137.6 0.8 copy-start.4

commit v5 on v4

--- a/solution.py
+++ b/solution.py
@@ -286,14 +286,8 @@
     )(stations_of, counts, *args)
 
 
-def power_total(power, owners):
-    if owners & (owners - 1):
-        return lax.psum(power, "ev")
-    step = 1
-    while step < owners:
-        power += lax.ppermute(power, "ev", [(i, i ^ step) for i in range(owners)])
-        step *= 2
-    return power
+def add_across(power, step, owners):
+    return power + lax.ppermute(power, "ev", [(i, i ^ step) for i in range(owners)])
 
 
 def shards(windows, rotation, source_inverse, send_rows, tile_station, tile_count, pair_rows):
@@ -321,13 +315,21 @@
     )
     swapped = lax.ppermute(rows, "ev", across)
     sends = own_sends(half_arg, rows, send_rows)
+    step = 1
+    while step < peers // 2:
+        power = add_across(power, step, owners)
+        step *= 2
+    sends, power = lax.optimization_barrier((sends, power))
+    power = add_across(power, step, owners)
     own = to_peers(sends)
-    weight = 1.0 / (power_total(power, owners) / (ev_dev * owners) + epsilon)
     groups = cap // SUB
     parts = [groups * part // sum(SPLIT) for part in SPLIT[:-1]]
     sizes = parts + [groups - sum(parts)]
     sends = relay_sends(swapped, peers, sizes)
 
+    sends, own, power = lax.optimization_barrier((sends, own, power))
+    power = add_across(power, peers, owners)
+    weight = 1.0 / (power / (ev_dev * owners) + epsilon)
     source = pair_rows // cap
     side = source // peers != half
     places = jnp.where(side, peers * SUB, 0) + source % peers * SUB + pair_rows % SUB

time: 147 us -> 142 us (0.966)
  waiting for transfers between devices: 79.8 us -> 74.4 us
    ppermute x1, waiting for transfers between devices: 47.6 us -> 0.01 us  [shards(): swapped = lax.ppermute(rows, 'ev', across)]
    ppermute x5, waiting for transfers between devices: 32.2 us -> 53.5 us  [add_across(): lax.ppermute(power, 'ev', [(i, i ^ step) for i in range(owners)])]
    all_to_all x2, waiting for transfers between devices: 0.01 us -> 20.9 us  [shards(): far = to_peers(send)]
    ppermute x5, starting transfers between devices: 3.74 us -> 10.1 us  [add_across(): lax.ppermute(power, 'ev', [(i, i ^ step) for i in range(owners)])]
    all_to_all x2, starting transfers between devices: 13.1 us -> 8.89 us  [shards(): far = to_peers(send)]
    all_to_all x1, starting transfers between devices: 6.45 us -> 4.48 us  [shards(): own = to_peers(sends)]
  transfers between devices with their start and end apart: 9 -> 9, of which waited for: 6 -> 4; matrix products, arithmetic and copies ran while one was open for 1% -> 1% of each run, Pallas kernels for 14% -> 16%
where the time goes in v5:
time: 142 us
  waiting for transfers between devices  74.4 us (52%)
  Pallas kernels  36.4 us (26%)
  starting transfers between devices  26.1 us (18%)
  local copies, waits for them, and re-layouts  2.67 us (2%)
  other arithmetic  2.15 us (2%)
    ppermute x5, waiting for transfers between devices, add_across(): lax.ppermute(power, 'ev', [(i, i ^ step) for i in range(owners)])  53.5 us
    pallas_call x2, Pallas kernels, correlate(): pl.pallas_call(partial(pair_kernel, geo, first), grid_spec=pltpu.Prefetch...  25.6 us
    all_to_all x2, waiting for transfers between devices, shards(): far = to_peers(send)  20.9 us
    ppermute x5, starting transfers between devices, add_across(): lax.ppermute(power, 'ev', [(i, i ^ step) for i in range(owners)])  10.1 us
    all_to_all x2, starting transfers between devices, shards(): far = to_peers(send)  8.89 us
    pallas_call x1, Pallas kernels, event_rows(): pl.pallas_call(partial(spectra_kernel, steps), grid_spec=pltpu.PrefetchSc...  5.41 us
    all_to_all x1, starting transfers between devices, shards(): own = to_peers(sends)  4.48 us
  transfers between devices with their start and end apart: 9, of which 4 were waited for; matrix products, arithmetic and copies ran while one was open for 1% of the time, Pallas kernels for 16%

profile of v5, /device:TPU:0, one launch (start us, length us, event | category | flops | bytes accessed | tf_op | source)
XLA Modules:
  0.0 141.8 jit_solution(4220316604340667475)
XLA Ops:
  0.0 5.4 %spectra.1 = (bf16[528,1024]{1,0:T(8,128)(2,1)}, f32[64,512]{1,0:T(8,128)}) custom-call(s32[1]{0:T(128)} %bitcast.half_ref, bf16[8,3,64,1024]{3,2,1,0:T(8,128)(2,1)} %win_ref.1, bf16[3,8,64]{2,1,0:T(8,128)(2,1)} %bitcast.11, bf16[8,1024]{1,0:T(8,128)(2,1)} %inv_ref.1, bf16[1024,1024]{1,0:T(8,128)(2,1)} %constant.83.table_ref, s32[32,64]{1,0:T(8,128)} %index_ref.3), custom_call_target="tpu_custom_call" | custom-call | tf_op jit(solution)/shard_map/spectra/pallas_call | solution.py:117
  5.4 0.5 collective-permute-start.1
  5.9 1.2 collective-permute-done.1
  7.1 0.9 add.44
  8.0 2.9 %collective-permute-start.2 = (f32[64,512]{1,0:T(8,128)S(1)}, f32[64,512]{1,0:T(8,128)S(1)}, u32[]{:S(2)}, u32[]{:S(2)}) collective-permute-start(f32[64,512]{1,0:T(8,128)S(1)} %add.44), channel_id=1, source_target_pairs={{0,2},{1,3},{2,0},{3,1},{4,6},{5,7},{6,4},{7,5},{8,10},{9,11},{10,... | collective-permute-start | bytes 393224 | tf_op jit(solution)/shard_map/ppermute | solution.py:290
  10.9 3.8 %collective-permute-done.2 = f32[64,512]{1,0:T(8,128)S(1)} collective-permute-done((f32[64,512]{1,0:T(8,128)S(1)}, f32[64,512]{1,0:T(8,128)S(1)}, u32[]{:S(2)}, u32[]{:S(2)}) %collective-permute-start.2) | collective-permute-done | bytes 131104 | tf_op jit(solution)/shard_map/ppermute | solution.py:290
  14.8 1.8 %collective-permute-start.3 = (f32[64,512]{1,0:T(8,128)S(1)}, f32[64,512]{1,0:T(8,128)S(1)}, u32[]{:S(2)}, u32[]{:S(2)}) collective-permute-start(f32[64,512]{1,0:T(8,128)S(1)} %add.45), channel_id=1, source_target_pairs={{0,4},{1,5},{2,6},{3,7},{4,0},{5,1},{6,2},{7,3},{8,12},{9,13},{10,... | collective-permute-start | bytes 393224 | tf_op jit(solution)/shard_map/ppermute | solution.py:290
  16.6 0.0 copy-done.2
  16.6 1.2 copy-done
  17.9 2.7 %own.1 = bf16[16,64,1024]{2,1,0:T(8,128)(2,1)} custom-call(s32[1]{0:T(128)} %bitcast.half_ref, bf16[528,1024]{1,0:T(8,128)(2,1)S(1)} %copy-done, s32[32,64]{1,0:T(8,128)S(1)} %copy-done.2), custom_call_target="tpu_custom_call" | custom-call | tf_op jit(solution)/shard_map/own/pallas_call | solution.py:166
  20.6 0.0 collective-permute-done.3
  20.6 4.5 %all-to-all-start = ((bf16[16,64,1024]{2,1,0:T(8,128)(2,1)}), bf16[16,64,1024]{2,1,0:T(8,128)(2,1)S(1)}, u32[]{:S(2)}, u32[]{:S(2)}) async-start(bf16[16,64,1024]{2,1,0:T(8,128)(2,1)} %own.1), calls=%async_computation | async-start | bytes 4194304 | tf_op jit(solution)/shard_map/all_to_all | solution.py:324
  25.1 0.0 copy-done.1
  25.1 2.6 %collective-permute-start = (bf16[528,1024]{1,0:T(8,128)(2,1)S(1)}, bf16[528,1024]{1,0:T(8,128)(2,1)S(1)}, u32[]{:S(2)}, u32[]{:S(2)}) collective-permute-start(bf16[528,1024]{1,0:T(8,128)(2,1)S(1)} %copy-done.1), channel_id=1, source_target_pairs={{0,16},{1,17},{2,18},{3,19},{4,20},{5,21},{6,22},{7,23},{8,24},{9,... | collective-permute-start | bytes 3244040 | tf_op jit(solution)/shard_map/ppermute | solution.py:316
  27.7 1.9 %collective-permute-start.4 = (f32[64,512]{1,0:T(8,128)S(1)}, f32[64,512]{1,0:T(8,128)S(1)}, u32[]{:S(2)}, u32[]{:S(2)}) collective-permute-start(f32[64,512]{1,0:T(8,128)S(1)} %add.46), channel_id=1, source_target_pairs={{0,8},{1,9},{2,10},{3,11},{4,12},{5,13},{6,14},{7,15},{8,0},{9,1},... | collective-permute-start | bytes 393224 | tf_op jit(solution)/shard_map/ppermute | solution.py:290
  29.7 48.5 %collective-permute-done.4 = f32[64,512]{1,0:T(8,128)S(1)} collective-permute-done((f32[64,512]{1,0:T(8,128)S(1)}, f32[64,512]{1,0:T(8,128)S(1)}, u32[]{:S(2)}, u32[]{:S(2)}) %collective-permute-start.4) | collective-permute-done | bytes 131104 | tf_op jit(solution)/shard_map/ppermute | solution.py:290
  78.2 0.0 copy-start.5
  78.2 0.0 collective-permute-done.rows_ref
  78.2 2.7 %relay.1 = (bf16[16,48,1024]{2,1,0:T(8,128)(2,1)}, bf16[16,16,1024]{2,1,0:T(8,128)(2,1)}) custom-call(bf16[528,1024]{1,0:T(8,128)(2,1)S(1)} %collective-permute-done.rows_ref), custom_call_target="tpu_custom_call" | custom-call | tf_op jit(solution)/shard_map/relay/pallas_call | solution.py:198
  80.9 0.0 all-to-all-done.own_ref
  80.9 5.3 %all-to-all-start.2 = ((bf16[16,48,1024]{2,1,0:T(8,128)(2,1)}), bf16[16,48,1024]{2,1,0:T(8,128)(2,1)}, u32[]{:S(2)}, u32[]{:S(2)}) async-start(bf16[16,48,1024]{2,1,0:T(8,128)(2,1)} %get-tuple-element.24), calls=%async_computation.2 | async-start | bytes 3145728 | tf_op jit(solution)/shard_map/all_to_all | solution.py:342
  86.3 2.9 %collective-permute-start.5 = (f32[64,512]{1,0:T(8,128)S(1)}, f32[64,512]{1,0:T(8,128)S(1)}, u32[]{:S(2)}, u32[]{:S(2)}) collective-permute-start(f32[64,512]{1,0:T(8,128)S(1)} %add.47), channel_id=1, source_target_pairs={{0,16},{1,17},{2,18},{3,19},{4,20},{5,21},{6,22},{7,23},{8,24},{9,... | collective-permute-start | bytes 393224 | tf_op jit(solution)/shard_map/ppermute | solution.py:290
  89.2 0.5 fusion.3
  89.7 0.6 copy.13
  90.3 20.9 %all-to-all-done.2.far_ref = bf16[16,48,1024]{2,1,0:T(8,128)(2,1)} async-done(((bf16[16,48,1024]{2,1,0:T(8,128)(2,1)}), bf16[16,48,1024]{2,1,0:T(8,128)(2,1)}, u32[]{:S(2)}, u32[]{:S(2)}) %all-to-all-start.2) | async-done | bytes 1572896 | tf_op jit(solution)/shard_map/all_to_all | solution.py:342
  111.1 3.6 %all-to-all-start.1 = ((bf16[16,16,1024]{2,1,0:T(8,128)(2,1)}), bf16[16,16,1024]{2,1,0:T(8,128)(2,1)S(1)}, u32[]{:S(2)}, u32[]{:S(2)}) async-start(bf16[16,16,1024]{2,1,0:T(8,128)(2,1)} %get-tuple-element.22), calls=%async_computation.1 | async-start | bytes 1048576 | tf_op jit(solution)/shard_map/all_to_all | solution.py:342
  114.7 0.0 collective-permute-done.5
  114.7 0.7 add_divide_fusion.weight_ref
  115.4 17.7 %pairs.2.refs_0_ = f32[1,8192,255]{2,1,0:T(8,128)} custom-call(s32[64]{0:T(128)} %station_ref.3, s32[64]{0:T(128)} %count_ref.3, s32[2,1,64,128]{3,2,1,0:T(8,128)} %bitcast.9, bf16[16,64,1024]{2,1,0:T(8,128)(2,1)} %copy-done.3, bf16[16,48,1024]{2,1,0:T(8,128)(2,1)} %all-to-all-done.2.far_ref, f32[64,512]{1,0:T(8,128)} %add_divide_fusion.weight_ref, ...), custom_call_target="tpu_custom_call" | custom-call | flops 9663676416 | bytes 6266880 | tf_op jit(solution)/shard_map/pairs/pallas_call | solution.py:271
  133.1 0.0 all-to-all-done.1.far_ref
  133.1 0.8 copy-done.4
  133.9 7.9 %pairs.3 = f32[1,8192,255]{2,1,0:T(8,128)} custom-call(s32[64]{0:T(128)} %station_ref.3, s32[64]{0:T(128)} %count_ref.3, s32[2,1,64,128]{3,2,1,0:T(8,128)} %bitcast.10, bf16[16,64,1024]{2,1,0:T(8,128)(2,1)} %copy-done.3, bf16[16,16,1024]{2,1,0:T(8,128)(2,1)} %copy-done.4, f32[64,512]{1,0:T(8,128)} %add_divide_fusion.weight_ref, ...), custom_call_target="tpu_custom_call", output_to_operand_aliasing={{}: (7, {})} | custom-call | flops 3221225472 | bytes 2088960 | tf_op jit(solution)/shard_map/pairs/pallas_call | solution.py:271
  (10 shorter events, 0.1 us)
Async XLA Ops:
  0.0 16.6 %copy-start.2 = (s32[32,64]{1,0:T(8,128)S(1)}, s32[32,64]{1,0:T(8,128)}, u32[]{:S(2)}) copy-start(s32[32,64]{1,0:T(8,128)} %index_ref.3) | copy-start | bytes 24580
  5.4 1.7 %collective-permute-start.1 = (f32[64,512]{1,0:T(8,128)}, f32[64,512]{1,0:T(8,128)S(1)}, u32[]{:S(2)}, u32[]{:S(2)}) collective-permute-start(f32[64,512]{1,0:T(8,128)} %get-tuple-element.18), channel_id=1, source_target_pairs={{0,1},{1,0},{2,3},{3,2},{4,5},{5,4},{6,7},{7,6},{8,9},{9,8},{10,11... | collective-permute-start | bytes 393224 | tf_op jit(solution)/shard_map/ppermute | solution.py:290
  8.0 6.7 %collective-permute-start.2 = (f32[64,512]{1,0:T(8,128)S(1)}, f32[64,512]{1,0:T(8,128)S(1)}, u32[]{:S(2)}, u32[]{:S(2)}) collective-permute-start(f32[64,512]{1,0:T(8,128)S(1)} %add.44), channel_id=1, source_target_pairs={{0,2},{1,3},{2,0},{3,1},{4,6},{5,7},{6,4},{7,5},{8,10},{9,11},{10,... | collective-permute-start | bytes 393224 | tf_op jit(solution)/shard_map/ppermute | solution.py:290
  14.8 5.8 %collective-permute-start.3 = (f32[64,512]{1,0:T(8,128)S(1)}, f32[64,512]{1,0:T(8,128)S(1)}, u32[]{:S(2)}, u32[]{:S(2)}) collective-permute-start(f32[64,512]{1,0:T(8,128)S(1)} %add.45), channel_id=1, source_target_pairs={{0,4},{1,5},{2,6},{3,7},{4,0},{5,1},{6,2},{7,3},{8,12},{9,13},{10,... | collective-permute-start | bytes 393224 | tf_op jit(solution)/shard_map/ppermute | solution.py:290
  16.6 1.2 copy-start
  20.6 4.5 %copy-start.1 = (bf16[528,1024]{1,0:T(8,128)(2,1)S(1)}, bf16[528,1024]{1,0:T(8,128)(2,1)}, u32[]{:S(2)}) copy-start(bf16[528,1024]{1,0:T(8,128)(2,1)} %get-tuple-element.15.rows_ref) | copy-start | bytes 3244036
  20.6 60.3 %all-to-all-start = ((bf16[16,64,1024]{2,1,0:T(8,128)(2,1)}), bf16[16,64,1024]{2,1,0:T(8,128)(2,1)S(1)}, u32[]{:S(2)}, u32[]{:S(2)}) async-start(bf16[16,64,1024]{2,1,0:T(8,128)(2,1)} %own.1), calls=%async_computation | async-start | bytes 4194304 | tf_op jit(solution)/shard_map/all_to_all | solution.py:324
  25.1 53.1 %collective-permute-start = (bf16[528,1024]{1,0:T(8,128)(2,1)S(1)}, bf16[528,1024]{1,0:T(8,128)(2,1)S(1)}, u32[]{:S(2)}, u32[]{:S(2)}) collective-permute-start(bf16[528,1024]{1,0:T(8,128)(2,1)S(1)} %copy-done.1), channel_id=1, source_target_pairs={{0,16},{1,17},{2,18},{3,19},{4,20},{5,21},{6,22},{7,23},{8,24},{9,... | collective-permute-start | bytes 3244040 | tf_op jit(solution)/shard_map/ppermute | solution.py:316
  27.7 50.4 %collective-permute-start.4 = (f32[64,512]{1,0:T(8,128)S(1)}, f32[64,512]{1,0:T(8,128)S(1)}, u32[]{:S(2)}, u32[]{:S(2)}) collective-permute-start(f32[64,512]{1,0:T(8,128)S(1)} %add.46), channel_id=1, source_target_pairs={{0,8},{1,9},{2,10},{3,11},{4,12},{5,13},{6,14},{7,15},{8,0},{9,1},... | collective-permute-start | bytes 393224 | tf_op jit(solution)/shard_map/ppermute | solution.py:290
  78.2 11.0 %copy-start.5 = (s32[2,8192]{1,0:T(2,128)S(1)}, s32[2,8192]{1,0:T(2,128)}, u32[]{:S(2)}) copy-start(s32[2,8192]{1,0:T(2,128)} %param.15) | copy-start | bytes 196612
  80.9 30.2 %copy-start.3 = (bf16[16,64,1024]{2,1,0:T(8,128)(2,1)}, bf16[16,64,1024]{2,1,0:T(8,128)(2,1)S(1)}, u32[]{:S(2)}) copy-start(bf16[16,64,1024]{2,1,0:T(8,128)(2,1)S(1)} %all-to-all-done.own_ref) | copy-start | bytes 6291460
  80.9 30.2 %all-to-all-start.2 = ((bf16[16,48,1024]{2,1,0:T(8,128)(2,1)}), bf16[16,48,1024]{2,1,0:T(8,128)(2,1)}, u32[]{:S(2)}, u32[]{:S(2)}) async-start(bf16[16,48,1024]{2,1,0:T(8,128)(2,1)} %get-tuple-element.24), calls=%async_computation.2 | async-start | bytes 3145728 | tf_op jit(solution)/shard_map/all_to_all | solution.py:342
  86.3 28.5 %collective-permute-start.5 = (f32[64,512]{1,0:T(8,128)S(1)}, f32[64,512]{1,0:T(8,128)S(1)}, u32[]{:S(2)}, u32[]{:S(2)}) collective-permute-start(f32[64,512]{1,0:T(8,128)S(1)} %add.47), channel_id=1, source_target_pairs={{0,16},{1,17},{2,18},{3,19},{4,20},{5,21},{6,22},{7,23},{8,24},{9,... | collective-permute-start | bytes 393224 | tf_op jit(solution)/shard_map/ppermute | solution.py:290
  111.1 22.0 %all-to-all-start.1 = ((bf16[16,16,1024]{2,1,0:T(8,128)(2,1)}), bf16[16,16,1024]{2,1,0:T(8,128)(2,1)S(1)}, u32[]{:S(2)}, u32[]{:S(2)}) async-start(bf16[16,16,1024]{2,1,0:T(8,128)(2,1)} %get-tuple-element.22), calls=%async_computation.1 | async-start | bytes 1048576 | tf_op jit(solution)/shard_map/all_to_all | solution.py:342
  133.1 0.8 copy-start.4

commit v6 on v5

--- a/solution.py
+++ b/solution.py
@@ -148,59 +148,80 @@
             store(first + j, picked[j * cap : (j + 1) * cap])
 
 
-def own_kernel(half_ref, rows_ref, index_ref, send_ref):
-    peers = send_ref.shape[0]
+def spread(index, rows, refs, skips):
+    def store(peer, picked):
+        start = 0
+        for ref, skip in zip(refs, skips):
+            count = ref.shape[1] - skip
+            ref[peer, skip:, :] = picked[start : start + count]
+            start += count
+
+    pick_rows(index, rows, store)
+
+
+def own_kernel(half_ref, rows_ref, index_ref, *send_refs):
+    peers = send_refs[0].shape[0]
     mine = pl.multiple_of(half_ref[0] * peers, peers)
-
-    def store(peer, picked):
-        send_ref[peer] = picked
-
-    pick_rows(index_ref[pl.ds(mine, peers), :], rows_ref[...], store)
-
-
-def own_sends(half, rows, send_rows):
+    spread(index_ref[pl.ds(mine, peers), :], rows_ref[...], send_refs, (0, 0))
+
+
+def own_sends(half, rows, send_rows, sizes):
     owners, cap = send_rows.shape
     peers = owners // 2
     length = rows.shape[1]
     whole = lambda *shape: pl.BlockSpec(shape, lambda i, *_: (0,) * len(shape))
+    shapes = [(peers, size * SUB, length) for size in sizes]
     return pl.pallas_call(
         own_kernel,
         grid_spec=pltpu.PrefetchScalarGridSpec(
             num_scalar_prefetch=1,
             grid=(1,),
             in_specs=[whole(rows.shape[0] - peers, length), whole(owners, cap)],
-            out_specs=whole(peers, cap, length),
+            out_specs=[whole(*shape) for shape in shapes],
         ),
-        out_shape=jax.ShapeDtypeStruct((peers, cap, length), BF16),
+        out_shape=[jax.ShapeDtypeStruct(shape, BF16) for shape in shapes],
         compiler_params=pltpu.CompilerParams(vmem_limit_bytes=SMALL),
         name="own",
     )(half, rows, send_rows)
 
 
-def relay_kernel(rows_ref, *send_refs):
-    peers = send_refs[0].shape[0]
-    cap = sum(ref.shape[1] for ref in send_refs)
+def relay_kernel(cap, rows_ref, rest_ref, first_ref, last_ref):
+    peers, kept, _ = rest_ref.shape
     tail = rows_ref.shape[0] - peers
     digits = rows_ref[tail:, :].astype(F32).astype(jnp.int32)
     index = digits[:, :cap] * LANES + digits[:, LANES : LANES + cap]
-
-    def store(peer, picked):
-        start = 0
-        for ref in send_refs:
-            ref[peer] = picked[start : start + ref.shape[1]]
-            start += ref.shape[1]
-
-    pick_rows(index, rows_ref[:tail, :], store)
-
-
-def relay_sends(rows, peers, sizes):
-    length = rows.shape[1]
-    return pl.pallas_call(
-        relay_kernel,
-        out_shape=[jax.ShapeDtypeStruct((peers, size * SUB, length), BF16) for size in sizes],
+    spread(index, rows_ref[:tail, :], (first_ref, last_ref), (0, kept))
+    last_ref[:, :kept, :] = rest_ref[...]
+
+
+def relay_sends(rows, rest, cap):
+    peers, kept, length = rest.shape
+    shapes = [(peers, cap - kept, length), (peers, 2 * kept, length)]
+    return pl.pallas_call(
+        partial(relay_kernel, cap),
+        out_shape=[jax.ShapeDtypeStruct(shape, BF16) for shape in shapes],
         compiler_params=pltpu.CompilerParams(vmem_limit_bytes=SMALL),
         name="relay",
-    )(rows)
+    )(rows, rest)
+
+
+def place_kernel(peers, half_ref, pair_ref, place_ref):
+    cap = pair_ref.shape[2]
+    pair = pair_ref[...]
+    source = lax.div(pair, cap)
+    side = lax.div(source, peers) != half_ref[0]
+    offset = jnp.where(side, peers * SUB, 0)
+    place_ref[...] = offset + lax.rem(source, peers) * SUB + lax.rem(pair, SUB)
+
+
+def place_rows(half, pairs, peers):
+    return pl.pallas_call(
+        partial(place_kernel, peers),
+        in_specs=[pl.BlockSpec(memory_space=pltpu.SMEM), pl.BlockSpec(memory_space=pltpu.VMEM)],
+        out_shape=jax.ShapeDtypeStruct(pairs.shape, jnp.int32),
+        compiler_params=pltpu.CompilerParams(vmem_limit_bytes=SMALL),
+        name="places",
+    )(half, pairs)
 
 
 def pair_kernel(geo, first, station_ref, count_ref, place_ref, own_ref, far_ref, weight_ref, lag_ref, *refs):
@@ -251,12 +272,13 @@
 
 
 def correlate(first, steps, geo, stations_of, counts, places, own, far, weight, lag_tab, previous):
+    (own, own_at), (far, far_at) = own, far
     peers, cap, joint = geo
     length = own.shape[-1]
     in_specs = [
         pl.BlockSpec((2, joint, SUB, LANES), lambda i, *_: (0, 0, i + first, 0)),
-        pl.BlockSpec((peers, SUB, length), lambda i, *_: (0, i + first, 0)),
-        pl.BlockSpec((peers, SUB, length), lambda i, *_: (0, i, 0)),
+        pl.BlockSpec((peers, SUB, length), lambda i, *_: (0, i + own_at, 0)),
+        pl.BlockSpec((peers, SUB, length), lambda i, *_: (0, i + far_at, 0)),
         pl.BlockSpec(weight.shape, lambda i, *_: (0, 0)),
         pl.BlockSpec(lag_tab.shape, lambda i, *_: (0, 0)),
     ]
@@ -313,37 +335,31 @@
     rows, power = event_rows(
         half_arg, windows, rotation, source_inverse, send_rows, spectral_table(length)
     )
+    groups = cap // SUB
+    early = groups * SPLIT[0] // sum(SPLIT)
+    sizes = (early, groups - early)
     swapped = lax.ppermute(rows, "ev", across)
-    sends = own_sends(half_arg, rows, send_rows)
+    send, rest = own_sends(half_arg, rows, send_rows, sizes)
     step = 1
     while step < peers // 2:
         power = add_across(power, step, owners)
         step *= 2
-    sends, power = lax.optimization_barrier((sends, power))
+    send, power = lax.optimization_barrier((send, power))
     power = add_across(power, step, owners)
-    own = to_peers(sends)
-    groups = cap // SUB
-    parts = [groups * part // sum(SPLIT) for part in SPLIT[:-1]]
-    sizes = parts + [groups - sum(parts)]
-    sends = relay_sends(swapped, peers, sizes)
-
+    own = to_peers(send)
+    sends = relay_sends(swapped, rest, cap)
     sends, own, power = lax.optimization_barrier((sends, own, power))
     power = add_across(power, peers, owners)
     weight = 1.0 / (power / (ev_dev * owners) + epsilon)
-    source = pair_rows // cap
-    side = source // peers != half
-    places = jnp.where(side, peers * SUB, 0) + source % peers * SUB + pair_rows % SUB
-    places = places.reshape(2, joint, cap, LANES)
+    places = place_rows(half_arg, pair_rows.reshape(2, joint, cap, LANES), peers)
     lag_tab = lag_table(length, LAGS, LAGS + 1)
     geo = (peers, cap, joint)
-    result = None
-    first = 0
-    for steps, send in zip(sizes, sends):
-        far = to_peers(send)
-        result = correlate(
-            first, steps, geo, tile_station, tile_count, places, own, far, weight, lag_tab, result
-        )
-        first += steps
+    far = to_peers(sends[0])
+    last = to_peers(sends[1])
+    run = partial(correlate, geo=geo, stations_of=tile_station, counts=tile_count, places=places)
+    run = partial(run, weight=weight, lag_tab=lag_tab)
+    result = run(0, sizes[0], own=(own, 0), far=(far, 0), previous=None)
+    result = run(early, sizes[1], own=(last, 0), far=(last, sizes[1]), previous=result)
     return result.reshape(tiles_dev * LANES, LAGS)
 
 

time: 142 us -> 152 us (1.070); the launches traced: 142 us -> 150 us
  blocking collectives: 0 us -> 25.7 us
  waiting for transfers between devices: 74.4 us -> 61.5 us
  starting transfers between devices: 26.1 us -> 21.7 us
    all_to_all x0 -> x1, blocking collectives: none -> 25.7 us  [shards(): far = to_peers(sends[0])]
    all_to_all x3 -> x2, waiting for transfers between devices: 20.9 us -> 0.01 us  [the longest x1 0.01 us: shards(): own = to_peers(send)]
    ppermute x1, waiting for transfers between devices: 0.01 us -> 5.76 us  [shards(): swapped = lax.ppermute(rows, 'ev', across)]
    all_to_all x3 -> x2, starting transfers between devices: 13.4 us -> 8.49 us  [the longest x1 4.71 us: shards(): own = to_peers(send)]
    ppermute x5, waiting for transfers between devices: 53.5 us -> 55.8 us  [add_across(): lax.ppermute(power, 'ev', [(i, i ^ step) for i in range(owners)])]
  transfers between devices with their start and end apart: 9 -> 8, of which waited for: 4 -> 5; matrix products, arithmetic and copies ran while one was open for 1% -> 0% of each run, Pallas kernels for 16% -> 15%
where the time goes in v6:
time: 152 us; the launch traced here: 150 us
  waiting for transfers between devices  61.5 us (40%)
  Pallas kernels  36 us (24%)
  blocking collectives  25.7 us (17%)
  starting transfers between devices  21.7 us (14%)
  local copies, waits for them, and re-layouts  2.86 us (2%)
  other arithmetic  1.68 us (1%)
    ppermute x5, waiting for transfers between devices, add_across(): lax.ppermute(power, 'ev', [(i, i ^ step) for i in range(owners)])  55.8 us
    all_to_all x1, blocking collectives, shards(): far = to_peers(sends[0])  25.7 us
    pallas_call x2, Pallas kernels, correlate(): pl.pallas_call(partial(pair_kernel, geo, first), grid_spec=pltpu.Prefetch...  25.5 us
    ppermute x5, starting transfers between devices, add_across(): lax.ppermute(power, 'ev', [(i, i ^ step) for i in range(owners)])  10.6 us
    ppermute x1, waiting for transfers between devices, shards(): swapped = lax.ppermute(rows, 'ev', across)  5.76 us
    pallas_call x1, Pallas kernels, event_rows(): pl.pallas_call(partial(spectra_kernel, steps), grid_spec=pltpu.PrefetchSc...  5.49 us
    all_to_all x1, starting transfers between devices, shards(): own = to_peers(send)  4.71 us
    all_to_all x1, starting transfers between devices, shards(): last = to_peers(sends[1])  3.78 us
  transfers between devices with their start and end apart: 8, of which 5 were waited for; matrix products, arithmetic and copies ran while one was open for 0% of the time, Pallas kernels for 15%

profile of v6, /device:TPU:0, one launch (start us, length us, event | category | flops | bytes accessed | tf_op | source)
XLA Modules:
  0.0 149.5 jit_solution(16255098483872089621)
XLA Ops:
  0.0 5.5 %spectra.1 = (bf16[528,1024]{1,0:T(8,128)(2,1)}, f32[64,512]{1,0:T(8,128)}) custom-call(s32[1]{0:T(128)} %bitcast.half_ref, bf16[8,3,64,1024]{3,2,1,0:T(8,128)(2,1)} %win_ref.1, bf16[3,8,64]{2,1,0:T(8,128)(2,1)} %bitcast.10, bf16[8,1024]{1,0:T(8,128)(2,1)} %inv_ref.1, bf16[1024,1024]{1,0:T(8,128)(2,1)} %constant.36.table_ref, s32[32,64]{1,0:T(8,128)} %index_ref.3), custom_call_target="tpu_custom_call" | custom-call | tf_op jit(solution)/shard_map/spectra/pallas_call | solution.py:117
  5.5 0.5 collective-permute-start.1
  6.0 1.2 collective-permute-done.1
  7.2 0.9 add.22
  8.1 2.9 %collective-permute-start.2 = (f32[64,512]{1,0:T(8,128)S(1)}, f32[64,512]{1,0:T(8,128)S(1)}, u32[]{:S(2)}, u32[]{:S(2)}) collective-permute-start(f32[64,512]{1,0:T(8,128)S(1)} %add.22), channel_id=1, source_target_pairs={{0,2},{1,3},{2,0},{3,1},{4,6},{5,7},{6,4},{7,5},{8,10},{9,11},{10,... | collective-permute-start | bytes 393224 | tf_op jit(solution)/shard_map/ppermute | solution.py:312
  11.0 3.8 %collective-permute-done.2 = f32[64,512]{1,0:T(8,128)S(1)} collective-permute-done((f32[64,512]{1,0:T(8,128)S(1)}, f32[64,512]{1,0:T(8,128)S(1)}, u32[]{:S(2)}, u32[]{:S(2)}) %collective-permute-start.2) | collective-permute-done | bytes 131104 | tf_op jit(solution)/shard_map/ppermute | solution.py:312
  14.9 1.8 %collective-permute-start.3 = (f32[64,512]{1,0:T(8,128)S(1)}, f32[64,512]{1,0:T(8,128)S(1)}, u32[]{:S(2)}, u32[]{:S(2)}) collective-permute-start(f32[64,512]{1,0:T(8,128)S(1)} %add.23), channel_id=1, source_target_pairs={{0,4},{1,5},{2,6},{3,7},{4,0},{5,1},{6,2},{7,3},{8,12},{9,13},{10,... | collective-permute-start | bytes 393224 | tf_op jit(solution)/shard_map/ppermute | solution.py:312
  16.7 0.0 copy-done.3
  16.7 1.2 copy-done
  17.9 2.5 %own.1 = (bf16[16,48,1024]{2,1,0:T(8,128)(2,1)}, bf16[16,16,1024]{2,1,0:T(8,128)(2,1)S(1)}) custom-call(s32[1]{0:T(128)} %bitcast.half_ref, bf16[528,1024]{1,0:T(8,128)(2,1)S(1)} %copy-done, s32[32,64]{1,0:T(8,128)S(1)} %copy-done.3), custom_call_target="tpu_custom_call" | custom-call | tf_op jit(solution)/shard_map/own/pallas_call | solution.py:174
  20.5 0.0 collective-permute-done.3
  20.5 0.0 copy-start.1
  20.5 4.7 %all-to-all-start = ((bf16[16,48,1024]{2,1,0:T(8,128)(2,1)}), bf16[16,48,1024]{2,1,0:T(8,128)(2,1)}, u32[]{:S(2)}, u32[]{:S(2)}) async-start(bf16[16,48,1024]{2,1,0:T(8,128)(2,1)} %get-tuple-element.23), calls=%async_computation | async-start | bytes 3145728 | tf_op jit(solution)/shard_map/all_to_all | solution.py:349
  25.2 0.0 copy-done.1
  25.2 2.7 %collective-permute-start = (bf16[528,1024]{1,0:T(8,128)(2,1)S(1)}, bf16[528,1024]{1,0:T(8,128)(2,1)S(1)}, u32[]{:S(2)}, u32[]{:S(2)}) collective-permute-start(bf16[528,1024]{1,0:T(8,128)(2,1)S(1)} %copy-done.1), channel_id=1, source_target_pairs={{0,16},{1,17},{2,18},{3,19},{4,20},{5,21},{6,22},{7,23},{8,24},{9,... | collective-permute-start | bytes 3244040 | tf_op jit(solution)/shard_map/ppermute | solution.py:341
  27.9 1.9 %collective-permute-start.4 = (f32[64,512]{1,0:T(8,128)S(1)}, f32[64,512]{1,0:T(8,128)S(1)}, u32[]{:S(2)}, u32[]{:S(2)}) collective-permute-start(f32[64,512]{1,0:T(8,128)S(1)} %add.24), channel_id=1, source_target_pairs={{0,8},{1,9},{2,10},{3,11},{4,12},{5,13},{6,14},{7,15},{8,0},{9,1},... | collective-permute-start | bytes 393224 | tf_op jit(solution)/shard_map/ppermute | solution.py:312
  29.7 40.0 %collective-permute-done.4 = f32[64,512]{1,0:T(8,128)S(1)} collective-permute-done((f32[64,512]{1,0:T(8,128)S(1)}, f32[64,512]{1,0:T(8,128)S(1)}, u32[]{:S(2)}, u32[]{:S(2)}) %collective-permute-start.4) | collective-permute-done | bytes 131104 | tf_op jit(solution)/shard_map/ppermute | solution.py:312
  69.8 5.8 %collective-permute-done.rows_ref = bf16[528,1024]{1,0:T(8,128)(2,1)S(1)} collective-permute-done((bf16[528,1024]{1,0:T(8,128)(2,1)S(1)}, bf16[528,1024]{1,0:T(8,128)(2,1)S(1)}, u32[]{:S(2)}, u32[]{:S(2)}) %collective-permute-start) | collective-permute-done | bytes 1081376 | tf_op jit(solution)/shard_map/ppermute | solution.py:341
  75.5 2.4 %relay.1 = (bf16[16,48,1024]{2,1,0:T(8,128)(2,1)S(1)}, bf16[16,32,1024]{2,1,0:T(8,128)(2,1)}) custom-call(bf16[528,1024]{1,0:T(8,128)(2,1)S(1)} %collective-permute-done.rows_ref, bf16[16,16,1024]{2,1,0:T(8,128)(2,1)S(1)} %get-tuple-element.18.rest_ref), custom_call_target="tpu_custom_call" | custom-call | tf_op jit(solution)/shard_map/relay/pallas_call | solution.py:200
  77.9 0.0 all-to-all-done.own_ref
  77.9 25.7 %all_to_all.15.far_ref = bf16[16,48,1024]{2,1,0:T(8,128)(2,1)} all-to-all(bf16[16,48,1024]{2,1,0:T(8,128)(2,1)S(1)} %get-tuple-element.28), channel_id=1, replica_groups={{0,1,2,3,4,5,6,7,8,9,10,11,12,13,14,15},{16,17,18,19,20,21,22,23,24,25,..., dimensions={0} | all-to-all | bytes 3145728 | tf_op jit(solution)/shard_map/all_to_all | solution.py:357
  103.6 3.8 %all-to-all-start.1 = ((bf16[16,32,1024]{2,1,0:T(8,128)(2,1)}), bf16[16,32,1024]{2,1,0:T(8,128)(2,1)S(1)}, u32[]{:S(2)}, u32[]{:S(2)}) async-start(bf16[16,32,1024]{2,1,0:T(8,128)(2,1)} %get-tuple-element.25), calls=%async_computation.1 | async-start | bytes 2097152 | tf_op jit(solution)/shard_map/all_to_all | solution.py:358
  107.4 3.4 %collective-permute-start.5 = (f32[64,512]{1,0:T(8,128)S(1)}, f32[64,512]{1,0:T(8,128)S(1)}, u32[]{:S(2)}, u32[]{:S(2)}) collective-permute-start(f32[64,512]{1,0:T(8,128)S(1)} %add.25), channel_id=1, source_target_pairs={{0,16},{1,17},{2,18},{3,19},{4,20},{5,21},{6,22},{7,23},{8,24},{9,... | collective-permute-start | bytes 393224 | tf_op jit(solution)/shard_map/ppermute | solution.py:312
  110.8 0.1 places.1.place_ref
  110.9 0.0 copy-start.2
  110.9 0.6 copy-done.2
  111.5 10.8 %collective-permute-done.5 = f32[64,512]{1,0:T(8,128)S(1)} collective-permute-done((f32[64,512]{1,0:T(8,128)S(1)}, f32[64,512]{1,0:T(8,128)S(1)}, u32[]{:S(2)}, u32[]{:S(2)}) %collective-permute-start.5) | collective-permute-done | bytes 131104 | tf_op jit(solution)/shard_map/ppermute | solution.py:312
  122.3 0.7 add_divide_fusion.weight_ref
  123.0 17.6 %pairs.2.refs_0_ = f32[1,8192,255]{2,1,0:T(8,128)} custom-call(s32[64]{0:T(128)} %station_ref.3, s32[64]{0:T(128)} %count_ref.3, s32[2,1,64,128]{3,2,1,0:T(8,128)} %copy-done.2, bf16[16,48,1024]{2,1,0:T(8,128)(2,1)} %all-to-all-done.own_ref, bf16[16,48,1024]{2,1,0:T(8,128)(2,1)} %all_to_all.15.far_ref, f32[64,512]{1,0:T(8,128)} %add_divide_fusion.weight_ref, ...), custom_call_target="tpu_custom_call" | custom-call | flops 9663676416 | bytes 6266880 | tf_op jit(solution)/shard_map/pairs/pallas_call | solution.py:293
  140.6 0.0 all-to-all-done.1.own_ref.far_ref
  140.7 1.0 copy-done.4
  141.6 7.9 %pairs.3 = f32[1,8192,255]{2,1,0:T(8,128)} custom-call(s32[64]{0:T(128)} %station_ref.3, s32[64]{0:T(128)} %count_ref.3, s32[2,1,64,128]{3,2,1,0:T(8,128)} %copy-done.2, bf16[16,32,1024]{2,1,0:T(8,128)(2,1)} %copy-done.4, bf16[16,32,1024]{2,1,0:T(8,128)(2,1)} %copy-done.4, f32[64,512]{1,0:T(8,128)} %add_divide_fusion.weight_ref, ...), custom_call_target="tpu_custom_call", output_to_operand_aliasing={{}: (7, {})} | custom-call | flops 3221225472 | bytes 2088960 | tf_op jit(solution)/shard_map/pairs/pallas_call | solution.py:293
  (9 shorter events, 0.1 us)
Async XLA Ops:
  0.0 16.7 %copy-start.3 = (s32[32,64]{1,0:T(8,128)S(1)}, s32[32,64]{1,0:T(8,128)}, u32[]{:S(2)}) copy-start(s32[32,64]{1,0:T(8,128)} %index_ref.3) | copy-start | bytes 24580
  5.5 1.7 %collective-permute-start.1 = (f32[64,512]{1,0:T(8,128)}, f32[64,512]{1,0:T(8,128)S(1)}, u32[]{:S(2)}, u32[]{:S(2)}) collective-permute-start(f32[64,512]{1,0:T(8,128)} %get-tuple-element.22), channel_id=1, source_target_pairs={{0,1},{1,0},{2,3},{3,2},{4,5},{5,4},{6,7},{7,6},{8,9},{9,8},{10,11... | collective-permute-start | bytes 393224 | tf_op jit(solution)/shard_map/ppermute | solution.py:312
  8.1 6.7 %collective-permute-start.2 = (f32[64,512]{1,0:T(8,128)S(1)}, f32[64,512]{1,0:T(8,128)S(1)}, u32[]{:S(2)}, u32[]{:S(2)}) collective-permute-start(f32[64,512]{1,0:T(8,128)S(1)} %add.22), channel_id=1, source_target_pairs={{0,2},{1,3},{2,0},{3,1},{4,6},{5,7},{6,4},{7,5},{8,10},{9,11},{10,... | collective-permute-start | bytes 393224 | tf_op jit(solution)/shard_map/ppermute | solution.py:312
  14.9 5.6 %collective-permute-start.3 = (f32[64,512]{1,0:T(8,128)S(1)}, f32[64,512]{1,0:T(8,128)S(1)}, u32[]{:S(2)}, u32[]{:S(2)}) collective-permute-start(f32[64,512]{1,0:T(8,128)S(1)} %add.23), channel_id=1, source_target_pairs={{0,4},{1,5},{2,6},{3,7},{4,0},{5,1},{6,2},{7,3},{8,12},{9,13},{10,... | collective-permute-start | bytes 393224 | tf_op jit(solution)/shard_map/ppermute | solution.py:312
  16.7 1.2 copy-start
  20.5 4.7 %copy-start.1 = (bf16[528,1024]{1,0:T(8,128)(2,1)S(1)}, bf16[528,1024]{1,0:T(8,128)(2,1)}, u32[]{:S(2)}) copy-start(bf16[528,1024]{1,0:T(8,128)(2,1)} %get-tuple-element.17.rows_ref) | copy-start | bytes 3244036
  20.5 57.4 %all-to-all-start = ((bf16[16,48,1024]{2,1,0:T(8,128)(2,1)}), bf16[16,48,1024]{2,1,0:T(8,128)(2,1)}, u32[]{:S(2)}, u32[]{:S(2)}) async-start(bf16[16,48,1024]{2,1,0:T(8,128)(2,1)} %get-tuple-element.23), calls=%async_computation | async-start | bytes 3145728 | tf_op jit(solution)/shard_map/all_to_all | solution.py:349
  25.2 50.3 %collective-permute-start = (bf16[528,1024]{1,0:T(8,128)(2,1)S(1)}, bf16[528,1024]{1,0:T(8,128)(2,1)S(1)}, u32[]{:S(2)}, u32[]{:S(2)}) collective-permute-start(bf16[528,1024]{1,0:T(8,128)(2,1)S(1)} %copy-done.1), channel_id=1, source_target_pairs={{0,16},{1,17},{2,18},{3,19},{4,20},{5,21},{6,22},{7,23},{8,24},{9,... | collective-permute-start | bytes 3244040 | tf_op jit(solution)/shard_map/ppermute | solution.py:341
  27.9 41.9 %collective-permute-start.4 = (f32[64,512]{1,0:T(8,128)S(1)}, f32[64,512]{1,0:T(8,128)S(1)}, u32[]{:S(2)}, u32[]{:S(2)}) collective-permute-start(f32[64,512]{1,0:T(8,128)S(1)} %add.24), channel_id=1, source_target_pairs={{0,8},{1,9},{2,10},{3,11},{4,12},{5,13},{6,14},{7,15},{8,0},{9,1},... | collective-permute-start | bytes 393224 | tf_op jit(solution)/shard_map/ppermute | solution.py:312
  103.6 7.2 %copy-start.5 = (s32[2,8192]{1,0:T(2,128)S(1)}, s32[2,8192]{1,0:T(2,128)}, u32[]{:S(2)}) copy-start(s32[2,8192]{1,0:T(2,128)} %param.15) | copy-start | bytes 196612
  103.6 37.1 %all-to-all-start.1 = ((bf16[16,32,1024]{2,1,0:T(8,128)(2,1)}), bf16[16,32,1024]{2,1,0:T(8,128)(2,1)S(1)}, u32[]{:S(2)}, u32[]{:S(2)}) async-start(bf16[16,32,1024]{2,1,0:T(8,128)(2,1)} %get-tuple-element.25), calls=%async_computation.1 | async-start | bytes 2097152 | tf_op jit(solution)/shard_map/all_to_all | solution.py:358
  107.4 14.9 %collective-permute-start.5 = (f32[64,512]{1,0:T(8,128)S(1)}, f32[64,512]{1,0:T(8,128)S(1)}, u32[]{:S(2)}, u32[]{:S(2)}) collective-permute-start(f32[64,512]{1,0:T(8,128)S(1)} %add.25), channel_id=1, source_target_pairs={{0,16},{1,17},{2,18},{3,19},{4,20},{5,21},{6,22},{7,23},{8,24},{9,... | collective-permute-start | bytes 393224 | tf_op jit(solution)/shard_map/ppermute | solution.py:312
  110.9 0.6 copy-start.2
  140.7 1.0 copy-start.4

commit v7 on v6

--- a/solution.py
+++ b/solution.py
@@ -15,7 +15,6 @@
 LANES = 128
 SPLIT = (6, 2)
 TOGETHER = 2
-VMEM = 60 << 20
 SMALL = 20 << 20
 
 epsilon = 1e-06
@@ -113,6 +112,8 @@
     steps = 2 if ev_dev % 2 == 0 else 1
     events = ev_dev // steps
     total = ev_dev * stations + owners // 2
+    args = (windows, rotation.swapaxes(0, 1), source_inverse, table, send_rows)
+    args = [pltpu.with_memory_space_constraint(x, pltpu.HBM) for x in args]
     whole = lambda *shape: pl.BlockSpec(shape, lambda i, *_: (0,) * len(shape))
     return pl.pallas_call(
         partial(spectra_kernel, steps),
@@ -132,9 +133,9 @@
             jax.ShapeDtypeStruct((total, length), BF16),
             jax.ShapeDtypeStruct((stations, length // 2), F32),
         ],
-        compiler_params=pltpu.CompilerParams(vmem_limit_bytes=VMEM),
+        compiler_params=pltpu.CompilerParams(vmem_limit_bytes=SMALL),
         name="spectra",
-    )(half, windows, rotation.swapaxes(0, 1), source_inverse, table, send_rows)
+    )(half, *args)
 
 
 def pick_rows(index, rows, store):
@@ -300,7 +301,7 @@
         ),
         out_shape=jax.ShapeDtypeStruct((joint, cap * LANES, LAGS), F32),
         input_output_aliases=aliases,
-        compiler_params=pltpu.CompilerParams(vmem_limit_bytes=VMEM),
+        compiler_params=pltpu.CompilerParams(vmem_limit_bytes=SMALL),
         cost_estimate=pl.CostEstimate(
             flops=2 * macs, bytes_accessed=tiles * LANES * LAGS * 4, transcendentals=0
         ),
@@ -344,7 +345,6 @@
     while step < peers // 2:
         power = add_across(power, step, owners)
         step *= 2
-    send, power = lax.optimization_barrier((send, power))
     power = add_across(power, step, owners)
     own = to_peers(send)
     sends = relay_sends(swapped, rest, cap)
@@ -358,6 +358,7 @@
     last = to_peers(sends[1])
     run = partial(correlate, geo=geo, stations_of=tile_station, counts=tile_count, places=places)
     run = partial(run, weight=weight, lag_tab=lag_tab)
+    far = pltpu.with_memory_space_constraint(far, pltpu.HBM)
     result = run(0, sizes[0], own=(own, 0), far=(far, 0), previous=None)
     result = run(early, sizes[1], own=(last, 0), far=(last, sizes[1]), previous=result)
     return result.reshape(tiles_dev * LANES, LAGS)

time: 152 us -> 138 us (0.908)
  the two profiles are of different devices: /device:TPU:0 before, /device:TPU:8 now
where the time goes in v7:
time: 138 us
  waiting for transfers between devices  58.6 us (42%)
  Pallas kernels  32.2 us (23%)
  blocking collectives  25.4 us (18%)
  starting transfers between devices  19.4 us (14%)
  local copies, waits for them, and re-layouts  1.79 us (1%)
    ppermute x5, waiting for transfers between devices, add_across(): lax.ppermute(power, 'ev', [(i, i ^ step) for i in range(owners)])  54.4 us
    all_to_all x1, blocking collectives, shards(): far = to_peers(sends[0])  25.4 us
    pallas_call x2, Pallas kernels, correlate(): pl.pallas_call(partial(pair_kernel, geo, first), grid_spec=pltpu.Prefetch...  23.6 us
    ppermute x5, starting transfers between devices, add_across(): lax.ppermute(power, 'ev', [(i, i ^ step) for i in range(owners)])  6.47 us
    all_to_all x1, starting transfers between devices, shards(): own = to_peers(send)  5.2 us
    all_to_all x1, starting transfers between devices, shards(): last = to_peers(sends[1])  5.1 us
    pallas_call x1, Pallas kernels, event_rows(): pl.pallas_call(partial(spectra_kernel, steps), grid_spec=pltpu.PrefetchSc...  4.66 us
    ppermute x1, waiting for transfers between devices, shards(): swapped = lax.ppermute(rows, 'ev', across)  4.12 us
  transfers between devices with their start and end apart: 8, of which 6 were waited for; matrix products, arithmetic and copies ran while one was open for 0% of the time, Pallas kernels for 13%

profile of v7, /device:TPU:8, one launch (start us, length us, event | category | flops | bytes accessed | tf_op | source)
XLA Modules:
  0.0 137.6 jit_solution(16213794717594930943)
XLA Ops:
  0.0 4.7 %spectra.1 = (bf16[528,1024]{1,0:T(8,128)(2,1)S(1)}, f32[64,512]{1,0:T(8,128)S(1)}) custom-call(s32[1]{0:T(128)} %bitcast.half_ref, bf16[8,3,64,1024]{3,2,1,0:T(8,128)(2,1)} %win_ref.1, bf16[3,8,64]{2,1,0:T(8,128)(2,1)} %bitcast.10, bf16[8,1024]{1,0:T(8,128)(2,1)} %inv_ref.1, bf16[1024,1024]{1,0:T(8,128)(2,1)} %constant.36.table_ref, s32[32,64]{1,0:T(8,128)} %index_ref.3), custom_call_target="tpu_custom_call" | custom-call | tf_op jit(solution)/shard_map/spectra/pallas_call | solution.py:118
  4.7 0.0 copy-done.4
  4.7 2.5 %own.1 = (bf16[16,48,1024]{2,1,0:T(8,128)(2,1)}, bf16[16,16,1024]{2,1,0:T(8,128)(2,1)S(1)}) custom-call(s32[1]{0:T(128)} %bitcast.half_ref, bf16[528,1024]{1,0:T(8,128)(2,1)S(1)} %get-tuple-element.15.rows_ref, s32[32,64]{1,0:T(8,128)S(1)} %copy-done.4), custom_call_target="tpu_custom_call" | custom-call | tf_op jit(solution)/shard_map/own/pallas_call | solution.py:175
  7.2 0.8 copy-done.2
  8.0 5.2 %all-to-all-start = ((bf16[16,48,1024]{2,1,0:T(8,128)(2,1)}), bf16[16,48,1024]{2,1,0:T(8,128)(2,1)S(1)}, u32[]{:S(2)}, u32[]{:S(2)}) async-start(bf16[16,48,1024]{2,1,0:T(8,128)(2,1)} %get-tuple-element.19), calls=%async_computation | async-start | bytes 3145728 | tf_op jit(solution)/shard_map/all_to_all | solution.py:349
  13.2 2.7 %collective-permute-start = (bf16[528,1024]{1,0:T(8,128)(2,1)S(1)}, bf16[528,1024]{1,0:T(8,128)(2,1)S(1)}, u32[]{:S(2)}, u32[]{:S(2)}) collective-permute-start(bf16[528,1024]{1,0:T(8,128)(2,1)S(1)} %get-tuple-element.15.rows_ref), channel_id=1, source_target_pairs={{0,16},{1,17},{2,18},{3,19},{4,20},{5,21},{6,22},{7,23},{8,24},{9,... | collective-permute-start | bytes 3244040 | tf_op jit(solution)/shard_map/ppermute | solution.py:342
  15.9 0.0 collective-permute-start.1
  15.9 1.3 collective-permute-done.1
  17.2 1.5 %collective-permute-start.2 = (f32[64,512]{1,0:T(8,128)S(1)}, f32[64,512]{1,0:T(8,128)S(1)}, u32[]{:S(2)}, u32[]{:S(2)}) collective-permute-start(f32[64,512]{1,0:T(8,128)S(1)} %add.22), channel_id=1, source_target_pairs={{0,2},{1,3},{2,0},{3,1},{4,6},{5,7},{6,4},{7,5},{8,10},{9,11},{10,... | collective-permute-start | bytes 393224 | tf_op jit(solution)/shard_map/ppermute | solution.py:313
  18.8 18.1 %collective-permute-done.2 = f32[64,512]{1,0:T(8,128)S(1)} collective-permute-done((f32[64,512]{1,0:T(8,128)S(1)}, f32[64,512]{1,0:T(8,128)S(1)}, u32[]{:S(2)}, u32[]{:S(2)}) %collective-permute-start.2) | collective-permute-done | bytes 131104 | tf_op jit(solution)/shard_map/ppermute | solution.py:313
  36.9 1.5 %collective-permute-start.3 = (f32[64,512]{1,0:T(8,128)S(1)}, f32[64,512]{1,0:T(8,128)S(1)}, u32[]{:S(2)}, u32[]{:S(2)}) collective-permute-start(f32[64,512]{1,0:T(8,128)S(1)} %add.23), channel_id=1, source_target_pairs={{0,4},{1,5},{2,6},{3,7},{4,0},{5,1},{6,2},{7,3},{8,12},{9,13},{10,... | collective-permute-start | bytes 393224 | tf_op jit(solution)/shard_map/ppermute | solution.py:313
  38.4 4.0 %collective-permute-done.3 = f32[64,512]{1,0:T(8,128)S(1)} collective-permute-done((f32[64,512]{1,0:T(8,128)S(1)}, f32[64,512]{1,0:T(8,128)S(1)}, u32[]{:S(2)}, u32[]{:S(2)}) %collective-permute-start.3) | collective-permute-done | bytes 131104 | tf_op jit(solution)/shard_map/ppermute | solution.py:313
  42.5 0.1 collective-permute-start.4
  42.5 15.8 %collective-permute-done.4 = f32[64,512]{1,0:T(8,128)S(1)} collective-permute-done((f32[64,512]{1,0:T(8,128)S(1)}, f32[64,512]{1,0:T(8,128)S(1)}, u32[]{:S(2)}, u32[]{:S(2)}) %collective-permute-start.4) | collective-permute-done | bytes 131104 | tf_op jit(solution)/shard_map/ppermute | solution.py:313
  58.4 4.1 %collective-permute-done.rows_ref = bf16[528,1024]{1,0:T(8,128)(2,1)S(1)} collective-permute-done((bf16[528,1024]{1,0:T(8,128)(2,1)S(1)}, bf16[528,1024]{1,0:T(8,128)(2,1)S(1)}, u32[]{:S(2)}, u32[]{:S(2)}) %collective-permute-start) | collective-permute-done | bytes 1081376 | tf_op jit(solution)/shard_map/ppermute | solution.py:342
  62.5 0.0 copy-done.3
  62.5 1.4 %relay.1 = (bf16[16,48,1024]{2,1,0:T(8,128)(2,1)S(1)}, bf16[16,32,1024]{2,1,0:T(8,128)(2,1)S(1)}) custom-call(bf16[528,1024]{1,0:T(8,128)(2,1)S(1)} %collective-permute-done.rows_ref, bf16[16,16,1024]{2,1,0:T(8,128)(2,1)S(1)} %copy-done.3), custom_call_target="tpu_custom_call" | custom-call | tf_op jit(solution)/shard_map/relay/pallas_call | solution.py:201
  63.9 0.0 copy-start
  63.9 1.0 copy-done
  64.9 0.0 all-to-all-done.own_ref
  64.9 25.4 %all_to_all.15.far_ref = bf16[16,48,1024]{2,1,0:T(8,128)(2,1)} all-to-all(bf16[16,48,1024]{2,1,0:T(8,128)(2,1)S(1)} %get-tuple-element.24), channel_id=1, replica_groups={{0,1,2,3,4,5,6,7,8,9,10,11,12,13,14,15},{16,17,18,19,20,21,22,23,24,25,..., dimensions={0} | all-to-all | bytes 3145728 | tf_op jit(solution)/shard_map/all_to_all | solution.py:357
  90.3 5.1 %all-to-all-start.1 = ((bf16[16,32,1024]{2,1,0:T(8,128)(2,1)}), bf16[16,32,1024]{2,1,0:T(8,128)(2,1)S(1)}, u32[]{:S(2)}, u32[]{:S(2)}) async-start(bf16[16,32,1024]{2,1,0:T(8,128)(2,1)} %copy-done), calls=%async_computation.1 | async-start | bytes 2097152 | tf_op jit(solution)/shard_map/all_to_all | solution.py:358
  95.4 3.4 %collective-permute-start.5 = (f32[64,512]{1,0:T(8,128)S(1)}, f32[64,512]{1,0:T(8,128)S(1)}, u32[]{:S(2)}, u32[]{:S(2)}) collective-permute-start(f32[64,512]{1,0:T(8,128)S(1)} %add.25), channel_id=1, source_target_pairs={{0,16},{1,17},{2,18},{3,19},{4,20},{5,21},{6,22},{7,23},{8,24},{9,... | collective-permute-start | bytes 393224 | tf_op jit(solution)/shard_map/ppermute | solution.py:313
  98.7 0.0 copy-done.7
  98.7 0.1 places.1.place_ref
  98.8 15.1 %collective-permute-done.5 = f32[64,512]{1,0:T(8,128)S(1)} collective-permute-done((f32[64,512]{1,0:T(8,128)S(1)}, f32[64,512]{1,0:T(8,128)S(1)}, u32[]{:S(2)}, u32[]{:S(2)}) %collective-permute-start.5) | collective-permute-done | bytes 131104 | tf_op jit(solution)/shard_map/ppermute | solution.py:313
  114.0 0.0 copy-done.1
  114.0 0.0 copy-done.5
  114.0 0.0 copy-done.6
  114.0 17.1 %pairs.2.refs_0_ = f32[1,8192,255]{2,1,0:T(8,128)} custom-call(s32[64]{0:T(128)S(1)} %copy-done.5, s32[64]{0:T(128)S(1)} %copy-done.6, s32[2,1,64,128]{3,2,1,0:T(8,128)S(1)} %places.1.place_ref, bf16[16,48,1024]{2,1,0:T(8,128)(2,1)S(1)} %all-to-all-done.own_ref, bf16[16,48,1024]{2,1,0:T(8,128)(2,1)} %all_to_all.15.far_ref, ...), custom_call_target="tpu_custom_call" | custom-call | flops 9663676416 | bytes 6266880 | tf_op jit(solution)/shard_map/pairs/pallas_call | solution.py:294
  131.2 0.0 all-to-all-done.1.own_ref.far_ref
  131.2 6.5 %pairs.3 = f32[1,8192,255]{2,1,0:T(8,128)} custom-call(s32[64]{0:T(128)S(1)} %copy-done.5, s32[64]{0:T(128)S(1)} %copy-done.6, s32[2,1,64,128]{3,2,1,0:T(8,128)S(1)} %places.1.place_ref, bf16[16,32,1024]{2,1,0:T(8,128)(2,1)S(1)} %all-to-all-done.1.own_ref.far_ref, ...), custom_call_target="tpu_custom_call", output_to_operand_aliasing={{}: (7, {})} | custom-call | flops 3221225472 | bytes 2088960 | tf_op jit(solution)/shard_map/pairs/pallas_call | solution.py:294
  (13 shorter events, 0.1 us)
Async XLA Ops:
  0.0 4.7 %copy-start.4 = (s32[32,64]{1,0:T(8,128)S(1)}, s32[32,64]{1,0:T(8,128)}, u32[]{:S(2)}) copy-start(s32[32,64]{1,0:T(8,128)} %index_ref.3) | copy-start | bytes 24580
  7.2 0.8 copy-start.2
  8.0 56.9 %all-to-all-start = ((bf16[16,48,1024]{2,1,0:T(8,128)(2,1)}), bf16[16,48,1024]{2,1,0:T(8,128)(2,1)S(1)}, u32[]{:S(2)}, u32[]{:S(2)}) async-start(bf16[16,48,1024]{2,1,0:T(8,128)(2,1)} %get-tuple-element.19), calls=%async_computation | async-start | bytes 3145728 | tf_op jit(solution)/shard_map/all_to_all | solution.py:349
  13.2 49.3 %copy-start.3 = (bf16[16,16,1024]{2,1,0:T(8,128)(2,1)S(1)}, bf16[16,16,1024]{2,1,0:T(8,128)(2,1)}, u32[]{:S(2)}) copy-start(bf16[16,16,1024]{2,1,0:T(8,128)(2,1)} %copy-done.2) | copy-start | bytes 1572868
  13.2 49.3 %collective-permute-start = (bf16[528,1024]{1,0:T(8,128)(2,1)S(1)}, bf16[528,1024]{1,0:T(8,128)(2,1)S(1)}, u32[]{:S(2)}, u32[]{:S(2)}) collective-permute-start(bf16[528,1024]{1,0:T(8,128)(2,1)S(1)} %get-tuple-element.15.rows_ref), channel_id=1, source_target_pairs={{0,16},{1,17},{2,18},{3,19},{4,20},{5,21},{6,22},{7,23},{8,24},{9,... | collective-permute-start | bytes 3244040 | tf_op jit(solution)/shard_map/ppermute | solution.py:342
  15.9 1.3 collective-permute-start.1
  17.2 19.7 %collective-permute-start.2 = (f32[64,512]{1,0:T(8,128)S(1)}, f32[64,512]{1,0:T(8,128)S(1)}, u32[]{:S(2)}, u32[]{:S(2)}) collective-permute-start(f32[64,512]{1,0:T(8,128)S(1)} %add.22), channel_id=1, source_target_pairs={{0,2},{1,3},{2,0},{3,1},{4,6},{5,7},{6,4},{7,5},{8,10},{9,11},{10,... | collective-permute-start | bytes 393224 | tf_op jit(solution)/shard_map/ppermute | solution.py:313
  36.9 5.5 %collective-permute-start.3 = (f32[64,512]{1,0:T(8,128)S(1)}, f32[64,512]{1,0:T(8,128)S(1)}, u32[]{:S(2)}, u32[]{:S(2)}) collective-permute-start(f32[64,512]{1,0:T(8,128)S(1)} %add.23), channel_id=1, source_target_pairs={{0,4},{1,5},{2,6},{3,7},{4,0},{5,1},{6,2},{7,3},{8,12},{9,13},{10,... | collective-permute-start | bytes 393224 | tf_op jit(solution)/shard_map/ppermute | solution.py:313
  42.5 15.9 %collective-permute-start.4 = (f32[64,512]{1,0:T(8,128)S(1)}, f32[64,512]{1,0:T(8,128)S(1)}, u32[]{:S(2)}, u32[]{:S(2)}) collective-permute-start(f32[64,512]{1,0:T(8,128)S(1)} %add.24), channel_id=1, source_target_pairs={{0,8},{1,9},{2,10},{3,11},{4,12},{5,13},{6,14},{7,15},{8,0},{9,1},... | collective-permute-start | bytes 393224 | tf_op jit(solution)/shard_map/ppermute | solution.py:313
  63.9 1.0 copy-start
  90.2 8.5 %copy-start.7 = (s32[2,8192]{1,0:T(2,128)S(1)}, s32[2,8192]{1,0:T(2,128)}, u32[]{:S(2)}) copy-start(s32[2,8192]{1,0:T(2,128)} %param.15) | copy-start | bytes 196612
  90.2 23.7 %copy-start.1 = (bf16[1024,256]{1,0:T(8,128)(2,1)S(1)}, bf16[1024,256]{1,0:T(8,128)(2,1)}, u32[]{:S(2)}) copy-start(bf16[1024,256]{1,0:T(8,128)(2,1)} %constant.37.lag_ref) | copy-start | bytes 1572868
  90.2 23.8 %copy-start.5 = (s32[64]{0:T(128)S(1)}, s32[64]{0:T(128)}, u32[]{:S(2)}) copy-start(s32[64]{0:T(128)} %station_ref.3) | copy-start | bytes 772
  90.2 23.8 %copy-start.6 = (s32[64]{0:T(128)S(1)}, s32[64]{0:T(128)}, u32[]{:S(2)}) copy-start(s32[64]{0:T(128)} %count_ref.3) | copy-start | bytes 772
  90.3 40.9 %all-to-all-start.1 = ((bf16[16,32,1024]{2,1,0:T(8,128)(2,1)}), bf16[16,32,1024]{2,1,0:T(8,128)(2,1)S(1)}, u32[]{:S(2)}, u32[]{:S(2)}) async-start(bf16[16,32,1024]{2,1,0:T(8,128)(2,1)} %copy-done), calls=%async_computation.1 | async-start | bytes 2097152 | tf_op jit(solution)/shard_map/all_to_all | solution.py:358
  95.4 18.6 %collective-permute-start.5 = (f32[64,512]{1,0:T(8,128)S(1)}, f32[64,512]{1,0:T(8,128)S(1)}, u32[]{:S(2)}, u32[]{:S(2)}) collective-permute-start(f32[64,512]{1,0:T(8,128)S(1)} %add.25), channel_id=1, source_target_pairs={{0,16},{1,17},{2,18},{3,19},{4,20},{5,21},{6,22},{7,23},{8,24},{9,... | collective-permute-start | bytes 393224 | tf_op jit(solution)/shard_map/ppermute | solution.py:313

commit v8 on v7

--- a/solution.py
+++ b/solution.py
@@ -309,12 +309,12 @@
     )(stations_of, counts, *args)
 
 
-def add_across(power, step, owners):
-    return power + lax.ppermute(power, "ev", [(i, i ^ step) for i in range(owners)])
+def pair_up(value, step, owners):
+    return lax.ppermute(value, "ev", [(i, i ^ step) for i in range(owners)])
 
 
 def shards(windows, rotation, source_inverse, send_rows, tile_station, tile_count, pair_rows):
-    ev_dev, _, _, length = windows.shape
+    ev_dev, _, stations, length = windows.shape
     owners = lax.axis_size("ev")
     cap = send_rows.shape[1]
     tiles_dev = tile_station.shape[0]
@@ -341,15 +341,23 @@
     sizes = (early, groups - early)
     swapped = lax.ppermute(rows, "ev", across)
     send, rest = own_sends(half_arg, rows, send_rows, sizes)
-    step = 1
-    while step < peers // 2:
-        power = add_across(power, step, owners)
+    stations = power.shape[0]
+    share = stations // 2
+    low = lax.axis_index("ev") % 2 == 0
+    parts = power[:share], power[share:]
+    kept, passed = (jnp.where(low, *parts), jnp.where(low, *parts[::-1]))
+    part = kept + pair_up(passed, 1, owners)
+    step = 2
+    while step < peers:
+        part += pair_up(part, step, owners)
         step *= 2
-    power = add_across(power, step, owners)
     own = to_peers(send)
     sends = relay_sends(swapped, rest, cap)
-    sends, own, power = lax.optimization_barrier((sends, own, power))
-    power = add_across(power, peers, owners)
+    sends = [pltpu.with_memory_space_constraint(send, pltpu.HBM) for send in sends]
+    sends, own, part = lax.optimization_barrier((sends, own, part))
+    part += pair_up(part, peers, owners)
+    twin = pair_up(part, 1, owners)
+    power = jnp.concatenate([jnp.where(low, part, twin), jnp.where(low, twin, part)], axis=0)
     weight = 1.0 / (power / (ev_dev * owners) + epsilon)
     places = place_rows(half_arg, pair_rows.reshape(2, joint, cap, LANES), peers)
     lag_tab = lag_table(length, LAGS, LAGS + 1)

time: 138 us -> 145 us (1.051)
  the two profiles are of different devices: /device:TPU:8 before, /device:TPU:9 now
where the time goes in v8:
time: 145 us; the launch traced here: 144 us
  waiting for transfers between devices  57.9 us (40%)
  Pallas kernels  33.2 us (23%)
  blocking collectives  25.4 us (18%)
  starting transfers between devices  20.5 us (14%)
  local copies, waits for them, and re-layouts  7.1 us (5%)
    ppermute x6, waiting for transfers between devices, pair_up(): return lax.ppermute(value, 'ev', [(i, i ^ step) for i in range(owners)])  52.8 us
    all_to_all x1, blocking collectives, shards(): far = to_peers(sends[0])  25.4 us
    pallas_call x2, Pallas kernels, correlate(): pl.pallas_call(partial(pair_kernel, geo, first), grid_spec=pltpu.Prefetch...  24.6 us
    unnamed x25, local copies, waits for them, and re-layouts  7.1 us
    ppermute x6, starting transfers between devices, pair_up(): return lax.ppermute(value, 'ev', [(i, i ^ step) for i in range(owners)])  6.77 us
    all_to_all x1, starting transfers between devices, shards(): last = to_peers(sends[1])  5.98 us
    all_to_all x1, starting transfers between devices, shards(): own = to_peers(send)  5.47 us
    ppermute x1, waiting for transfers between devices, shards(): swapped = lax.ppermute(rows, 'ev', across)  5.12 us
  transfers between devices with their start and end apart: 9, of which 7 were waited for; matrix products, arithmetic and copies ran while one was open for 0% of the time, Pallas kernels for 13%

profile of v8, /device:TPU:9, one launch (start us, length us, event | category | flops | bytes accessed | tf_op | source)
XLA Modules:
  0.0 144.3 jit_solution(13167826380804475669)
XLA Ops:
  0.0 4.7 %spectra.1 = (bf16[528,1024]{1,0:T(8,128)(2,1)S(1)}, f32[64,512]{1,0:T(8,128)S(1)}) custom-call(s32[1]{0:T(128)} %bitcast.half_ref, bf16[8,3,64,1024]{3,2,1,0:T(8,128)(2,1)} %win_ref.1, bf16[3,8,64]{2,1,0:T(8,128)(2,1)} %bitcast.10, bf16[8,1024]{1,0:T(8,128)(2,1)} %inv_ref.1, bf16[1024,1024]{1,0:T(8,128)(2,1)} %constant.48.table_ref, s32[32,64]{1,0:T(8,128)} %index_ref.3), custom_call_target="tpu_custom_call" | custom-call | tf_op jit(solution)/shard_map/spectra/pallas_call | solution.py:118
  4.7 2.5 %own.1 = (bf16[16,48,1024]{2,1,0:T(8,128)(2,1)}, bf16[16,16,1024]{2,1,0:T(8,128)(2,1)S(1)}) custom-call(s32[1]{0:T(128)} %bitcast.half_ref, bf16[528,1024]{1,0:T(8,128)(2,1)S(1)} %get-tuple-element.15.rows_ref, s32[32,64]{1,0:T(8,128)S(1)} %copy-done.7), custom_call_target="tpu_custom_call" | custom-call | tf_op jit(solution)/shard_map/own/pallas_call | solution.py:175
  7.2 1.0 copy-done.2
  8.2 0.8 copy-done.5
  9.0 5.5 %all-to-all-start = ((bf16[16,48,1024]{2,1,0:T(8,128)(2,1)}), bf16[16,48,1024]{2,1,0:T(8,128)(2,1)S(1)}, u32[]{:S(2)}, u32[]{:S(2)}) async-start(bf16[16,48,1024]{2,1,0:T(8,128)(2,1)} %get-tuple-element.19), calls=%async_computation | async-start | bytes 3145728 | tf_op jit(solution)/shard_map/all_to_all | solution.py:354
  14.5 2.3 %collective-permute-start = (bf16[528,1024]{1,0:T(8,128)(2,1)}, bf16[528,1024]{1,0:T(8,128)(2,1)S(1)}, u32[]{:S(2)}, u32[]{:S(2)}) collective-permute-start(bf16[528,1024]{1,0:T(8,128)(2,1)} %copy-done.2), channel_id=1, source_target_pairs={{0,16},{1,17},{2,18},{3,19},{4,20},{5,21},{6,22},{7,23},{8,24},{9,... | collective-permute-start | bytes 3244040 | tf_op jit(solution)/shard_map/ppermute | solution.py:342
  16.8 0.7 collective-permute-start.1
  17.6 0.9 collective-permute-done.1
  18.5 1.2 collective-permute-start.2
  19.7 17.0 %collective-permute-done.2 = f32[32,512]{1,0:T(8,128)S(1)} collective-permute-done((f32[32,512]{1,0:T(8,128)S(1)}, f32[32,512]{1,0:T(8,128)S(1)}, u32[]{:S(2)}, u32[]{:S(2)}) %collective-permute-start.2) | collective-permute-done | bytes 65568 | tf_op jit(solution)/shard_map/ppermute | solution.py:313
  36.8 0.7 collective-permute-start.3
  37.5 2.8 %collective-permute-done.3 = f32[32,512]{1,0:T(8,128)S(1)} collective-permute-done((f32[32,512]{1,0:T(8,128)S(1)}, f32[32,512]{1,0:T(8,128)S(1)}, u32[]{:S(2)}, u32[]{:S(2)}) %collective-permute-start.3) | collective-permute-done | bytes 65568 | tf_op jit(solution)/shard_map/ppermute | solution.py:313
  40.3 0.1 collective-permute-start.4
  40.3 17.7 %collective-permute-done.4 = f32[32,512]{1,0:T(8,128)S(1)} collective-permute-done((f32[32,512]{1,0:T(8,128)S(1)}, f32[32,512]{1,0:T(8,128)S(1)}, u32[]{:S(2)}, u32[]{:S(2)}) %collective-permute-start.4) | collective-permute-done | bytes 65568 | tf_op jit(solution)/shard_map/ppermute | solution.py:313
  58.1 5.1 %collective-permute-done.rows_ref = bf16[528,1024]{1,0:T(8,128)(2,1)S(1)} collective-permute-done((bf16[528,1024]{1,0:T(8,128)(2,1)}, bf16[528,1024]{1,0:T(8,128)(2,1)S(1)}, u32[]{:S(2)}, u32[]{:S(2)}) %collective-permute-start) | collective-permute-done | bytes 1081376 | tf_op jit(solution)/shard_map/ppermute | solution.py:342
  63.2 1.0 copy-done
  64.2 1.2 copy-done.1
  65.4 1.0 copy-done.6
  66.5 1.4 relay.1
  67.9 1.0 copy-done.3
  68.8 0.0 all-to-all-done.own_ref
  68.8 25.4 %all_to_all.15.far_ref = bf16[16,48,1024]{2,1,0:T(8,128)(2,1)} all-to-all(bf16[16,48,1024]{2,1,0:T(8,128)(2,1)S(1)} %get-tuple-element.24), channel_id=1, replica_groups={{0,1,2,3,4,5,6,7,8,9,10,11,12,13,14,15},{16,17,18,19,20,21,22,23,24,25,..., dimensions={0} | all-to-all | bytes 3145728 | tf_op jit(solution)/shard_map/all_to_all | solution.py:365
  94.2 6.0 %all-to-all-start.1 = ((bf16[16,32,1024]{2,1,0:T(8,128)(2,1)}), bf16[16,32,1024]{2,1,0:T(8,128)(2,1)S(1)}, u32[]{:S(2)}, u32[]{:S(2)}) async-start(bf16[16,32,1024]{2,1,0:T(8,128)(2,1)} %copy-done.3), calls=%async_computation.1 | async-start | bytes 2097152 | tf_op jit(solution)/shard_map/all_to_all | solution.py:366
  100.2 3.0 %collective-permute-start.5 = (f32[32,512]{1,0:T(8,128)S(1)}, f32[32,512]{1,0:T(8,128)S(1)}, u32[]{:S(2)}, u32[]{:S(2)}) collective-permute-start(f32[32,512]{1,0:T(8,128)S(1)} %add.30), channel_id=1, source_target_pairs={{0,16},{1,17},{2,18},{3,19},{4,20},{5,21},{6,22},{7,23},{8,24},{9,... | collective-permute-start | bytes 196616 | tf_op jit(solution)/shard_map/ppermute | solution.py:313
  103.2 13.5 %collective-permute-done.5 = f32[32,512]{1,0:T(8,128)S(1)} collective-permute-done((f32[32,512]{1,0:T(8,128)S(1)}, f32[32,512]{1,0:T(8,128)S(1)}, u32[]{:S(2)}, u32[]{:S(2)}) %collective-permute-start.5) | collective-permute-done | bytes 65568 | tf_op jit(solution)/shard_map/ppermute | solution.py:313
  116.7 1.0 collective-permute-start.6
  117.8 0.1 places.1.place_ref
  117.8 0.8 collective-permute-done.6
  118.7 17.1 %pairs.2.refs_0_ = f32[1,8192,255]{2,1,0:T(8,128)} custom-call(s32[64]{0:T(128)S(1)} %copy-done.8, s32[64]{0:T(128)S(1)} %copy-done.9, s32[2,1,64,128]{3,2,1,0:T(8,128)S(1)} %places.1.place_ref, bf16[16,48,1024]{2,1,0:T(8,128)(2,1)S(1)} %all-to-all-done.own_ref, bf16[16,48,1024]{2,1,0:T(8,128)(2,1)} %all_to_all.15.far_ref, f32[64,512]{1,0:T(8,128)S(1)} %fusion.1.weight_ref, ...), custom_call_target="tpu_custom_call" | custom-call | flops 9663676416 | bytes 6266880 | tf_op jit(solution)/shard_map/pairs/pallas_call | solution.py:294
  135.9 0.0 all-to-all-done.1.own_ref.far_ref
  135.9 1.0 copy-done.10
  136.9 7.4 %pairs.3 = f32[1,8192,255]{2,1,0:T(8,128)} custom-call(s32[64]{0:T(128)S(1)} %copy-done.8, s32[64]{0:T(128)S(1)} %copy-done.9, s32[2,1,64,128]{3,2,1,0:T(8,128)S(1)} %places.1.place_ref, bf16[16,32,1024]{2,1,0:T(8,128)(2,1)} %copy-done.10, bf16[16,32,1024]{2,1,0:T(8,128)(2,1)} %copy-done.10, ...), custom_call_target="tpu_custom_call", output_to_operand_aliasing={{}: (7, {})} | custom-call | flops 3221225472 | bytes 2088960 | tf_op jit(solution)/shard_map/pairs/pallas_call | solution.py:294
  (26 shorter events, 0.1 us)
Async XLA Ops:
  0.0 4.7 %copy-start.7 = (s32[32,64]{1,0:T(8,128)S(1)}, s32[32,64]{1,0:T(8,128)}, u32[]{:S(2)}) copy-start(s32[32,64]{1,0:T(8,128)} %index_ref.3) | copy-start | bytes 24580
  7.2 1.0 copy-start.2
  8.2 0.8 copy-start.5
  9.0 59.8 %all-to-all-start = ((bf16[16,48,1024]{2,1,0:T(8,128)(2,1)}), bf16[16,48,1024]{2,1,0:T(8,128)(2,1)S(1)}, u32[]{:S(2)}, u32[]{:S(2)}) async-start(bf16[16,48,1024]{2,1,0:T(8,128)(2,1)} %get-tuple-element.19), calls=%async_computation | async-start | bytes 3145728 | tf_op jit(solution)/shard_map/all_to_all | solution.py:354
  14.5 48.7 %collective-permute-start = (bf16[528,1024]{1,0:T(8,128)(2,1)}, bf16[528,1024]{1,0:T(8,128)(2,1)S(1)}, u32[]{:S(2)}, u32[]{:S(2)}) collective-permute-start(bf16[528,1024]{1,0:T(8,128)(2,1)} %copy-done.2), channel_id=1, source_target_pairs={{0,16},{1,17},{2,18},{3,19},{4,20},{5,21},{6,22},{7,23},{8,24},{9,... | collective-permute-start | bytes 3244040 | tf_op jit(solution)/shard_map/ppermute | solution.py:342
  16.8 1.6 %collective-permute-start.1 = (f32[32,512]{1,0:T(8,128)S(1)}, f32[32,512]{1,0:T(8,128)S(1)}, u32[]{:S(2)}, u32[]{:S(2)}) collective-permute-start(f32[32,512]{1,0:T(8,128)S(1)} %slice_select_fusion), channel_id=1, source_target_pairs={{0,1},{1,0},{2,3},{3,2},{4,5},{5,4},{6,7},{7,6},{8,9},{9,8},{10,11... | collective-permute-start | bytes 196616 | tf_op jit(solution)/shard_map/ppermute | solution.py:313
  18.5 18.3 %collective-permute-start.2 = (f32[32,512]{1,0:T(8,128)S(1)}, f32[32,512]{1,0:T(8,128)S(1)}, u32[]{:S(2)}, u32[]{:S(2)}) collective-permute-start(f32[32,512]{1,0:T(8,128)S(1)} %select_add_fusion), channel_id=1, source_target_pairs={{0,2},{1,3},{2,0},{3,1},{4,6},{5,7},{6,4},{7,5},{8,10},{9,11},{10,... | collective-permute-start | bytes 196616 | tf_op jit(solution)/shard_map/ppermute | solution.py:313
  36.8 3.5 %collective-permute-start.3 = (f32[32,512]{1,0:T(8,128)S(1)}, f32[32,512]{1,0:T(8,128)S(1)}, u32[]{:S(2)}, u32[]{:S(2)}) collective-permute-start(f32[32,512]{1,0:T(8,128)S(1)} %add.28), channel_id=1, source_target_pairs={{0,4},{1,5},{2,6},{3,7},{4,0},{5,1},{6,2},{7,3},{8,12},{9,13},{10,... | collective-permute-start | bytes 196616 | tf_op jit(solution)/shard_map/ppermute | solution.py:313
  40.3 17.8 %collective-permute-start.4 = (f32[32,512]{1,0:T(8,128)S(1)}, f32[32,512]{1,0:T(8,128)S(1)}, u32[]{:S(2)}, u32[]{:S(2)}) collective-permute-start(f32[32,512]{1,0:T(8,128)S(1)} %add.29), channel_id=1, source_target_pairs={{0,8},{1,9},{2,10},{3,11},{4,12},{5,13},{6,14},{7,15},{8,0},{9,1},... | collective-permute-start | bytes 196616 | tf_op jit(solution)/shard_map/ppermute | solution.py:313
  63.2 1.0 copy-start
  64.2 1.2 copy-start.1
  65.4 1.0 copy-start.6
  67.9 1.0 copy-start.3
  94.2 23.5 %copy-start.11 = (s32[2,8192]{1,0:T(2,128)S(1)}, s32[2,8192]{1,0:T(2,128)}, u32[]{:S(2)}) copy-start(s32[2,8192]{1,0:T(2,128)} %param.15) | copy-start | bytes 196612
  94.2 24.5 %copy-start.4 = (bf16[1024,256]{1,0:T(8,128)(2,1)S(1)}, bf16[1024,256]{1,0:T(8,128)(2,1)}, u32[]{:S(2)}) copy-start(bf16[1024,256]{1,0:T(8,128)(2,1)} %constant.49.lag_ref) | copy-start | bytes 1572868
  94.2 24.5 %copy-start.8 = (s32[64]{0:T(128)S(1)}, s32[64]{0:T(128)}, u32[]{:S(2)}) copy-start(s32[64]{0:T(128)} %station_ref.3) | copy-start | bytes 772
  94.2 24.5 %copy-start.9 = (s32[64]{0:T(128)S(1)}, s32[64]{0:T(128)}, u32[]{:S(2)}) copy-start(s32[64]{0:T(128)} %count_ref.3) | copy-start | bytes 772
  94.2 41.7 %all-to-all-start.1 = ((bf16[16,32,1024]{2,1,0:T(8,128)(2,1)}), bf16[16,32,1024]{2,1,0:T(8,128)(2,1)S(1)}, u32[]{:S(2)}, u32[]{:S(2)}) async-start(bf16[16,32,1024]{2,1,0:T(8,128)(2,1)} %copy-done.3), calls=%async_computation.1 | async-start | bytes 2097152 | tf_op jit(solution)/shard_map/all_to_all | solution.py:366
  100.2 16.5 %collective-permute-start.5 = (f32[32,512]{1,0:T(8,128)S(1)}, f32[32,512]{1,0:T(8,128)S(1)}, u32[]{:S(2)}, u32[]{:S(2)}) collective-permute-start(f32[32,512]{1,0:T(8,128)S(1)} %add.30), channel_id=1, source_target_pairs={{0,16},{1,17},{2,18},{3,19},{4,20},{5,21},{6,22},{7,23},{8,24},{9,... | collective-permute-start | bytes 196616 | tf_op jit(solution)/shard_map/ppermute | solution.py:313
  116.7 1.9 %collective-permute-start.6 = (f32[32,512]{1,0:T(8,128)S(1)}, f32[32,512]{1,0:T(8,128)S(1)}, u32[]{:S(2)}, u32[]{:S(2)}) collective-permute-start(f32[32,512]{1,0:T(8,128)S(1)} %add.31), channel_id=1, source_target_pairs={{0,1},{1,0},{2,3},{3,2},{4,5},{5,4},{6,7},{7,6},{8,9},{9,8},{10,11... | collective-permute-start | bytes 196616 | tf_op jit(solution)/shard_map/ppermute | solution.py:313
  135.9 1.0 copy-start.10

commit v9 on v8

--- a/solution.py
+++ b/solution.py
@@ -14,7 +14,7 @@
 SUB = 8
 LANES = 128
 SPLIT = (6, 2)
-TOGETHER = 2
+TOGETHER = 8
 SMALL = 20 << 20
 
 epsilon = 1e-06
@@ -109,7 +109,7 @@
 def event_rows(half, windows, rotation, source_inverse, send_rows, table):
     ev_dev, comps, stations, length = windows.shape
     owners, cap = send_rows.shape
-    steps = 2 if ev_dev % 2 == 0 else 1
+    steps = 4 if ev_dev % 4 == 0 else 1
     events = ev_dev // steps
     total = ev_dev * stations + owners // 2
     args = (windows, rotation.swapaxes(0, 1), source_inverse, table, send_rows)
@@ -263,7 +263,13 @@
                     )
                 )
             cross = jnp.concatenate(halves, axis=0)
-            lagged = jnp.dot(cross, lag_ref[...], preferred_element_type=F32)
+            lagged = jnp.concatenate(
+                [
+                    jnp.dot(piece, lag_ref[...], preferred_element_type=F32)
+                    for piece in (cross[: many // 2], cross[many // 2 :])
+                ],
+                axis=0,
+            )
             for n in range(TOGETHER):
                 tile = j * cap + group * SUB + i + n
                 piece = lagged[n * LANES : (n + 1) * LANES]
@@ -353,7 +359,6 @@
         step *= 2
     own = to_peers(send)
     sends = relay_sends(swapped, rest, cap)
-    sends = [pltpu.with_memory_space_constraint(send, pltpu.HBM) for send in sends]
     sends, own, part = lax.optimization_barrier((sends, own, part))
     part += pair_up(part, peers, owners)
     twin = pair_up(part, 1, owners)

time: 145 us -> 140 us (0.966)
  Pallas kernels: 33.2 us -> 29.8 us
    pallas_call x2, Pallas kernels: 24.6 us -> 20.7 us  [correlate(): pl.pallas_call(partial(pair_kernel, geo, first), grid_spec=pltpu.Prefetch...]
    unnamed x25 -> x23, local copies, waits for them, and re-layouts: 7.1 us -> 6.11 us
  transfers between devices with their start and end apart: 9 -> 9, of which waited for: 7 -> 7; matrix products, arithmetic and copies ran while one was open for 0% -> 0% of each run, Pallas kernels for 13% -> 12%
where the time goes in v9:
time: 140 us
  waiting for transfers between devices  57.9 us (41%)
  Pallas kernels  29.8 us (21%)
  blocking collectives  25.4 us (18%)
  starting transfers between devices  20.5 us (15%)
  local copies, waits for them, and re-layouts  6.11 us (4%)
    ppermute x6, waiting for transfers between devices, pair_up(): return lax.ppermute(value, 'ev', [(i, i ^ step) for i in range(owners)])  52.7 us
    all_to_all x1, blocking collectives, shards(): far = to_peers(sends[0])  25.4 us
    pallas_call x2, Pallas kernels, correlate(): pl.pallas_call(partial(pair_kernel, geo, first), grid_spec=pltpu.Prefetch...  20.7 us
    ppermute x6, starting transfers between devices, pair_up(): return lax.ppermute(value, 'ev', [(i, i ^ step) for i in range(owners)])  6.77 us
    unnamed x23, local copies, waits for them, and re-layouts  6.11 us
    all_to_all x1, starting transfers between devices, shards(): last = to_peers(sends[1])  5.98 us
    all_to_all x1, starting transfers between devices, shards(): own = to_peers(send)  5.48 us
    pallas_call x1, Pallas kernels, event_rows(): pl.pallas_call(partial(spectra_kernel, steps), grid_spec=pltpu.PrefetchSc...  5.16 us
  transfers between devices with their start and end apart: 9, of which 7 were waited for; matrix products, arithmetic and copies ran while one was open for 0% of the time, Pallas kernels for 12%

profile of v9, /device:TPU:9, one launch (start us, length us, event | category | flops | bytes accessed | tf_op | source)
XLA Modules:
  0.0 139.9 jit_solution(2352941968726896305)
XLA Ops:
  0.0 5.2 %spectra.1 = (bf16[528,1024]{1,0:T(8,128)(2,1)S(1)}, f32[64,512]{1,0:T(8,128)S(1)}) custom-call(s32[1]{0:T(128)} %bitcast.half_ref, bf16[8,3,64,1024]{3,2,1,0:T(8,128)(2,1)} %win_ref.1, bf16[3,8,64]{2,1,0:T(8,128)(2,1)} %bitcast.10, bf16[8,1024]{1,0:T(8,128)(2,1)} %inv_ref.1, bf16[1024,1024]{1,0:T(8,128)(2,1)} %constant.48.table_ref, s32[32,64]{1,0:T(8,128)} %index_ref.3), custom_call_target="tpu_custom_call" | custom-call | tf_op jit(solution)/shard_map/spectra/pallas_call | solution.py:118
  5.2 2.5 %own.1 = (bf16[16,48,1024]{2,1,0:T(8,128)(2,1)}, bf16[16,16,1024]{2,1,0:T(8,128)(2,1)S(1)}) custom-call(s32[1]{0:T(128)} %bitcast.half_ref, bf16[528,1024]{1,0:T(8,128)(2,1)S(1)} %get-tuple-element.15.rows_ref, s32[32,64]{1,0:T(8,128)S(1)} %copy-done.7), custom_call_target="tpu_custom_call" | custom-call | tf_op jit(solution)/shard_map/own/pallas_call | solution.py:175
  7.7 1.0 copy-done.2
  8.7 0.8 copy-done.5
  9.5 5.5 %all-to-all-start = ((bf16[16,48,1024]{2,1,0:T(8,128)(2,1)}), bf16[16,48,1024]{2,1,0:T(8,128)(2,1)S(1)}, u32[]{:S(2)}, u32[]{:S(2)}) async-start(bf16[16,48,1024]{2,1,0:T(8,128)(2,1)} %get-tuple-element.19), calls=%async_computation | async-start | bytes 3145728 | tf_op jit(solution)/shard_map/all_to_all | solution.py:360
  15.0 2.3 %collective-permute-start = (bf16[528,1024]{1,0:T(8,128)(2,1)}, bf16[528,1024]{1,0:T(8,128)(2,1)S(1)}, u32[]{:S(2)}, u32[]{:S(2)}) collective-permute-start(bf16[528,1024]{1,0:T(8,128)(2,1)} %copy-done.2), channel_id=1, source_target_pairs={{0,16},{1,17},{2,18},{3,19},{4,20},{5,21},{6,22},{7,23},{8,24},{9,... | collective-permute-start | bytes 3244040 | tf_op jit(solution)/shard_map/ppermute | solution.py:348
  17.3 0.7 collective-permute-start.1
  18.1 0.9 collective-permute-done.1
  19.0 1.2 collective-permute-start.2
  20.2 17.0 %collective-permute-done.2 = f32[32,512]{1,0:T(8,128)S(1)} collective-permute-done((f32[32,512]{1,0:T(8,128)S(1)}, f32[32,512]{1,0:T(8,128)S(1)}, u32[]{:S(2)}, u32[]{:S(2)}) %collective-permute-start.2) | collective-permute-done | bytes 65568 | tf_op jit(solution)/shard_map/ppermute | solution.py:319
  37.3 0.7 collective-permute-start.3
  37.9 2.8 %collective-permute-done.3 = f32[32,512]{1,0:T(8,128)S(1)} collective-permute-done((f32[32,512]{1,0:T(8,128)S(1)}, f32[32,512]{1,0:T(8,128)S(1)}, u32[]{:S(2)}, u32[]{:S(2)}) %collective-permute-start.3) | collective-permute-done | bytes 65568 | tf_op jit(solution)/shard_map/ppermute | solution.py:319
  40.8 0.1 collective-permute-start.4
  40.8 17.7 %collective-permute-done.4 = f32[32,512]{1,0:T(8,128)S(1)} collective-permute-done((f32[32,512]{1,0:T(8,128)S(1)}, f32[32,512]{1,0:T(8,128)S(1)}, u32[]{:S(2)}, u32[]{:S(2)}) %collective-permute-start.4) | collective-permute-done | bytes 65568 | tf_op jit(solution)/shard_map/ppermute | solution.py:319
  58.6 5.1 %collective-permute-done.rows_ref = bf16[528,1024]{1,0:T(8,128)(2,1)S(1)} collective-permute-done((bf16[528,1024]{1,0:T(8,128)(2,1)}, bf16[528,1024]{1,0:T(8,128)(2,1)S(1)}, u32[]{:S(2)}, u32[]{:S(2)}) %collective-permute-start) | collective-permute-done | bytes 1081376 | tf_op jit(solution)/shard_map/ppermute | solution.py:348
  63.7 1.0 copy-done
  64.7 1.2 copy-done.1
  65.9 1.0 copy-done.6
  67.0 1.4 relay.1
  68.4 1.0 copy-done.3
  69.3 0.0 all-to-all-done.own_ref
  69.3 25.4 %all_to_all.15.far_ref = bf16[16,48,1024]{2,1,0:T(8,128)(2,1)} all-to-all(bf16[16,48,1024]{2,1,0:T(8,128)(2,1)S(1)} %get-tuple-element.24), channel_id=1, replica_groups={{0,1,2,3,4,5,6,7,8,9,10,11,12,13,14,15},{16,17,18,19,20,21,22,23,24,25,..., dimensions={0} | all-to-all | bytes 3145728 | tf_op jit(solution)/shard_map/all_to_all | solution.py:370
  94.7 6.0 %all-to-all-start.1 = ((bf16[16,32,1024]{2,1,0:T(8,128)(2,1)}), bf16[16,32,1024]{2,1,0:T(8,128)(2,1)S(1)}, u32[]{:S(2)}, u32[]{:S(2)}) async-start(bf16[16,32,1024]{2,1,0:T(8,128)(2,1)} %copy-done.3), calls=%async_computation.1 | async-start | bytes 2097152 | tf_op jit(solution)/shard_map/all_to_all | solution.py:371
  100.7 3.0 %collective-permute-start.5 = (f32[32,512]{1,0:T(8,128)S(1)}, f32[32,512]{1,0:T(8,128)S(1)}, u32[]{:S(2)}, u32[]{:S(2)}) collective-permute-start(f32[32,512]{1,0:T(8,128)S(1)} %add.30), channel_id=1, source_target_pairs={{0,16},{1,17},{2,18},{3,19},{4,20},{5,21},{6,22},{7,23},{8,24},{9,... | collective-permute-start | bytes 196616 | tf_op jit(solution)/shard_map/ppermute | solution.py:319
  103.7 13.5 %collective-permute-done.5 = f32[32,512]{1,0:T(8,128)S(1)} collective-permute-done((f32[32,512]{1,0:T(8,128)S(1)}, f32[32,512]{1,0:T(8,128)S(1)}, u32[]{:S(2)}, u32[]{:S(2)}) %collective-permute-start.5) | collective-permute-done | bytes 65568 | tf_op jit(solution)/shard_map/ppermute | solution.py:319
  117.2 1.0 collective-permute-start.6
  118.3 0.0 copy-done.10
  118.3 0.1 places.1.place_ref
  118.3 0.8 collective-permute-done.6
  119.2 14.9 %pairs.2.refs_0_ = f32[1,8192,255]{2,1,0:T(8,128)} custom-call(s32[64]{0:T(128)S(1)} %copy-done.8, s32[64]{0:T(128)S(1)} %copy-done.9, s32[2,1,64,128]{3,2,1,0:T(8,128)S(1)} %places.1.place_ref, bf16[16,48,1024]{2,1,0:T(8,128)(2,1)S(1)} %all-to-all-done.own_ref, bf16[16,48,1024]{2,1,0:T(8,128)(2,1)} %all_to_all.15.far_ref, f32[64,512]{1,0:T(8,128)S(1)} %fusion.1.weight_ref, ...), custom_call_target="tpu_custom_call" | custom-call | flops 9663676416 | bytes 6266880 | tf_op jit(solution)/shard_map/pairs/pallas_call | solution.py:300
  134.2 0.0 all-to-all-done.1.own_ref.far_ref
  134.2 5.7 %pairs.3 = f32[1,8192,255]{2,1,0:T(8,128)} custom-call(s32[64]{0:T(128)S(1)} %copy-done.8, s32[64]{0:T(128)S(1)} %copy-done.9, s32[2,1,64,128]{3,2,1,0:T(8,128)S(1)} %places.1.place_ref, bf16[16,32,1024]{2,1,0:T(8,128)(2,1)S(1)} %all-to-all-done.1.own_ref.far_ref, ...), custom_call_target="tpu_custom_call", output_to_operand_aliasing={{}: (7, {})} | custom-call | flops 3221225472 | bytes 2088960 | tf_op jit(solution)/shard_map/pairs/pallas_call | solution.py:300
  (24 shorter events, 0.1 us)
Async XLA Ops:
  0.0 5.2 %copy-start.7 = (s32[32,64]{1,0:T(8,128)S(1)}, s32[32,64]{1,0:T(8,128)}, u32[]{:S(2)}) copy-start(s32[32,64]{1,0:T(8,128)} %index_ref.3) | copy-start | bytes 24580
  7.7 1.0 copy-start.2
  8.7 0.8 copy-start.5
  9.5 59.8 %all-to-all-start = ((bf16[16,48,1024]{2,1,0:T(8,128)(2,1)}), bf16[16,48,1024]{2,1,0:T(8,128)(2,1)S(1)}, u32[]{:S(2)}, u32[]{:S(2)}) async-start(bf16[16,48,1024]{2,1,0:T(8,128)(2,1)} %get-tuple-element.19), calls=%async_computation | async-start | bytes 3145728 | tf_op jit(solution)/shard_map/all_to_all | solution.py:360
  15.0 48.7 %collective-permute-start = (bf16[528,1024]{1,0:T(8,128)(2,1)}, bf16[528,1024]{1,0:T(8,128)(2,1)S(1)}, u32[]{:S(2)}, u32[]{:S(2)}) collective-permute-start(bf16[528,1024]{1,0:T(8,128)(2,1)} %copy-done.2), channel_id=1, source_target_pairs={{0,16},{1,17},{2,18},{3,19},{4,20},{5,21},{6,22},{7,23},{8,24},{9,... | collective-permute-start | bytes 3244040 | tf_op jit(solution)/shard_map/ppermute | solution.py:348
  17.3 1.6 %collective-permute-start.1 = (f32[32,512]{1,0:T(8,128)S(1)}, f32[32,512]{1,0:T(8,128)S(1)}, u32[]{:S(2)}, u32[]{:S(2)}) collective-permute-start(f32[32,512]{1,0:T(8,128)S(1)} %slice_select_fusion), channel_id=1, source_target_pairs={{0,1},{1,0},{2,3},{3,2},{4,5},{5,4},{6,7},{7,6},{8,9},{9,8},{10,11... | collective-permute-start | bytes 196616 | tf_op jit(solution)/shard_map/ppermute | solution.py:319
  19.0 18.3 %collective-permute-start.2 = (f32[32,512]{1,0:T(8,128)S(1)}, f32[32,512]{1,0:T(8,128)S(1)}, u32[]{:S(2)}, u32[]{:S(2)}) collective-permute-start(f32[32,512]{1,0:T(8,128)S(1)} %select_add_fusion), channel_id=1, source_target_pairs={{0,2},{1,3},{2,0},{3,1},{4,6},{5,7},{6,4},{7,5},{8,10},{9,11},{10,... | collective-permute-start | bytes 196616 | tf_op jit(solution)/shard_map/ppermute | solution.py:319
  37.3 3.5 %collective-permute-start.3 = (f32[32,512]{1,0:T(8,128)S(1)}, f32[32,512]{1,0:T(8,128)S(1)}, u32[]{:S(2)}, u32[]{:S(2)}) collective-permute-start(f32[32,512]{1,0:T(8,128)S(1)} %add.28), channel_id=1, source_target_pairs={{0,4},{1,5},{2,6},{3,7},{4,0},{5,1},{6,2},{7,3},{8,12},{9,13},{10,... | collective-permute-start | bytes 196616 | tf_op jit(solution)/shard_map/ppermute | solution.py:319
  40.8 17.8 %collective-permute-start.4 = (f32[32,512]{1,0:T(8,128)S(1)}, f32[32,512]{1,0:T(8,128)S(1)}, u32[]{:S(2)}, u32[]{:S(2)}) collective-permute-start(f32[32,512]{1,0:T(8,128)S(1)} %add.29), channel_id=1, source_target_pairs={{0,8},{1,9},{2,10},{3,11},{4,12},{5,13},{6,14},{7,15},{8,0},{9,1},... | collective-permute-start | bytes 196616 | tf_op jit(solution)/shard_map/ppermute | solution.py:319
  63.7 1.0 copy-start
  64.7 1.2 copy-start.1
  65.9 1.0 copy-start.6
  68.4 1.0 copy-start.3
  94.7 23.5 %copy-start.10 = (s32[2,8192]{1,0:T(2,128)S(1)}, s32[2,8192]{1,0:T(2,128)}, u32[]{:S(2)}) copy-start(s32[2,8192]{1,0:T(2,128)} %param.15) | copy-start | bytes 196612
  94.7 24.5 %copy-start.4 = (bf16[1024,256]{1,0:T(8,128)(2,1)S(1)}, bf16[1024,256]{1,0:T(8,128)(2,1)}, u32[]{:S(2)}) copy-start(bf16[1024,256]{1,0:T(8,128)(2,1)} %constant.49.lag_ref) | copy-start | bytes 1572868
  94.7 24.5 %copy-start.8 = (s32[64]{0:T(128)S(1)}, s32[64]{0:T(128)}, u32[]{:S(2)}) copy-start(s32[64]{0:T(128)} %station_ref.3) | copy-start | bytes 772
  94.7 24.5 %copy-start.9 = (s32[64]{0:T(128)S(1)}, s32[64]{0:T(128)}, u32[]{:S(2)}) copy-start(s32[64]{0:T(128)} %count_ref.3) | copy-start | bytes 772
  94.7 39.5 %all-to-all-start.1 = ((bf16[16,32,1024]{2,1,0:T(8,128)(2,1)}), bf16[16,32,1024]{2,1,0:T(8,128)(2,1)S(1)}, u32[]{:S(2)}, u32[]{:S(2)}) async-start(bf16[16,32,1024]{2,1,0:T(8,128)(2,1)} %copy-done.3), calls=%async_computation.1 | async-start | bytes 2097152 | tf_op jit(solution)/shard_map/all_to_all | solution.py:371
  100.7 16.5 %collective-permute-start.5 = (f32[32,512]{1,0:T(8,128)S(1)}, f32[32,512]{1,0:T(8,128)S(1)}, u32[]{:S(2)}, u32[]{:S(2)}) collective-permute-start(f32[32,512]{1,0:T(8,128)S(1)} %add.30), channel_id=1, source_target_pairs={{0,16},{1,17},{2,18},{3,19},{4,20},{5,21},{6,22},{7,23},{8,24},{9,... | collective-permute-start | bytes 196616 | tf_op jit(solution)/shard_map/ppermute | solution.py:319
  117.2 1.9 %collective-permute-start.6 = (f32[32,512]{1,0:T(8,128)S(1)}, f32[32,512]{1,0:T(8,128)S(1)}, u32[]{:S(2)}, u32[]{:S(2)}) collective-permute-start(f32[32,512]{1,0:T(8,128)S(1)} %add.31), channel_id=1, source_target_pairs={{0,1},{1,0},{2,3},{3,2},{4,5},{5,4},{6,7},{7,6},{8,9},{9,8},{10,11... | collective-permute-start | bytes 196616 | tf_op jit(solution)/shard_map/ppermute | solution.py:319
